TPU v7x, 32 devices: a whole 2x2x4 slice. The times are simulated.
32 devices in a mesh: dp: 16 (over z, x, core), tensor: 2 (over y).
Axes of the slice: x: 2, y: 2, z: 4, core: 2. Of those that a mesh axis runs over, the one named last changes fastest.
Arguments:
- tokens: bfloat16 [8192, 2048], P('dp'), may hold values from -6 to 6
- segments: int32 [16, 512], P('dp'), may hold values from 0 to 3, never falling along the last dimension, each value on 1 to 384 neighbouring positions
- cotangent: bfloat16 [8192, 2048], P('dp'), may hold values from -6 to 6
- norm_gain: float32 [2048], P('dp'), may hold values from 0.1 to 1.9
- attn_weight: float32 [2048, 4, 2048], P('dp', None, 'tensor'), may hold values from -0.125 to 0.125
- beta_weight: float32 [2048, 16], P('dp', 'tensor'), may hold values from -0.125 to 0.125
- conv_weight: float32 [3, 4, 16, 128], P(None, None, 'tensor', 'dp'), may hold values from -3 to 3
- out_gain: float32 [128], P('dp'), may hold values from 0.1 to 1.9
- mlp_gain: float32 [2048], P('dp'), may hold values from 0.1 to 1.9
- mlp_weight: float32 [2048, 3, 5632], P('dp', None, 'tensor'), may hold values from -0.125 to 0.125
Outputs:
- output: bfloat16 [8192, 2048], P('dp')
- input_grad: float32 [8192, 2048], P('dp')
- norm_gain_grad: float32 [2048], P('dp')
- attn_weight_grad: float32 [2048, 4, 2048], P('dp', None, 'tensor')
- beta_weight_grad: float32 [2048, 16], P('dp', 'tensor')
- conv_weight_grad: float32 [3, 4, 16, 128], P(None, None, 'tensor', 'dp')
- out_gain_grad: float32 [128], P('dp')
- mlp_gain_grad: float32 [2048], P('dp')
- mlp_weight_grad: float32 [2048, 3, 5632], P('dp', None, 'tensor')
Inputs may be any that keep to these rules, and one draw needn't show every extreme that they name: `segments`: within a sequence the numbers never fall; a document (a run of one number) has 1 to 384 tokens, and some document has exactly 384.
All inputs are finite; a program needn't handle non-finite values.
Results may differ from a plain program's by a relative error of at most 0.017.
The roundings to bfloat16 on the way count: a program that leaves them out, or rounds other values in their place, can miss the bound.
Values may be sent and summed in bfloat16 or wider, within the bound.
No kernel may reach another device: no remote copies, remote signals or barrier semaphores. Data moves between devices by JAX's collectives and lax.ppermute only.
A program may use at most 384 MiB of HBM per device.

v0:
```python
import jax
import jax.numpy as jnp
from jax import lax
from jax.sharding import PartitionSpec as P

BLOCK = 64


highest = lax.Precision.HIGHEST


def rms_scale(values, gain_values, epsilon):
    return (
        values
        * lax.rsqrt(jnp.mean(values * values, axis=-1, keepdims=True) + epsilon)
        * gain_values
    )


def norm_apply(values, gain_values):
    return rms_scale(values, gain_values, 1e-05)


def short_conv(signal, weight, seg_ids):
    length = signal.shape[0]
    summed = signal * weight[3]
    for offset in range(1, 4):
        pad_rows = jnp.zeros((offset,) + signal.shape[1:], signal.dtype)
        shifted = jnp.concatenate([pad_rows, signal[: length - offset]], axis=0)
        prior_ids = jnp.concatenate(
            [jnp.full((offset,), -1, jnp.int32), seg_ids[: length - offset]], axis=0
        )
        allowed = (prior_ids == seg_ids).astype(signal.dtype)
        summed = summed + shifted * allowed[:, None, None] * weight[3 - offset]
    return summed


def delta_block(memory, inputs):
    queries, key_vecs, values, strength, seg_ids, prior_id = inputs
    block_len = seg_ids.shape[0]
    carry_in = (seg_ids == prior_id).astype(queries.dtype)
    same_doc = (seg_ids[:, None] == seg_ids[None, :]).astype(queries.dtype)
    row_ids = jnp.arange(block_len)
    strict = (row_ids[:, None] > row_ids[None, :]).astype(queries.dtype)
    causal = (row_ids[:, None] >= row_ids[None, :]).astype(queries.dtype)
    key_inner = jnp.einsum("ihd,jhd->hij", key_vecs, key_vecs, precision=highest) * (
        same_doc * strict
    )
    weights_t = jnp.transpose(strength)
    system = jnp.eye(block_len, dtype=queries.dtype) + weights_t[:, :, None] * key_inner
    recalled = jnp.einsum("hvd,ihd->hiv", memory, key_vecs, precision=highest)
    target = weights_t[:, :, None] * (
        jnp.transpose(values, (1, 0, 2)) - carry_in[None, :, None] * recalled
    )
    writes = lax.linalg.triangular_solve(
        system, target, left_side=True, lower=True, unit_diagonal=True
    )
    scores = jnp.einsum("ihd,jhd->hij", queries, key_vecs, precision=highest) * (same_doc * causal)
    carried = jnp.einsum("hvd,ihd->hiv", memory, queries, precision=highest)
    output = carry_in[None, :, None] * carried + jnp.einsum(
        "hij,hjv->hiv", scores, writes, precision=highest
    )
    final_doc = same_doc[block_len - 1]
    updated = carry_in[block_len - 1] * memory + jnp.einsum(
        "hjv,jhd->hvd", writes * final_doc[None, :, None], key_vecs, precision=highest
    )
    return (updated, jnp.transpose(output, (1, 0, 2)))


def delta_sequence(queries, key_vecs, values, strength, seg_ids):
    length = queries.shape[0]
    head_count = queries.shape[1]
    head_width = queries.shape[2]
    block_count = length // BLOCK
    prior_ids = jnp.concatenate(
        [jnp.full((1,), -1, jnp.int32), seg_ids[BLOCK - 1 : length - 1 : BLOCK]], axis=0
    )

    def blocked(array_in):
        return array_in.reshape((block_count, BLOCK) + array_in.shape[1:])

    initial = jnp.zeros((head_count, head_width, head_width), queries.dtype)
    final_state, outputs = lax.scan(
        jax.checkpoint(delta_block),
        initial,
        (
            blocked(queries),
            blocked(key_vecs),
            blocked(values),
            blocked(strength),
            blocked(seg_ids),
            prior_ids,
        ),
    )
    return outputs.reshape(queries.shape)


def token_mixer(projected, beta_logits, conv_weight, out_gain, seg_ids):
    length = projected.shape[0]
    convolved = [
        jax.nn.silu(short_conv(projected[:, which], conv_weight[which], seg_ids))
        for which in range(3)
    ]
    queries = convolved[0] * lax.rsqrt(
        jnp.sum(convolved[0] * convolved[0], axis=-1, keepdims=True) + 1e-06
    )
    key_vecs = convolved[1] * lax.rsqrt(
        jnp.sum(convolved[1] * convolved[1], axis=-1, keepdims=True) + 1e-06
    )
    strength = jax.nn.sigmoid(beta_logits)
    output = delta_sequence(queries, key_vecs, convolved[2], strength, seg_ids)
    return rms_scale(output, out_gain, 1e-05).reshape(length, -1)


def body(
    tokens,
    segments,
    cotangent,
    norm_gain,
    attn_weight,
    beta_weight,
    conv_weight,
    out_gain,
    mlp_gain,
    mlp_weight,
):
    seg_ids = segments[0]
    length = tokens.shape[0]
    gain_in_low = norm_gain.astype(jnp.bfloat16)
    attn_low = attn_weight.astype(jnp.bfloat16)
    beta_low = beta_weight.astype(jnp.bfloat16)
    gain_mid_low = mlp_gain.astype(jnp.bfloat16)
    mlp_low = mlp_weight.astype(jnp.bfloat16)
    gain_in, attn_mat, beta_mat, conv_full, gain_heads = (
        lax.all_gather(gain_in_low, "dp", axis=0, tiled=True),
        lax.all_gather(attn_low, "dp", axis=0, tiled=True),
        lax.all_gather(beta_low, "dp", axis=0, tiled=True),
        lax.all_gather(conv_weight.astype(jnp.bfloat16), "dp", axis=3, tiled=True),
        lax.all_gather(out_gain.astype(jnp.bfloat16), "dp", axis=0, tiled=True),
    )
    gain_mid, mlp_mat = (
        lax.all_gather(gain_mid_low, "dp", axis=0, tiled=True),
        lax.all_gather(mlp_low, "dp", axis=0, tiled=True),
    )
    model_width = attn_mat.shape[0]
    local_width = attn_mat.shape[2]
    head_count = conv_full.shape[2]
    head_width = conv_full.shape[3]
    inputs_f = tokens.astype(jnp.float32)
    normed = rms_scale(inputs_f, gain_in.astype(jnp.float32), 1e-05).astype(jnp.bfloat16)
    qkv_mat = attn_mat[:, :3].reshape(model_width, 3 * local_width)
    projected = jnp.dot(normed, qkv_mat, preferred_element_type=jnp.float32)
    beta_logits = jnp.dot(normed, beta_mat, preferred_element_type=jnp.float32)

    def local_mixer(proj_value, logit_value, conv_value, heads_gain):
        return token_mixer(
            proj_value.reshape(length, 3, head_count, head_width),
            logit_value,
            conv_value,
            heads_gain,
            seg_ids,
        )

    mixed, mixer_pull = jax.vjp(
        local_mixer,
        projected,
        beta_logits,
        conv_full.astype(jnp.float32),
        gain_heads.astype(jnp.float32),
    )
    mixed_low = mixed.astype(jnp.bfloat16)
    attn_part = jnp.einsum(
        "tc,oc->to", mixed_low, attn_mat[:, 3], preferred_element_type=jnp.float32
    )
    attended = lax.psum(attn_part, "tensor")
    hidden = inputs_f + attended
    normed_mlp = rms_scale(hidden, gain_mid.astype(jnp.float32), 1e-05).astype(jnp.bfloat16)
    gate_up = jnp.einsum(
        "td,dgf->tgf", normed_mlp, mlp_mat[:, :2], preferred_element_type=jnp.float32
    )
    gate_vals = gate_up[:, 0]
    up_vals = gate_up[:, 1]
    activated = (jax.nn.silu(gate_vals) * up_vals).astype(jnp.bfloat16)
    down_part = jnp.einsum(
        "tf,of->to", activated, mlp_mat[:, 2], preferred_element_type=jnp.float32
    )
    mlp_out = lax.psum(down_part.astype(jnp.bfloat16), "tensor").astype(jnp.float32)
    result = (hidden + mlp_out).astype(jnp.bfloat16)
    gain_in, attn_mat, beta_mat = (
        lax.all_gather(gain_in_low, "dp", axis=0, tiled=True),
        lax.all_gather(attn_low, "dp", axis=0, tiled=True),
        lax.all_gather(beta_low, "dp", axis=0, tiled=True),
    )
    gain_mid, mlp_mat = (
        lax.all_gather(gain_mid_low, "dp", axis=0, tiled=True),
        lax.all_gather(mlp_low, "dp", axis=0, tiled=True),
    )
    grad_act = jnp.einsum("to,of->tf", cotangent, mlp_mat[:, 2], preferred_element_type=jnp.float32)
    gate_sig = jax.nn.sigmoid(gate_vals)
    grad_gate = grad_act * up_vals * gate_sig * (1.0 + gate_vals * (1.0 - gate_sig))
    grad_up = grad_act * gate_vals * gate_sig
    grad_gate_up = jnp.stack([grad_gate, grad_up], axis=1).astype(jnp.bfloat16)
    normed_rows = normed_mlp
    grad_rows = cotangent
    first_part = jnp.einsum(
        "tc,tgf->cgf", normed_rows, grad_gate_up, preferred_element_type=jnp.float32
    )
    last_part = jnp.einsum("tc,tf->cf", grad_rows, activated, preferred_element_type=jnp.float32)
    mlp_grad = lax.psum_scatter(
        jnp.concatenate([first_part, last_part[:, None]], axis=1),
        "dp",
        scatter_dimension=0,
        tiled=True,
    )
    grad_normed_mlp_part = jnp.einsum(
        "tgf,dgf->td", grad_gate_up, mlp_mat[:, :2], preferred_element_type=jnp.float32
    )
    grad_normed_mlp = lax.psum(grad_normed_mlp_part.astype(jnp.bfloat16), "tensor").astype(
        jnp.float32
    )
    normed_again, mid_pull = jax.vjp(norm_apply, hidden, gain_mid.astype(jnp.float32))
    grad_hidden_norm, grad_gain_mid = mid_pull(grad_normed_mlp)
    grad_hidden = cotangent.astype(jnp.float32) + grad_hidden_norm
    grad_hidden_low = grad_hidden.astype(jnp.bfloat16)
    grad_mixed = jnp.einsum(
        "to,oc->tc", grad_hidden_low, attn_mat[:, 3], preferred_element_type=jnp.float32
    )
    grad_proj, grad_logits, grad_conv, grad_gain_heads = mixer_pull(grad_mixed)
    grad_proj_low = grad_proj.reshape(length, 3, local_width).astype(jnp.bfloat16)
    grad_logits_low = grad_logits.astype(jnp.bfloat16)
    normed_rows = normed
    grad_rows = grad_hidden_low
    first_part = jnp.einsum(
        "tc,tpe->cpe", normed_rows, grad_proj_low, preferred_element_type=jnp.float32
    )
    last_part = jnp.einsum("tc,te->ce", grad_rows, mixed_low, preferred_element_type=jnp.float32)
    attn_grad = lax.psum_scatter(
        jnp.concatenate([first_part, last_part[:, None]], axis=1),
        "dp",
        scatter_dimension=0,
        tiled=True,
    )
    grad_beta = jnp.einsum("td,th->dh", normed, grad_logits_low, preferred_element_type=jnp.float32)
    grad_normed_part = jnp.einsum(
        "tpe,dpe->td", grad_proj_low, attn_mat[:, :3], preferred_element_type=jnp.float32
    )
    grad_normed_part = grad_normed_part + jnp.einsum(
        "th,dh->td", grad_logits_low, beta_mat, preferred_element_type=jnp.float32
    )
    grad_normed, grad_gain_heads = (
        lax.psum(grad_normed_part.astype(jnp.bfloat16), "tensor").astype(jnp.float32),
        lax.psum(grad_gain_heads.astype(jnp.bfloat16), "tensor").astype(jnp.float32),
    )
    normed_first, in_pull = jax.vjp(norm_apply, inputs_f, gain_in.astype(jnp.float32))
    grad_inputs_norm, grad_gain_in = in_pull(grad_normed)
    grad_inputs = grad_hidden + grad_inputs_norm
    small_sums = (
        lax.psum_scatter(grad_gain_in, "dp", scatter_dimension=0, tiled=True),
        lax.psum_scatter(grad_beta, "dp", scatter_dimension=0, tiled=True),
        lax.psum_scatter(grad_conv, "dp", scatter_dimension=3, tiled=True),
        lax.psum_scatter(grad_gain_heads, "dp", scatter_dimension=0, tiled=True),
        lax.psum_scatter(grad_gain_mid, "dp", scatter_dimension=0, tiled=True),
    )
    return (
        result,
        grad_inputs,
        small_sums[0],
        attn_grad,
        small_sums[1],
        small_sums[2],
        small_sums[3],
        small_sums[4],
        mlp_grad,
    )


def solution(mesh):
    return jax.shard_map(
        body,
        mesh=mesh,
        in_specs=(
            P("dp", None),
            P("dp", None),
            P("dp", None),
            P("dp"),
            P("dp", None, "tensor"),
            P("dp", "tensor"),
            P(None, None, "tensor", "dp"),
            P("dp"),
            P("dp"),
            P("dp", None, "tensor"),
        ),
        out_specs=(
            P("dp", None),
            P("dp", None),
            P("dp"),
            P("dp", None, "tensor"),
            P("dp", "tensor"),
            P(None, None, "tensor", "dp"),
            P("dp"),
            P("dp"),
            P("dp", None, "tensor"),
        ),
        check_vma=False,
    )
```

profile of v0, /device:TPU:0, one launch (start us, length us, event | category | flops | bytes accessed | tf_op | source)
XLA Modules:
  0.0 2766.3 jit_solution(18114808187447301338)
XLA Ops:
  12.9 36.1 %all-reduce.38 = bf16[128]{0:T(256)(128)(2,1)S(1)} all-reduce(bf16[128]{0:T(256)(128)(2,1)S(1)} %dynamic-update-slice), channel_id=1, replica_groups=mesh['dp'=16,'tensor'=2] {'dp'}, use_global_device_ids=true, to_apply=%add.38 | all-reduce | flops 128 | bytes 512
  50.2 17.1 all-gather
  67.4 19.8 all_gather.27
  89.2 20.9 all_gather.29
  111.8 33.6 %all-gather.5.cloned.1.call-done = bf16[2048,4,1024]{2,0,1:T(8,128)(2,1)} async-done(((bf16[128,4,1024]{2,0,1:T(8,128)(2,1)}), bf16[2048,4,1024]{2,0,1:T(8,128)(2,1)}) %all-gather.5.cloned.1.call-update) | async-done | bytes 16777232 | tf_op jit(solution)/shard_map/all_gather | solution.py:136
  145.4 10.6 slice.268
  156.0 17.0 copy.98
  173.0 9.4 fusion.144
  201.9 432.9 %while.38 = (s32[]{:T(128)}, f32[8,128,128]{2,1,0:T(8,128)S(1)}, f32[8,64,8,128]{3,1,2,0:T(8,128)}, f32[8,8,128,128]{3,2,1,0:T(8,128)}, s32[8,64]{1,0:T(8,128)S(...) while((s32[]{:T(128)}, f32[8,128,128]{2,1,0:T(8,128)S(1)}, ...), condition=%wide.region_4.6_spmd.clone, body=%wide.region_3.5_spmd.clone.sunk | while | flops 504746240 | bytes 7759869 | solution.py:83
  205.8 39.3 %custom-call.24 = f32[8,1,64,64]{2,3,1,0:T(8,128)S(1)} custom-call(f32[8,1,64,64]{3,2,1,0:T(8,128)S(1)} %fusion.307), custom_call_target="InvertDiagBlocksLowerTriangular" | custom-call | tf_op jit(solution)/shard_map/jvp()/while/body/eval_jaxpr/triangular_solve/custom-call.1 | solution.py:55
  259.9 39.3 %custom-call.24 = f32[8,1,64,64]{2,3,1,0:T(8,128)S(1)} custom-call(f32[8,1,64,64]{3,2,1,0:T(8,128)S(1)} %fusion.307), custom_call_target="InvertDiagBlocksLowerTriangular" | custom-call | tf_op jit(solution)/shard_map/jvp()/while/body/eval_jaxpr/triangular_solve/custom-call.1 | solution.py:55
  314.0 39.3 %custom-call.24 = f32[8,1,64,64]{2,3,1,0:T(8,128)S(1)} custom-call(f32[8,1,64,64]{3,2,1,0:T(8,128)S(1)} %fusion.307), custom_call_target="InvertDiagBlocksLowerTriangular" | custom-call | tf_op jit(solution)/shard_map/jvp()/while/body/eval_jaxpr/triangular_solve/custom-call.1 | solution.py:55
  368.1 39.3 %custom-call.24 = f32[8,1,64,64]{2,3,1,0:T(8,128)S(1)} custom-call(f32[8,1,64,64]{3,2,1,0:T(8,128)S(1)} %fusion.307), custom_call_target="InvertDiagBlocksLowerTriangular" | custom-call | tf_op jit(solution)/shard_map/jvp()/while/body/eval_jaxpr/triangular_solve/custom-call.1 | solution.py:55
  422.2 39.3 %custom-call.24 = f32[8,1,64,64]{2,3,1,0:T(8,128)S(1)} custom-call(f32[8,1,64,64]{3,2,1,0:T(8,128)S(1)} %fusion.307), custom_call_target="InvertDiagBlocksLowerTriangular" | custom-call | tf_op jit(solution)/shard_map/jvp()/while/body/eval_jaxpr/triangular_solve/custom-call.1 | solution.py:55
  476.3 39.3 %custom-call.24 = f32[8,1,64,64]{2,3,1,0:T(8,128)S(1)} custom-call(f32[8,1,64,64]{3,2,1,0:T(8,128)S(1)} %fusion.307), custom_call_target="InvertDiagBlocksLowerTriangular" | custom-call | tf_op jit(solution)/shard_map/jvp()/while/body/eval_jaxpr/triangular_solve/custom-call.1 | solution.py:55
  530.4 39.3 %custom-call.24 = f32[8,1,64,64]{2,3,1,0:T(8,128)S(1)} custom-call(f32[8,1,64,64]{3,2,1,0:T(8,128)S(1)} %fusion.307), custom_call_target="InvertDiagBlocksLowerTriangular" | custom-call | tf_op jit(solution)/shard_map/jvp()/while/body/eval_jaxpr/triangular_solve/custom-call.1 | solution.py:55
  584.5 39.3 %custom-call.24 = f32[8,1,64,64]{2,3,1,0:T(8,128)S(1)} custom-call(f32[8,1,64,64]{3,2,1,0:T(8,128)S(1)} %fusion.307), custom_call_target="InvertDiagBlocksLowerTriangular" | custom-call | tf_op jit(solution)/shard_map/jvp()/while/body/eval_jaxpr/triangular_solve/custom-call.1 | solution.py:55
  638.7 6.6 fusion.114
  651.2 18.3 all-gather.1
  677.4 6.9 copy.117
  684.3 67.2 %all-reduce.50.cloned.1.call-done = f32[512,2048]{1,0:T(8,128)} async-done(((f32[512,2048]{1,0:T(8,128)}), f32[512,2048]{1,0:T(8,128)}) %all-reduce.50.cloned.1.call-update) | async-done | bytes 4194320 | tf_op jit(solution)/shard_map/psum | solution.py:175
  756.2 170.0 %all-gather.7.cloned.1.call-done = bf16[2048,3,2816]{2,0,1:T(8,128)(2,1)} async-done(((bf16[128,3,2816]{2,0,1:T(8,128)(2,1)}), bf16[2048,3,2816]{2,0,1:T(8,128)(2,1)}) %all-gather.7.cloned.1.call-update) | async-done | bytes 34603024 | tf_op jit(solution)/shard_map/all_gather | solution.py:143
  926.2 20.5 fusion.86
  946.7 14.0 fusion.125
  960.7 19.3 bitcast_convert_fusion
  980.2 15.8 fusion.120
  996.0 47.1 %all-reduce.52.cloned.1.call-done = bf16[512,2048]{1,0:T(8,128)(2,1)} async-done(((bf16[512,2048]{1,0:T(8,128)(2,1)}), bf16[512,2048]{1,0:T(8,128)(2,1)}) %all-reduce.52.cloned.1.call-update) | async-done | bytes 2097168 | tf_op jit(solution)/shard_map/psum | solution.py:218
  1062.7 495.5 %while.39 = (s32[]{:T(128)}, f32[8,128,128]{2,1,0:T(8,128)S(1)}, f32[8,64,8,128]{3,1,0,2:T(8,128)}, f32[8,64,8,128]{3,1,0,2:T(8,128)}, f32[8,64,8,128]{3,1,0,2:T...) while((s32[]{:T(128)}, f32[8,128,128]{2,1,0:T(8,128)S(1)}, ...), condition=%wide.region_15.17_spmd.clone, body=%wide.region_12.16_spmd.clone.sunk | while | flops 1285967616 | bytes 23183872 | solution.py:83
  1071.0 39.3 %custom-call.25 = f32[8,1,64,64]{2,3,1,0:T(8,128)S(1)} custom-call(f32[8,1,64,64]{3,2,1,0:T(8,128)S(1)} %add_bitcast_fusion.8), custom_call_target="InvertDiagBlocksLowerTriangular" | custom-call | tf_op jit(solution)/shard_map/transpose(jvp())/while/body/eval_jaxpr/checkpoint/triangular_solve | solution.py:55
  1132.9 39.3 %custom-call.25 = f32[8,1,64,64]{2,3,1,0:T(8,128)S(1)} custom-call(f32[8,1,64,64]{3,2,1,0:T(8,128)S(1)} %add_bitcast_fusion.8), custom_call_target="InvertDiagBlocksLowerTriangular" | custom-call | tf_op jit(solution)/shard_map/transpose(jvp())/while/body/eval_jaxpr/checkpoint/triangular_solve | solution.py:55
  1194.8 39.3 %custom-call.25 = f32[8,1,64,64]{2,3,1,0:T(8,128)S(1)} custom-call(f32[8,1,64,64]{3,2,1,0:T(8,128)S(1)} %add_bitcast_fusion.8), custom_call_target="InvertDiagBlocksLowerTriangular" | custom-call | tf_op jit(solution)/shard_map/transpose(jvp())/while/body/eval_jaxpr/checkpoint/triangular_solve | solution.py:55
  1256.7 39.3 %custom-call.25 = f32[8,1,64,64]{2,3,1,0:T(8,128)S(1)} custom-call(f32[8,1,64,64]{3,2,1,0:T(8,128)S(1)} %add_bitcast_fusion.8), custom_call_target="InvertDiagBlocksLowerTriangular" | custom-call | tf_op jit(solution)/shard_map/transpose(jvp())/while/body/eval_jaxpr/checkpoint/triangular_solve | solution.py:55
  1318.6 39.3 %custom-call.25 = f32[8,1,64,64]{2,3,1,0:T(8,128)S(1)} custom-call(f32[8,1,64,64]{3,2,1,0:T(8,128)S(1)} %add_bitcast_fusion.8), custom_call_target="InvertDiagBlocksLowerTriangular" | custom-call | tf_op jit(solution)/shard_map/transpose(jvp())/while/body/eval_jaxpr/checkpoint/triangular_solve | solution.py:55
  1380.4 39.3 %custom-call.25 = f32[8,1,64,64]{2,3,1,0:T(8,128)S(1)} custom-call(f32[8,1,64,64]{3,2,1,0:T(8,128)S(1)} %add_bitcast_fusion.8), custom_call_target="InvertDiagBlocksLowerTriangular" | custom-call | tf_op jit(solution)/shard_map/transpose(jvp())/while/body/eval_jaxpr/checkpoint/triangular_solve | solution.py:55
  1442.3 39.3 %custom-call.25 = f32[8,1,64,64]{2,3,1,0:T(8,128)S(1)} custom-call(f32[8,1,64,64]{3,2,1,0:T(8,128)S(1)} %add_bitcast_fusion.8), custom_call_target="InvertDiagBlocksLowerTriangular" | custom-call | tf_op jit(solution)/shard_map/transpose(jvp())/while/body/eval_jaxpr/checkpoint/triangular_solve | solution.py:55
  1504.1 39.3 %custom-call.25 = f32[8,1,64,64]{2,3,1,0:T(8,128)S(1)} custom-call(f32[8,1,64,64]{3,2,1,0:T(8,128)S(1)} %add_bitcast_fusion.8), custom_call_target="InvertDiagBlocksLowerTriangular" | custom-call | tf_op jit(solution)/shard_map/transpose(jvp())/while/body/eval_jaxpr/checkpoint/triangular_solve | solution.py:55
  1564.2 12.5 multiply_reduce_fusion.11
  1585.1 10.8 fusion.181
  1604.3 6.1 convolution_bitcast_fusion.6
  1610.4 12.3 fusion.146
  1622.7 20.6 pad_maximum_fusion.1
  1643.4 16.3 convolution_bitcast_fusion.5
  1659.8 25.2 fusion.116
  1686.4 49.2 %pad_maximum_fusion = f32[2048,3,2816]{2,0,1:T(8,128)} fusion(f32[2048,1,2816]{2,0,1:T(8,128)} %convolution_bitcast_fusion.5, f32[2048,2,2816]{2,0,1:T(8,128)} %fusion.116), kind=kLoop, calls=%fused_computation.142 | loop fusion | flops 17301504 | bytes 138412032 | tf_op jit(solution)/shard_map/concatenate | solution.py:210
  1746.1 63.7 %all-reduce.55 = (f32[2048]{0:T(1024)S(1)}, f32[3,4,8,128]{3,2,1,0:T(8,128)S(1)}, f32[128]{0:T(128)S(1)}, f32[2048]{0:T(1024)S(1)}) all-reduce(f32[2048]{0:T(1024)S(1)} %get-tuple-element.569, f32[3,4,8,128]{3,2,1,0:T(8,128)S(1)} %pad_add_fusion, bf16[128]{0:T(256)(128)(2,1)S(1)} %psum.39, ...), channel_id=2, replica_groups=mesh['dp'=16,'tensor'=2] {'dp'}, use_global_device_ids=true, to_apply=%region_21.23.clone | all-reduce | flops 16512 | bytes 131840
  1820.5 224.0 %reduce-scatter.5.cloned.1.call-done = f32[128,4,1024]{2,0,1:T(8,128)} async-done(((f32[2048,4,1024]{2,0,1:T(8,128)}), f32[128,4,1024]{2,0,1:T(8,128)}) %reduce-scatter.5.cloned.1.call-update) | async-done | bytes 2097168 | tf_op jit(solution)/shard_map/reduce_scatter | solution.py:237
  2048.7 51.1 %reduce-scatter.7.cloned.1.call-done = f32[128,8]{0,1:T(8,128)} async-done(((f32[2048,8]{0,1:T(8,128)}), f32[128,8]{0,1:T(8,128)}) %reduce-scatter.7.cloned.1.call-update) | async-done | bytes 4112 | tf_op jit(solution)/shard_map/reduce_scatter | solution.py:259
  2099.8 659.4 %reduce-scatter.9.cloned.1.call-done = f32[128,3,2816]{2,0,1:T(8,128)} async-done(((f32[2048,3,2816]{2,0,1:T(8,128)}), f32[128,3,2816]{2,0,1:T(8,128)}) %reduce-scatter.9.cloned.1.call-update) | async-done | bytes 4325392 | tf_op jit(solution)/shard_map/reduce_scatter | solution.py:209
  (793 shorter events, 415.2 us)
Async XLA Ops:
  7.2 43.0 %copy-start.99 = (f32[128,8]{0,1:T(8,128)S(1)}, f32[128,8]{0,1:T(8,128)}, u32[]{:S(2)}) copy-start(f32[128,8]{0,1:T(8,128)} %param.21) | copy-start | bytes 12292
  7.2 43.0 %copy-start.102 = (f32[128]{0:T(128)S(1)}, f32[128]{0:T(128)}, u32[]{:S(2)}) copy-start(f32[128]{0:T(128)} %param.19) | copy-start | bytes 1540
  7.2 60.1 %copy-start.52 = (f32[3,4,8,8]{3,2,1,0:T(8,128)S(1)}, f32[3,4,8,8]{3,2,1,0:T(8,128)}, u32[]{:S(2)}) copy-start(f32[3,4,8,8]{3,2,1,0:T(8,128)} %param.22) | copy-start | bytes 9220
  7.2 80.0 %copy-start.6 = (bf16[512,2048]{1,0:T(8,128)(2,1)S(1)}, bf16[512,2048]{1,0:T(8,128)(2,1)}, u32[]{:S(2)}) copy-start(bf16[512,2048]{1,0:T(8,128)(2,1)} %param.16) | copy-start | bytes 6291460
  7.3 138.2 %all-gather.5.cloned.1.call-start = ((), (), s32[]{:S(2)}) async-start(), calls=%async_computation.3 | async-start | bytes 17825792 | tf_op jit(solution)/shard_map/all_gather | solution.py:136
  11.2 740.4 %all-reduce.50.cloned.1.call-start = ((), (), s32[]{:S(2)}) async-start(), calls=%async_computation.4 | async-start | bytes 8388608 | tf_op jit(solution)/shard_map/psum | solution.py:175
  67.3 105.6 %copy-start.39 = (f32[16,1,128]{2,1,0:T(1,128)}, f32[16,1,128]{2,1,0:T(1,128)S(1)}, u32[]{:S(2)}) copy-start(f32[16,1,128]{2,1,0:T(1,128)S(1)} %convert_element_type.232) | copy-start | bytes 24580
  87.8 22.4 copy-start.82
  87.8 85.2 %copy-start.78 = (f32[512]{0:T(512)}, f32[512]{0:T(512)S(1)}, u32[]{:S(2)}) copy-start(f32[512]{0:T(512)S(1)} %fusion.174) | copy-start | bytes 6148
  110.8 81.2 %copy-start.55 = (f32[8,128]{1,0:T(8,128)}, f32[8,128]{1,0:T(8,128)S(1)}, u32[]{:S(2)}) copy-start(f32[8,128]{1,0:T(8,128)S(1)} %copy.108) | copy-start | bytes 12292
  110.9 81.2 %copy-start.65 = (f32[8,128]{1,0:T(8,128)}, f32[8,128]{1,0:T(8,128)S(1)}, u32[]{:S(2)}) copy-start(f32[8,128]{1,0:T(8,128)S(1)} %copy.109) | copy-start | bytes 12292
  110.9 81.1 %copy-start.61 = (f32[8,128]{1,0:T(8,128)}, f32[8,128]{1,0:T(8,128)S(1)}, u32[]{:S(2)}) copy-start(f32[8,128]{1,0:T(8,128)S(1)} %copy.110) | copy-start | bytes 12292
  111.0 81.0 %copy-start.59 = (f32[8,128]{1,0:T(8,128)}, f32[8,128]{1,0:T(8,128)S(1)}, u32[]{:S(2)}) copy-start(f32[8,128]{1,0:T(8,128)S(1)} %copy.111) | copy-start | bytes 12292
  111.1 81.0 %copy-start.53 = (f32[8,128]{1,0:T(8,128)}, f32[8,128]{1,0:T(8,128)S(1)}, u32[]{:S(2)}) copy-start(f32[8,128]{1,0:T(8,128)S(1)} %copy.104) | copy-start | bytes 12292
  111.2 80.9 %copy-start.71 = (f32[8,128]{1,0:T(8,128)}, f32[8,128]{1,0:T(8,128)S(1)}, u32[]{:S(2)}) copy-start(f32[8,128]{1,0:T(8,128)S(1)} %copy.105) | copy-start | bytes 12292
  111.2 80.8 %copy-start.67 = (f32[8,128]{1,0:T(8,128)}, f32[8,128]{1,0:T(8,128)S(1)}, u32[]{:S(2)}) copy-start(f32[8,128]{1,0:T(8,128)S(1)} %copy.106) | copy-start | bytes 12292
  111.3 80.8 %copy-start.63 = (f32[8,128]{1,0:T(8,128)}, f32[8,128]{1,0:T(8,128)S(1)}, u32[]{:S(2)}) copy-start(f32[8,128]{1,0:T(8,128)S(1)} %copy.107) | copy-start | bytes 12292
  111.4 72.9 %copy-start.57 = (f32[8,128]{1,0:T(8,128)}, f32[8,128]{1,0:T(8,128)S(1)}, u32[]{:S(2)}) copy-start(f32[8,128]{1,0:T(8,128)S(1)} %copy.100) | copy-start | bytes 12292
  111.4 72.9 %copy-start.75 = (f32[8,128]{1,0:T(8,128)}, f32[8,128]{1,0:T(8,128)S(1)}, u32[]{:S(2)}) copy-start(f32[8,128]{1,0:T(8,128)S(1)} %copy.101) | copy-start | bytes 12292
  111.5 72.8 %copy-start.73 = (f32[8,128]{1,0:T(8,128)}, f32[8,128]{1,0:T(8,128)S(1)}, u32[]{:S(2)}) copy-start(f32[8,128]{1,0:T(8,128)S(1)} %copy.102) | copy-start | bytes 12292
  111.6 72.7 %copy-start.69 = (f32[8,128]{1,0:T(8,128)}, f32[8,128]{1,0:T(8,128)S(1)}, u32[]{:S(2)}) copy-start(f32[8,128]{1,0:T(8,128)S(1)} %copy.103) | copy-start | bytes 12292
  111.7 537.5 %copy-start.46 = (f32[512]{0:T(512)}, f32[512]{0:T(512)S(1)}, u32[]{:S(2)}) copy-start(f32[512]{0:T(512)S(1)} %get-tuple-element.697) | copy-start | bytes 6148
  111.7 538.1 %copy-start.48 = (f32[512]{0:T(512)}, f32[512]{0:T(512)S(1)}, u32[]{:S(2)}) copy-start(f32[512]{0:T(512)S(1)} %get-tuple-element.698) | copy-start | bytes 6148
  111.7 538.8 %copy-start.50 = (f32[512]{0:T(512)}, f32[512]{0:T(512)S(1)}, u32[]{:S(2)}) copy-start(f32[512]{0:T(512)S(1)} %get-tuple-element.699) | copy-start | bytes 6148
  182.3 9.8 copy-start
  183.0 9.1 copy-start.12
  183.0 9.1 copy-start.14
  183.6 8.5 copy-start.16
  183.6 8.5 copy-start.17
  645.3 280.9 %all-gather.7.cloned.1.call-start = ((), (), s32[]{:S(2)}) async-start(), calls=%async_computation.5 | async-start | bytes 36765696 | tf_op jit(solution)/shard_map/all_gather | solution.py:143
  649.2 393.9 %all-reduce.52.cloned.1.call-start = ((), (), s32[]{:S(2)}) async-start(), calls=%async_computation.6 | async-start | bytes 4194304 | tf_op jit(solution)/shard_map/psum | solution.py:218
  669.5 378.5 %copy-start.41 = (f32[16,1,128]{2,1,0:T(1,128)}, f32[16,1,128]{2,1,0:T(1,128)S(1)}, u32[]{:S(2)}) copy-start(f32[16,1,128]{2,1,0:T(1,128)S(1)} %convert_element_type.233) | copy-start | bytes 24580
  756.2 291.7 %copy-start.80 = (f32[512]{0:T(512)}, f32[512]{0:T(512)S(1)}, u32[]{:S(2)}) copy-start(f32[512]{0:T(512)S(1)} %fusion.175) | copy-start | bytes 6148
  926.2 20.5 copy-start.28
  980.0 762.4 %all-reduce.54.cloned.1.call-start = ((), (), s32[]{:S(2)}) async-start(), calls=%async_computation.10 | async-start | bytes 8388608 | tf_op jit(solution)/shard_map/psum | solution.py:187
  1062.7 495.6 %copy-start.44 = (f32[512,8]{0,1:T(8,128)S(1)}, f32[512,8]{0,1:T(8,128)}, u32[]{:S(2)}) copy-start(f32[512,8]{0,1:T(8,128)} %copy-done.43) | copy-start | bytes 49156
  1062.7 500.5 %copy-start.36 = (f32[512,8]{0,1:T(8,128)S(1)}, f32[512,8]{0,1:T(8,128)}, u32[]{:S(2)}) copy-start(f32[512,8]{0,1:T(8,128)} %copy-done.35) | copy-start | bytes 49156
  1564.2 12.6 copy-start.66
  1564.2 12.5 copy-start.72
  1564.2 12.5 copy-start.76
  1564.2 12.5 copy-start.98
  1585.1 10.9 copy-start.38
  1598.1 446.4 %reduce-scatter.5.cloned.1.call-start = ((), (), s32[]{:S(2)}) async-start(), calls=%async_computation.7 | async-start | bytes 35651584 | tf_op jit(solution)/shard_map/reduce_scatter | solution.py:237
  1643.4 16.4 copy-start.42
  1643.4 16.4 copy-start.81
  1643.4 456.4 %reduce-scatter.7.cloned.1.call-start = ((), (), s32[]{:S(2)}) async-start(), calls=%async_computation.8 | async-start | bytes 69632 | tf_op jit(solution)/shard_map/reduce_scatter | solution.py:259
  1686.3 1072.9 %reduce-scatter.9.cloned.1.call-start = ((), (), s32[]{:S(2)}) async-start(), calls=%async_computation.9 | async-start | bytes 73531392 | tf_op jit(solution)/shard_map/reduce_scatter | solution.py:209
  1742.4 69.8 %copy-start.83 = (f32[512]{0:T(512)S(1)}, f32[512]{0:T(512)}, u32[]{:S(2)}) copy-start(f32[512]{0:T(512)} %copy-done.82) | copy-start | bytes 6148
  (65 other events, 261.9 us)
Sparse Core Ops, SparseCore 0:
  11.3 134.1 all-gather.4
  645.4 106.0 all-reduce.49
  753.2 172.9 all-gather.6
  980.1 62.9 all-reduce.51
  1598.2 108.2 all-reduce.53
  1711.2 333.2 reduce-scatter.4
  2048.8 50.9 reduce-scatter.6
  2104.6 654.5 reduce-scatter.8
where the time goes:
time: 2770 us
  waiting for transfers between devices  1250 us (45%)
  other arithmetic  788 us (28%)
  matrix products  384 us (14%)
  blocking collectives  181 us (7%)
  local copies, waits for them, and re-layouts  140 us (5%)
    reduce_scatter x2, waiting for transfers between devices, body(): lax.psum_scatter(jnp.concatenate([first_part, last_part[:, None]], axis=1...  883 us
    another operation x64, other arithmetic, delta_block(): lax.linalg.triangular_solve(system, target, left_side=True, lower=True, u...  632 us
    all_gather x1, waiting for transfers between devices, body(): lax.all_gather(mlp_low, 'dp', axis=0, tiled=True)  170 us
    unnamed x2, blocking collectives  99.7 us
    concatenate x2, other arithmetic, body(): jnp.concatenate([first_part, last_part[:, None]], axis=1)  69.9 us
    psum x1, waiting for transfers between devices, body(): attended = lax.psum(attn_part, 'tensor')  67.2 us
  transfers between devices with their start and end apart: 8, of which 7 were waited for; matrix products, arithmetic and copies ran while one was open for 7% of the time, Pallas kernels for 0%

commit v1 on v0

v1 whole, which is shorter than its diff:
```python
import functools

import jax
import jax.numpy as jnp
from jax import lax
from jax.experimental import pallas as pl
from jax.experimental.pallas import tpu as pltpu
from jax.sharding import PartitionSpec as P

F32 = jnp.float32
BF16 = jnp.bfloat16
CHUNK = 128
NN = (((1,), (0,)), ((), ()))
NT = (((1,), (1,)), ((), ()))
TN = (((0,), (0,)), ((), ()))


def split2(value):
    high = value.astype(BF16)
    return high, (value - high.astype(F32)).astype(BF16)


def dot1(left, right, dims):
    return lax.dot_general(left, right, dims, preferred_element_type=F32)


def mul3(left, right, dims):
    (lh, ll), (rh, rl) = left, right
    return dot1(lh, rh, dims) + (dot1(lh, rl, dims) + dot1(ll, rh, dims))


def mul1(left, right, dims):
    return dot1(left[0], right[0], dims)


def iotas(size):
    return (
        lax.broadcasted_iota(jnp.int32, (size, size), 0),
        lax.broadcasted_iota(jnp.int32, (size, size), 1),
    )


def allowed_rows(seg_full, offset):
    rows = lax.broadcasted_iota(jnp.int32, seg_full.shape, 0)
    earlier = pltpu.roll(seg_full, offset, 0)
    return jnp.where((earlier == seg_full) & (rows >= offset), 1.0, 0.0).astype(F32)


def conv_taps(signal, taps, gates):
    summed = signal * taps[3:4]
    for offset in range(1, 4):
        summed = summed + pltpu.roll(signal, offset, 0) * gates[offset - 1] * taps[3 - offset : 4 - offset]
    return summed


def chunk_masks(segc_ref, segr_ref, chunk):
    start = chunk * CHUNK
    col = segc_ref[start : start + CHUNK, :]
    row = segr_ref[:, start : start + CHUNK]
    same = col == row
    last = segc_ref[start + CHUNK - 1 : start + CHUNK, :]
    if chunk == 0:
        carry = jnp.zeros(col.shape, F32)
        carry_last = jnp.zeros(last.shape, F32)
    else:
        prior = segc_ref[start - 1 : start, :]
        carry = (col == prior).astype(F32)
        carry_last = (last == prior).astype(F32)
    tail = (col == last).astype(F32)
    return same, carry, carry_last, tail


def head_logits(beta_ref, head):
    lanes = lax.broadcasted_iota(jnp.int32, beta_ref.shape, 1)
    return jnp.sum(jnp.where(lanes == head, beta_ref[...], 0.0), axis=1, keepdims=True)


def forward_kernel(heads, passes, proj_ref, beta_ref, conv_ref, gain_ref, segc_ref, segr_ref,
                   mixed_ref, out_ref, writes_ref, solve_ref, state_ref, q_scr, k_scr, v_scr):
    group = pl.program_id(0)
    length = proj_ref.shape[0]
    chunks = length // CHUNK
    width = 128
    mul = mul3 if passes == 3 else mul1
    seg_full = jnp.broadcast_to(segc_ref[...], (length, width))
    gates = [allowed_rows(seg_full, offset) for offset in (1, 2, 3)]
    betas = []
    for h in range(heads):
        for which, scr in enumerate((q_scr, k_scr, v_scr)):
            column = (which * heads + h) * width
            signal = proj_ref[:, column : column + width]
            mixed_in = conv_taps(signal, conv_ref[which, :, h * width : (h + 1) * width], gates)
            value = mixed_in * jax.nn.sigmoid(mixed_in)
            if which < 2:
                value = value * lax.rsqrt(jnp.sum(value * value, axis=1, keepdims=True) + 1e-6)
            scr[:, h * width : (h + 1) * width] = value
        betas.append(jax.nn.sigmoid(head_logits(beta_ref, group * heads + h)))
    rows, cols = iotas(CHUNK)
    masks = [chunk_masks(segc_ref, segr_ref, c) for c in range(chunks)]
    items = [(h, c) for c in range(chunks) for h in range(heads)]

    def part(scr, h, c):
        return scr[c * CHUNK : (c + 1) * CHUNK, h * width : (h + 1) * width]

    def beta_of(h, c):
        return betas[h][c * CHUNK : (c + 1) * CHUNK]

    system, inverse = {}, {}
    for h, c in items:
        keys = split2(part(k_scr, h, c))
        inner = mul(keys, keys, NT)
        keep = masks[c][0] & (rows > cols)
        system[h, c] = jnp.where(keep, inner * beta_of(h, c), 0.0)
        first = (rows // 2 == cols // 2)
        inverse[h, c] = jnp.where(rows == cols, 1.0, jnp.where(first, -system[h, c], 0.0))
    size = 2
    while size < CHUNK:
        off = (rows // (2 * size) == cols // (2 * size)) & (rows // size != cols // size)
        mid = {}
        for it in items:
            step = jnp.where(off, system[it], 0.0)
            if passes == 3:
                mid[it] = mul3(split2(inverse[it]), split2(step), NN)
            else:
                mid[it] = dot1(inverse[it].astype(BF16), step.astype(BF16), NN)
        for it in items:
            if passes == 3:
                inverse[it] = inverse[it] - mul3(split2(mid[it]), split2(inverse[it]), NN)
            else:
                inverse[it] = inverse[it] - dot1(mid[it].astype(BF16), inverse[it].astype(BF16), NN)
        size *= 2
    scores, fresh, decay = {}, {}, {}
    for h, c in items:
        same, carry, carry_last, tail = masks[c]
        keys, queries, values = part(k_scr, h, c), part(q_scr, h, c), part(v_scr, h, c)
        scores[h, c] = split2(jnp.where(same & (rows >= cols), mul(split2(queries), split2(keys), NT), 0.0))
        solver = split2(inverse[h, c])
        fresh[h, c] = mul(solver, split2(values * beta_of(h, c)), NN)
        decay[h, c] = split2(mul(solver, split2(keys * (beta_of(h, c) * carry)), NN))
        solve_ref[c * CHUNK : (c + 1) * CHUNK, h * width : (h + 1) * width] = inverse[h, c]
    state = {h: jnp.zeros((width, width), F32) for h in range(heads)}
    gain = gain_ref[...]
    for c in range(chunks):
        same, carry, carry_last, tail = masks[c]
        span = slice(c * CHUNK, (c + 1) * CHUNK)
        for h in range(heads):
            state_ref[span, h * width : (h + 1) * width] = state[h]
        writes = {}
        if c == 0:
            for h in range(heads):
                writes[h] = fresh[h, c]
        else:
            split_state = {h: split2(state[h]) for h in range(heads)}
            for h in range(heads):
                writes[h] = fresh[h, c] - mul(decay[h, c], split_state[h], NN)
        for h in range(heads):
            lanes = slice(h * width, (h + 1) * width)
            writes_ref[span, lanes] = writes[h]
            result = mul(scores[h, c], split2(writes[h]), NN)
            if c > 0:
                result = result + carry * mul(split2(part(q_scr, h, c)), split_state[h], NN)
            out_ref[span, lanes] = result
            scale = lax.rsqrt(jnp.mean(result * result, axis=1, keepdims=True) + 1e-5)
            mixed_ref[span, lanes] = (result * scale * gain).astype(BF16)
        if c + 1 < chunks:
            for h in range(heads):
                add = mul(split2(part(k_scr, h, c)), split2(writes[h] * tail), TN)
                state[h] = carry_last * state[h] + add


def backward_kernel(heads, passes, proj_ref, beta_ref, conv_ref, gain_ref, segc_ref, segr_ref,
                    out_ref, writes_ref, solve_ref, state_ref, gmix_ref,
                    gproj_ref, gbeta_ref, gconv_ref, ggain_ref,
                    q_scr, k_scr, v_scr, gq_scr, gk_scr, gv_scr, do_scr):
    group = pl.program_id(0)
    length = proj_ref.shape[0]
    chunks = length // CHUNK
    width = 128
    mul = mul3 if passes == 3 else mul1
    seg_full = jnp.broadcast_to(segc_ref[...], (length, width))
    gates = [allowed_rows(seg_full, offset) for offset in (1, 2, 3)]
    gain = gain_ref[...]

    @pl.when(group == 0)
    def _():
        gbeta_ref[...] = jnp.zeros_like(gbeta_ref)
        ggain_ref[...] = jnp.zeros_like(ggain_ref)

    def convolved(which, h):
        column = (which * heads + h) * width
        signal = proj_ref[:, column : column + width]
        mixed_in = conv_taps(signal, conv_ref[which, :, h * width : (h + 1) * width], gates)
        gate = jax.nn.sigmoid(mixed_in)
        return signal, mixed_in, gate

    betas = []
    for h in range(heads):
        lanes = slice(h * width, (h + 1) * width)
        for which, scr in enumerate((q_scr, k_scr, v_scr)):
            _, mixed_in, gate = convolved(which, h)
            value = mixed_in * gate
            if which < 2:
                value = value * lax.rsqrt(jnp.sum(value * value, axis=1, keepdims=True) + 1e-6)
            scr[:, lanes] = value
        betas.append(jax.nn.sigmoid(head_logits(beta_ref, group * heads + h)))
        result, grad = out_ref[:, lanes], gmix_ref[:, lanes]
        scale = lax.rsqrt(jnp.mean(result * result, axis=1, keepdims=True) + 1e-5)
        unit = result * scale
        ggain_ref[...] += jnp.sum(unit * grad, axis=0, keepdims=True)
        scaled = grad * gain
        do_scr[:, lanes] = scale * (scaled - unit * jnp.mean(unit * scaled, axis=1, keepdims=True))
    rows, cols = iotas(CHUNK)
    masks = [chunk_masks(segc_ref, segr_ref, c) for c in range(chunks)]
    items = [(h, c) for c in range(chunks) for h in range(heads)]

    def part(scr, h, c):
        return scr[c * CHUNK : (c + 1) * CHUNK, h * width : (h + 1) * width]

    def beta_of(h, c):
        return betas[h][c * CHUNK : (c + 1) * CHUNK]

    inner, base, reach, gscore = {}, {}, {}, {}
    for h, c in items:
        same, carry, carry_last, tail = masks[c]
        keys, queries = split2(part(k_scr, h, c)), split2(part(q_scr, h, c))
        grads, writes = split2(part(do_scr, h, c)), split2(part(writes_ref, h, c))
        inner[h, c] = mul(keys, keys, NT)
        causal = same & (rows >= cols)
        scores = split2(jnp.where(causal, mul(queries, keys, NT), 0.0))
        solver = split2(part(solve_ref, h, c))
        base[h, c] = mul(solver, split2(mul(scores, grads, TN)), TN)
        if c + 1 < chunks:
            reach[h, c] = split2(mul(solver, split2(part(k_scr, h, c) * tail), TN))
        gscore = split2(jnp.where(causal, mul(grads, writes, NT), 0.0))
        gq = mul(gscore, keys, NN)
        gk = mul(gscore, queries, TN)
        span, lanes = slice(c * CHUNK, (c + 1) * CHUNK), slice(h * width, (h + 1) * width)
        if c > 0:
            gq = gq + mul(split2(part(do_scr, h, c) * carry), split2(part(state_ref, h, c)), NT)
        gq_scr[span, lanes] = gq
        gk_scr[span, lanes] = gk
    gstate = {}
    gbetas = {}
    for c in reversed(range(chunks)):
        same, carry, carry_last, tail = masks[c]
        span = slice(c * CHUNK, (c + 1) * CHUNK)
        gtarget = {}
        for h in range(heads):
            gtarget[h] = base[h, c]
            if c + 1 < chunks:
                gtarget[h] = gtarget[h] + mul(reach[h, c], split2(gstate[h]), NN)
        for h in range(heads):
            lanes = slice(h * width, (h + 1) * width)
            gk = gk_scr[span, lanes]
            keys = split2(part(k_scr, h, c))
            beta = beta_of(h, c)
            writes = part(writes_ref, h, c)
            split_target = split2(gtarget[h])
            if c + 1 < chunks:
                gk = gk + mul(split2(writes * tail), split2(gstate[h]), NT)
            strict = same & (rows > cols)
            gsys = jnp.where(strict, mul(split_target, split2(writes), NT), 0.0)
            ginner = split2(gsys * beta)
            gbeta = -jnp.sum(gsys * inner[h, c], axis=1, keepdims=True)
            gk = gk - mul(ginner, keys, NN) - mul(ginner, keys, TN)
            target = part(v_scr, h, c)
            if c > 0:
                states = split2(part(state_ref, h, c))
                target = target - carry * mul(keys, states, NN)
                grecall = gtarget[h] * (beta * carry)
                split_recall = split2(grecall)
                gk = gk - mul(split_recall, states, NT)
                new_state = mul(split2(part(q_scr, h, c)), split2(part(do_scr, h, c) * carry), TN)
                new_state = new_state - mul(keys, split_recall, TN)
                if c + 1 < chunks:
                    new_state = new_state + carry_last * gstate[h]
                gstate[h] = new_state
            gbeta = gbeta + jnp.sum(gtarget[h] * target, axis=1, keepdims=True)
            gbetas[h, c] = gbeta * beta * (1.0 - beta)
            gk_scr[span, lanes] = gk
            gv_scr[span, lanes] = gtarget[h] * beta
    for c in range(chunks):
        span = slice(c * CHUNK, (c + 1) * CHUNK)
        lane_ids = lax.broadcasted_iota(jnp.int32, (CHUNK, gbeta_ref.shape[1]), 1)
        total = gbeta_ref[span, :]
        for h in range(heads):
            total = jnp.where(lane_ids == group * heads + h, gbetas[h, c], total)
        gbeta_ref[span, :] = total
    for h in range(heads):
        lanes = slice(h * width, (h + 1) * width)
        for which, (scr, gscr) in enumerate(((q_scr, gq_scr), (k_scr, gk_scr), (v_scr, gv_scr))):
            signal, mixed_in, gate = convolved(which, h)
            grad = gscr[:, lanes]
            if which < 2:
                value = mixed_in * gate
                scale = lax.rsqrt(jnp.sum(value * value, axis=1, keepdims=True) + 1e-6)
                unit = value * scale
                grad = scale * (grad - unit * jnp.sum(unit * grad, axis=1, keepdims=True))
            grad = grad * gate * (1.0 + mixed_in * (1.0 - gate))
            taps = conv_ref[which, :, h * width : (h + 1) * width]
            gsignal = grad * taps[3:4]
            gtaps = [None] * 4
            gtaps[3] = jnp.sum(grad * signal, axis=0, keepdims=True)
            for offset in range(1, 4):
                gated = grad * gates[offset - 1]
                gtaps[3 - offset] = jnp.sum(gated * pltpu.roll(signal, offset, 0), axis=0, keepdims=True)
                gsignal = gsignal + pltpu.roll(gated, length - offset, 0) * taps[3 - offset : 4 - offset]
            gconv_ref[which, :, lanes] = jnp.concatenate(gtaps, axis=0)
            column = (which * heads + h) * width
            gproj_ref[:, column : column + width] = gsignal.astype(BF16)


def mixer_forward(projected, logits, conv, gain, seg_ids, heads, passes):
    length, columns = projected.shape
    groups = columns // (3 * heads * 128)
    wide = heads * 128
    f32 = lambda: jax.ShapeDtypeStruct((length, groups * wide), F32)
    block = pl.BlockSpec((length, wide), lambda g: (0, g))
    fixed = lambda shape: pl.BlockSpec(shape, lambda g: (0,) * len(shape))
    return pl.pallas_call(
        functools.partial(forward_kernel, heads, passes),
        grid=(groups,),
        in_specs=[
            pl.BlockSpec((length, 3 * wide), lambda g: (0, g)),
            fixed((length, 128)),
            pl.BlockSpec((3, 4, wide), lambda g: (0, 0, g)),
            fixed((1, 128)),
            fixed((length, 1)),
            fixed((1, length)),
        ],
        out_specs=[block] * 5,
        out_shape=[jax.ShapeDtypeStruct((length, groups * wide), BF16), f32(), f32(), f32(), f32()],
        scratch_shapes=[pltpu.VMEM((length, wide), F32)] * 3,
        compiler_params=pltpu.CompilerParams(vmem_limit_bytes=56 * 2**20),
        name="mixer_forward",
    )(projected, logits, conv, gain, seg_ids[:, None], seg_ids[None, :])


def mixer_backward(projected, logits, conv, gain, seg_ids, saved, grad_mixed, heads, passes):
    length, columns = projected.shape
    groups = columns // (3 * heads * 128)
    wide = heads * 128
    block = pl.BlockSpec((length, wide), lambda g: (0, g))
    fixed = lambda shape: pl.BlockSpec(shape, lambda g: (0,) * len(shape))
    triple = pl.BlockSpec((length, 3 * wide), lambda g: (0, g))
    taps = pl.BlockSpec((3, 4, wide), lambda g: (0, 0, g))
    return pl.pallas_call(
        functools.partial(backward_kernel, heads, passes),
        grid=(groups,),
        in_specs=[triple, fixed((length, 128)), taps, fixed((1, 128)), fixed((length, 1)), fixed((1, length))] + [block] * 5,
        out_specs=[triple, fixed((length, 128)), taps, fixed((1, 128))],
        out_shape=[
            jax.ShapeDtypeStruct((length, columns), BF16),
            jax.ShapeDtypeStruct((length, 128), F32),
            jax.ShapeDtypeStruct((3, 4, groups * wide), F32),
            jax.ShapeDtypeStruct((1, 128), F32),
        ],
        scratch_shapes=[pltpu.VMEM((length, wide), F32)] * 7,
        compiler_params=pltpu.CompilerParams(vmem_limit_bytes=56 * 2**20),
        name="mixer_backward",
    )(projected, logits, conv, gain, seg_ids[:, None], seg_ids[None, :], *saved, grad_mixed)


HEADS_PER_STEP = 2
PASSES = 3


def matmul(left, right, dims, kind=F32):
    return lax.dot_general(left, right, dims, preferred_element_type=F32).astype(kind)


def ring_order(chips):
    return [2 * i for i in range(chips // 2)] + [2 * i + 1 for i in reversed(range(chips // 2))]


def swap_tensor(value):
    return lax.ppermute(value, "tensor", [(0, 1), (1, 0)])


def pair_sum(part):
    low = part.astype(BF16)
    return low.astype(F32) + swap_tensor(low).astype(F32)


def pair_split(rows, width, core):
    blocks = rows.reshape(rows.shape[0], -1, 2, width)
    own = lax.dynamic_index_in_dim(blocks, core, 2, keepdims=False)
    other = lax.dynamic_index_in_dim(blocks, 1 - core, 2, keepdims=False)
    flat = (rows.shape[0], -1)
    return own.reshape(flat), other.reshape(flat)


def ring_scatter(own, other, chip, forward):
    chips = lax.axis_size("dp") // 2
    rows = own.shape[0] // chips
    order = ring_order(chips)
    place = [order.index(c) for c in range(chips)]
    table = jnp.asarray(order, jnp.int32)
    here = jnp.asarray(place, jnp.int32)[chip]
    turn = 1 if forward else -1
    hops = []
    for position, source in enumerate(order):
        target = order[(position + turn) % chips]
        hops += [(2 * source, 2 * target), (2 * source + 1, 2 * target + 1)]

    def local(step):
        at = table[(here - turn * (step + 1)) % chips] * rows
        a = lax.dynamic_slice_in_dim(own, at, rows, 0)
        b = lax.dynamic_slice_in_dim(other, at, rows, 0)
        return a.astype(F32) + b.astype(F32)

    total = local(0)
    for step in range(1, chips):
        moved = lax.ppermute(total.astype(BF16), "dp", hops)
        total = local(step) + moved.astype(F32)
    return total


def scatter_grads(own, other, chip, core_swap):
    other = lax.ppermute(other, "dp", core_swap)
    half = own.shape[1] // 2
    return jnp.concatenate(
        [
            ring_scatter(own[:, :half], other[:, :half], chip, True),
            ring_scatter(own[:, half:], other[:, half:], chip, False),
        ],
        axis=1,
    )


def norm_back(values, scale, gain, grad):
    scaled = gain * grad
    inner = jnp.mean(values * scaled, axis=-1, keepdims=True)
    gain_grad = jnp.sum(values * scale * grad, axis=0)
    return scale * scaled - values * (scale * scale * scale) * inner, gain_grad


def body(
    tokens,
    segments,
    cotangent,
    norm_gain,
    attn_weight,
    beta_weight,
    conv_weight,
    out_gain,
    mlp_gain,
    mlp_weight,
):
    seg_ids = segments[0]
    length = tokens.shape[0]
    devices = lax.axis_size("dp")
    index = lax.axis_index("dp")
    chip, core = index // 2, index % 2
    core_swap = [(i, i ^ 1) for i in range(devices)]
    rows, _, local_width = attn_weight.shape
    head_count = beta_weight.shape[1]
    piece = conv_weight.shape[3]
    units = mlp_weight.shape[2]
    groups = head_count // HEADS_PER_STEP
    wide = local_width // groups
    model_width = rows * devices
    taps_size = conv_weight.size

    small = jnp.concatenate(
        [norm_gain, mlp_gain, beta_weight.reshape(-1), conv_weight.reshape(-1), out_gain]
    ).astype(BF16)
    small = lax.all_gather(small, "dp", axis=0)
    attn_low = attn_weight.astype(BF16)
    qkv_local = attn_low[:, :3].reshape(rows, 3, groups, wide).transpose(0, 2, 1, 3)
    attn_local = jnp.concatenate([qkv_local.reshape(rows, 3 * local_width), attn_low[:, 3]], axis=1)
    attn_mat = lax.all_gather(attn_local, "dp", axis=0, tiled=True)
    mlp_local = mlp_weight.astype(BF16).reshape(rows, 3 * units)
    mlp_mat = lax.all_gather(mlp_local, "dp", axis=0, tiled=True)
    qkv_mat, out_mat = attn_mat[:, : 3 * local_width], attn_mat[:, 3 * local_width :]
    gu_mat, down_mat = mlp_mat[:, : 2 * units], mlp_mat[:, 2 * units :]
    at = [0, rows, 2 * rows, 2 * rows + rows * head_count]
    gain_in = small[:, at[0] : at[1]].reshape(-1).astype(F32)
    gain_mid = small[:, at[1] : at[2]].reshape(-1).astype(F32)
    beta_mat = small[:, at[2] : at[3]].reshape(model_width, head_count)
    beta_pad = jnp.pad(beta_mat, ((0, 0), (0, 128 - head_count)))
    taps = small[:, at[3] : at[3] + taps_size].reshape(devices, 3, 4, head_count, piece)
    taps = taps.transpose(1, 2, 3, 0, 4).reshape(3, 4, local_width).astype(F32)
    gain_heads = small[:, at[3] + taps_size :].reshape(1, -1).astype(F32)

    inputs_f = tokens.astype(F32)
    scale_in = lax.rsqrt(jnp.mean(inputs_f * inputs_f, axis=-1, keepdims=True) + 1e-05)
    normed = (inputs_f * scale_in * gain_in).astype(BF16)
    projected = matmul(normed, qkv_mat, NN)
    logits = matmul(normed, beta_pad, NN)
    mixed, *saved = mixer_forward(
        projected, logits, taps, gain_heads, seg_ids, HEADS_PER_STEP, PASSES
    )
    hidden = inputs_f + pair_sum(matmul(mixed, out_mat, NT))

    scale_mid = lax.rsqrt(jnp.mean(hidden * hidden, axis=-1, keepdims=True) + 1e-05)
    normed_mlp = (hidden * scale_mid * gain_mid).astype(BF16)
    gate = matmul(normed_mlp, gu_mat[:, :units], NN)
    up = matmul(normed_mlp, gu_mat[:, units:], NN)
    gate_sig = jax.nn.sigmoid(gate)
    activated = (gate * gate_sig * up).astype(BF16)
    grad_act = matmul(cotangent, down_mat, NN)
    grad_gate = (grad_act * up * gate_sig * (1.0 + gate * (1.0 - gate_sig))).astype(BF16)
    grad_up = (grad_act * gate * gate_sig).astype(BF16)
    grad_gu = jnp.concatenate([grad_gate, grad_up], axis=1)
    down = pair_sum(matmul(activated, down_mat, NT))
    result = (hidden + down).astype(BF16)

    mlp_own, mlp_other = pair_split(normed_mlp, rows, core)
    cot_own, cot_other = pair_split(cotangent, rows, core)
    grad_gu_mat = scatter_grads(
        matmul(mlp_own, grad_gu, TN, BF16), matmul(mlp_other, grad_gu, TN, BF16), chip, core_swap
    )
    grad_down_mat = scatter_grads(
        matmul(cot_own, activated, TN, BF16), matmul(cot_other, activated, TN, BF16), chip, core_swap
    )
    mlp_grad = jnp.concatenate([grad_gu_mat, grad_down_mat], axis=1).reshape(rows, 3, units)
    grad_normed_mlp = pair_sum(matmul(grad_gu, gu_mat, NT))
    grad_norm, grad_gain_mid = norm_back(hidden, scale_mid, gain_mid, grad_normed_mlp)
    grad_hidden = cotangent.astype(F32) + grad_norm
    grad_hidden_low = grad_hidden.astype(BF16)

    grad_mixed = matmul(grad_hidden_low, out_mat, NN)
    grad_proj, grad_logits, grad_taps, grad_gain_heads = mixer_backward(
        projected, logits, taps, gain_heads, seg_ids, saved, grad_mixed, HEADS_PER_STEP, PASSES
    )
    grad_logits_low = grad_logits.astype(BF16)
    hid_own, hid_other = pair_split(grad_hidden_low, rows, core)
    in_own, in_other = pair_split(normed, rows, core)
    grad_out_mat = scatter_grads(
        matmul(hid_own, mixed, TN, BF16), matmul(hid_other, mixed, TN, BF16), chip, core_swap
    )
    grad_qkv_mat = scatter_grads(
        matmul(in_own, grad_proj, TN, BF16), matmul(in_other, grad_proj, TN, BF16), chip, core_swap
    )
    grad_qkv_mat = grad_qkv_mat.reshape(rows, groups, 3, wide).transpose(0, 2, 1, 3)
    attn_grad = jnp.concatenate(
        [grad_qkv_mat.reshape(rows, 3, local_width), grad_out_mat[:, None]], axis=1
    )
    grad_beta = matmul(normed, grad_logits_low, TN)[:, :head_count]
    grad_normed = pair_sum(
        matmul(grad_proj, qkv_mat, NT) + matmul(grad_logits_low, beta_pad, NT)
    )
    grad_first, grad_gain_in = norm_back(inputs_f, scale_in, gain_in, grad_normed)
    grad_inputs = grad_hidden + grad_first

    grad_gain_heads = grad_gain_heads[0] + swap_tensor(grad_gain_heads[0])
    grad_taps = grad_taps.reshape(3, 4, head_count, devices, piece).transpose(3, 0, 1, 2, 4)
    packed = jnp.concatenate(
        [
            grad_gain_in.reshape(devices, -1),
            grad_gain_mid.reshape(devices, -1),
            grad_beta.reshape(devices, -1),
            grad_taps.reshape(devices, -1),
            grad_gain_heads.reshape(devices, -1),
        ],
        axis=1,
    )
    packed = jnp.sum(lax.all_to_all(packed, "dp", 0, 0, tiled=True), axis=0)
    return (
        result,
        grad_inputs,
        packed[at[0] : at[1]],
        attn_grad,
        packed[at[2] : at[3]].reshape(rows, head_count),
        packed[at[3] : at[3] + taps_size].reshape(conv_weight.shape),
        packed[at[3] + taps_size :],
        packed[at[1] : at[2]],
        mlp_grad,
    )


def solution(mesh):
    return jax.shard_map(
        body,
        mesh=mesh,
        in_specs=(
            P("dp", None),
            P("dp", None),
            P("dp", None),
            P("dp"),
            P("dp", None, "tensor"),
            P("dp", "tensor"),
            P(None, None, "tensor", "dp"),
            P("dp"),
            P("dp"),
            P("dp", None, "tensor"),
        ),
        out_specs=(
            P("dp", None),
            P("dp", None),
            P("dp"),
            P("dp", None, "tensor"),
            P("dp", "tensor"),
            P(None, None, "tensor", "dp"),
            P("dp"),
            P("dp"),
            P("dp", None, "tensor"),
        ),
        check_vma=False,
    )
```

time: 2770 us -> 974 us (0.35)
  waiting for transfers between devices: 1250 us -> 374 us
  other arithmetic: 788 us -> 87 us
  matrix products: 384 us -> 156 us
  blocking collectives: 181 us -> 24.4 us
  Pallas kernels: 0 us -> 82.2 us
  starting transfers between devices: 0.5 us -> 72.7 us
    reduce_scatter x3 -> x0, waiting for transfers between devices: 934 us -> none  [the longest x2 883 us: body(): lax.psum_scatter(jnp.concatenate([first_part, last_part[:, None]], axis=1...]
    another operation x73 -> x2, other arithmetic: 632 us -> 0.01 us  [the longest x64 632 us: delta_block(): lax.linalg.triangular_solve(system, target, left_side=True, lower=True, u...]
    ppermute x0 -> x65, waiting for transfers between devices: none -> 222 us  [the longest x56 175 us: ring_scatter(): moved = lax.ppermute(total.astype(BF16), 'dp', hops)]
    dot_general x191 -> x19, matrix products: 359 us -> 155 us  [matmul(): lax.dot_general(left, right, dims, preferred_element_type=F32).astype(kind)]
    psum x3 -> x0, waiting for transfers between devices: 114 us -> none  [the longest x1 67.2 us: body(): attended = lax.psum(attn_part, 'tensor')]
    unnamed x2 -> x0, blocking collectives: 99.7 us -> none
    pallas_call x0 -> x2, Pallas kernels: none -> 82.2 us  [the longest x1 52.5 us: mixer_backward(): pl.pallas_call(functools.partial(backward_kernel, heads, passes), grid=(g...]
    ppermute x0 -> x65, starting transfers between devices: none -> 69.1 us  [the longest x56 62.4 us: ring_scatter(): moved = lax.ppermute(total.astype(BF16), 'dp', hops)]
  transfers between devices with their start and end apart: 8 -> 68, of which waited for: 7 -> 39; matrix products, arithmetic and copies ran while one was open for 7% -> 31% of each run, Pallas kernels for 0% -> 8%
where the time goes in v1:
time: 974 us; the launch traced here: 968 us
  waiting for transfers between devices  374 us (38%)
  matrix products  156 us (16%)
  local copies, waits for them, and re-layouts  136 us (14%)
  other arithmetic  87 us (9%)
  Pallas kernels  82.2 us (8%)
  starting transfers between devices  72.7 us (7%)
  between operations  36.1 us (4%)
  blocking collectives  24.4 us (3%)
    ppermute x56, waiting for transfers between devices, ring_scatter(): moved = lax.ppermute(total.astype(BF16), 'dp', hops)  175 us
    dot_general x19, matrix products, matmul(): lax.dot_general(left, right, dims, preferred_element_type=F32).astype(kind)  155 us
    all_gather x1, waiting for transfers between devices, body(): attn_mat = lax.all_gather(attn_local, 'dp', axis=0, tiled=True)  94.9 us
    ppermute x56, starting transfers between devices, ring_scatter(): moved = lax.ppermute(total.astype(BF16), 'dp', hops)  62.4 us
    all_gather x1, waiting for transfers between devices, body(): mlp_mat = lax.all_gather(mlp_local, 'dp', axis=0, tiled=True)  57.6 us
    pallas_call x1, Pallas kernels, mixer_backward(): pl.pallas_call(functools.partial(backward_kernel, heads, passes), grid=(g...  52.5 us
    unnamed x133, local copies, waits for them, and re-layouts  49.1 us
    ppermute x5, waiting for transfers between devices, swap_tensor(): return lax.ppermute(value, 'tensor', [(0, 1), (1, 0)])  46.4 us
  transfers between devices with their start and end apart: 68, of which 39 were waited for; matrix products, arithmetic and copies ran while one was open for 31% of the time, Pallas kernels for 8%

profile of v1, /device:TPU:0, one launch (start us, length us, event | category | flops | bytes accessed | tf_op | source)
XLA Modules:
  0.0 968.3 jit_solution(8155020699040295986)
XLA Ops:
  15.8 24.4 %all-gather = bf16[16,1,2056]{2,1,0:T(2,128)(2,1)S(1)} all-gather(bf16[1,1,2056]{2,1,0:T(2,128)(2,1)S(1)} %bitcast.141), channel_id=1, replica_groups=mesh['dp'=16,'tensor'=2] {'dp'}, dimensions={0}, use_global_device_ids=true | all-gather | bytes 69904 | tf_op jit(solution)/shard_map/all_gather | solution.py:468
  50.0 94.9 %all-gather.4.cloned.1.call-done = bf16[2048,4096]{0,1:T(8,128)(2,1)} async-done(((bf16[128,4096]{0,1:T(8,128)(2,1)}), bf16[2048,4096]{0,1:T(8,128)(2,1)}) %all-gather.4.cloned.1.call-update) | async-done | bytes 16777232 | tf_op jit(solution)/shard_map/all_gather | solution.py:472
  144.9 12.3 %fusion.8.proj_ref = f32[512,3072]{1,0:T(8,128)} fusion(bf16[512,2048]{1,0:T(8,128)(2,1)} %copy-done.4, bf16[2048,4096]{0,1:T(8,128)(2,1)} %all-gather.4.cloned.1.call-done), kind=kOutput, calls=%fused_computation.10 | convolution fusion | flops 6442450944 | bytes 20971520 | tf_op jit(solution)/shard_map/dot_general | solution.py:369
  157.1 29.7 %mixer_forward.1 = (bf16[512,1024]{1,0:T(8,128)(2,1)}, f32[512,1024]{1,0:T(8,128)}, f32[512,1024]{1,0:T(8,128)}, f32[512,1024]{1,0:T(8,128)}, f32[512,1024]{1,0:T(8,128)}) custom-call(f32[512,3072]{1,0:T(8,128)} %fusion.8.proj_ref, f32[512,128]{1,0:T(8,128)} %fusion.39.beta_ref, f32[3,4,1024]{2,1,0:T(4,128)} %reshape.551.conv_ref, ...), custom_call_target="tpu_custom_call" | custom-call | tf_op jit(solution)/shard_map/mixer_forward/pallas_call | solution.py:320
  186.8 6.3 fusion.32
  228.0 13.2 %collective-permute-done = bf16[512,2048]{1,0:T(8,128)(2,1)} collective-permute-done((bf16[512,2048]{1,0:T(8,128)(2,1)}, bf16[512,2048]{1,0:T(8,128)(2,1)}, u32[]{:S(2)}, u32[]{:S(2)}) %collective-permute-start) | collective-permute-done | bytes 2097184 | tf_op jit(solution)/shard_map/ppermute | solution.py:377
  251.4 6.3 constant_dynamic-slice_fusion.1
  257.8 6.0 copy.157
  263.7 5.8 copy.156
  269.6 57.6 %all-gather.6.cloned.1.call-done = bf16[2048,8448]{0,1:T(8,128)(2,1)} async-done(((bf16[128,8448]{0,1:T(8,128)(2,1)}), bf16[2048,8448]{0,1:T(8,128)(2,1)}) %all-gather.6.cloned.1.call-update) | async-done | bytes 34603024 | tf_op jit(solution)/shard_map/all_gather | solution.py:474
  327.1 11.3 %fusion.10 = f32[512,2816]{1,0:T(8,128)} fusion(bf16[512,2048]{1,0:T(8,128)(2,1)S(1)} %copy-done.16, bf16[2048,8448]{0,1:T(8,128)(2,1)} %all-gather.6.cloned.1.call-done), kind=kOutput, calls=%fused_computation.12 | convolution fusion | flops 5905580032 | bytes 19398656 | tf_op jit(solution)/shard_map/dot_general | solution.py:369
  338.4 11.5 %fusion.2 = f32[512,2816]{1,0:T(8,128)} fusion(bf16[512,2048]{1,0:T(8,128)(2,1)S(1)} %copy-done.18, bf16[2048,8448]{0,1:T(8,128)(2,1)} %all-gather.6.cloned.1.call-done), kind=kOutput, calls=%fused_computation.2 | convolution fusion | flops 5905580032 | bytes 19398656 | tf_op jit(solution)/shard_map/dot_general | solution.py:369
  350.0 15.6 %multiply_convert_fusion.1 = (bf16[512,2816]{1,0:T(8,128)(2,1)}, bf16[512,2816]{1,0:T(8,128)(2,1)}, bf16[512,2816]{1,0:T(8,128)(2,1)}) fusion(f32[512,2816]{1,0:T(8,128)} %fusion.10, f32[512,2816]{1,0:T(8,128)} %fusion.2, bf16[512,2048]{1,0:T(8,128)(2,1)S(1)} %copy-done.18, bf16[2048,8448]{0,1:T(8,128)(2,1)} %all-gather.6.cloned.1.call-done), kind=kOutput, calls=%fused_computation.23 | convolution fusion | flops 5928648704 | bytes 33816576 | tf_op jit(solution)/shard_map/dot_general | solution.py:369
  365.5 19.1 %fusion.29 = bf16[512,2048]{1,0:T(8,128)(2,1)} fusion(bf16[2048,8448]{0,1:T(8,128)(2,1)} %all-gather.6.cloned.1.call-done, bf16[512,2816]{1,0:T(8,128)(2,1)} %get-tuple-element.86, bf16[512,2816]{1,0:T(8,128)(2,1)} %get-tuple-element.84), kind=kOutput, calls=%fused_computation.55 | convolution fusion | flops 11823742976 | bytes 30932992 | tf_op jit(solution)/shard_map/dot_general | solution.py:369
  386.1 11.2 %fusion.35 = bf16[512,2048]{1,0:T(8,128)(2,1)} fusion(bf16[512,2816]{1,0:T(8,128)(2,1)} %get-tuple-element.85, bf16[2048,8448]{0,1:T(8,128)(2,1)} %all-gather.6.cloned.1.call-done), kind=kOutput, calls=%fused_computation.57 | convolution fusion | flops 5906628608 | bytes 16515072 | tf_op jit(solution)/shard_map/dot_general | solution.py:369
  397.9 5.1 convolution_convert_fusion.2
  411.4 9.1 convolution_convert_fusion
  421.0 9.2 convolution_convert_fusion.1
  430.2 9.3 fusion.51
  444.5 33.2 %collective-permute-done.1 = bf16[512,2048]{1,0:T(8,128)(2,1)} collective-permute-done((bf16[512,2048]{1,0:T(8,128)(2,1)}, bf16[512,2048]{1,0:T(8,128)(2,1)}, u32[]{:S(2)}, u32[]{:S(2)}) %collective-permute-start.1) | collective-permute-done | bytes 2097184 | tf_op jit(solution)/shard_map/ppermute | solution.py:377
  477.7 7.2 fusion.50
  489.5 5.9 fusion.25.gmix_ref
  495.4 52.5 %mixer_backward.1 = (bf16[512,3072]{1,0:T(8,128)(2,1)}, f32[512,128]{1,0:T(8,128)}, f32[3,4,1024]{2,1,0:T(4,128)}, f32[1,128]{1,0:T(1,128)}) custom-call(f32[512,3072]{1,0:T(8,128)} %fusion.8.proj_ref, f32[512,128]{1,0:T(8,128)} %fusion.39.beta_ref, f32[3,4,1024]{2,1,0:T(4,128)} %reshape.551.conv_ref, f32[1,128]{1,0:T(1,128)} %reshape.552.gain_ref, ...), custom_call_target="tpu_custom_call" | custom-call | tf_op jit(solution)/shard_map/mixer_backward/pallas_call | solution.py:347
  548.9 10.7 %fusion.6 = f32[512,2048]{1,0:T(8,128)S(1)} fusion(bf16[512,3072]{1,0:T(8,128)(2,1)} %get-tuple-element.23, bf16[2048,4096]{0,1:T(8,128)(2,1)} %all-gather.4.cloned.1.call-done), kind=kOutput, calls=%fused_computation.8 | convolution fusion | flops 6442450944 | bytes 19922944 | tf_op jit(solution)/shard_map/dot_general | solution.py:369
  563.8 9.9 %constant_dynamic-slice_fusion.5 = (bf16[512,8,1,128]{3,2,1,0:T(2,128)(2,1)}, bf16[512,8,1,128]{3,2,1,0:T(2,128)(2,1)}, bf16[512,8,1,128]{3,2,1,0:T(2,128)(2,1)}, bf16[512,8,1,128]{3,2,1,0:T(2,128)(2,1)}) fusion(bf16[512,8,2,128]{3,2,1,0:T(2,128)(2,1)S(1)} %copy-done.8, s32[]{:T(128)S(6)} %select_n.739, s32[]{:T(128)S(6)} %select_n.745, ...), kind=kLoop, calls=%fused_computation.140 | loop fusion | bytes 8388616 | tf_op jit(solution)/shard_map/jit(dynamic_index_in_dim)/dynamic_slice | solution.py:387
  584.9 7.3 convolution_convert_fusion.4
  594.9 7.3 convolution_convert_fusion.5
  682.4 6.9 collective-permute-done.58
  692.2 6.2 collective-permute-done.59
  701.2 5.9 collective-permute-done.60
  710.0 6.1 collective-permute-done.61
  718.9 7.1 collective-permute-done.62
  736.5 5.9 collective-permute-done.64
  749.2 8.7 collective-permute-done.13
  760.9 7.8 collective-permute-done.14
  771.9 6.9 collective-permute-done.15
  782.1 5.7 collective-permute-done.16
  790.2 9.7 collective-permute-done.17
  801.4 9.3 fusion.52
  818.1 13.1 %collective-permute-done.43 = bf16[128,2816]{1,0:T(8,128)(2,1)S(1)} collective-permute-done((bf16[128,2816]{1,0:T(8,128)(2,1)S(1)}, bf16[128,2816]{1,0:T(8,128)(2,1)S(1)}, u32[]{:S(2)}, u32[]{:S(2)}) %collective-permute-start.43) | collective-permute-done | bytes 720928 | tf_op jit(solution)/shard_map/ppermute | solution.py:414
  836.6 6.0 collective-permute-done.36
  853.8 8.2 collective-permute-done.37
  872.8 7.7 collective-permute-done.38
  889.8 8.3 collective-permute-done.39
  909.5 8.9 collective-permute-done.40
  937.1 8.7 collective-permute-done.42
  949.8 5.8 copy.145
  955.6 5.7 copy.148
  (383 shorter events, 281.6 us)
Async XLA Ops:
  7.2 137.7 %all-gather.4.cloned.1.call-start = ((), (), s32[]{:S(2)}) async-start(), calls=%async_computation.1 | async-start | bytes 17825792 | tf_op jit(solution)/shard_map/all_gather | solution.py:472
  10.5 316.6 %all-gather.6.cloned.1.call-start = ((), (), s32[]{:S(2)}) async-start(), calls=%async_computation.2 | async-start | bytes 36765696 | tf_op jit(solution)/shard_map/all_gather | solution.py:474
  193.1 48.1 %collective-permute-start = (bf16[512,2048]{1,0:T(8,128)(2,1)}, bf16[512,2048]{1,0:T(8,128)(2,1)}, u32[]{:S(2)}, u32[]{:S(2)}) collective-permute-start(bf16[512,2048]{1,0:T(8,128)(2,1)} %fusion.32), channel_id=1, source_target_pairs={{0,1},{1,0},{2,3},{3,2},{4,5},{5,4},{6,7},{7,6},{8,9},{9,8},{10,11... | collective-permute-start | bytes 6291464 | tf_op jit(solution)/shard_map/ppermute | solution.py:377
  384.7 54.8 %collective-permute-start.2 = (bf16[512,2048]{1,0:T(8,128)(2,1)}, bf16[512,2048]{1,0:T(8,128)(2,1)}, u32[]{:S(2)}, u32[]{:S(2)}) collective-permute-start(bf16[512,2048]{1,0:T(8,128)(2,1)} %fusion.29), channel_id=1, source_target_pairs={{0,1},{1,0},{2,3},{3,2},{4,5},{5,4},{6,7},{7,6},{8,9},{9,8},{10,11... | collective-permute-start | bytes 6291464 | tf_op jit(solution)/shard_map/ppermute | solution.py:377
  397.2 80.5 %collective-permute-start.1 = (bf16[512,2048]{1,0:T(8,128)(2,1)}, bf16[512,2048]{1,0:T(8,128)(2,1)}, u32[]{:S(2)}, u32[]{:S(2)}) collective-permute-start(bf16[512,2048]{1,0:T(8,128)(2,1)} %fusion.35), channel_id=1, source_target_pairs={{0,1},{1,0},{2,3},{3,2},{4,5},{5,4},{6,7},{7,6},{8,9},{9,8},{10,11... | collective-permute-start | bytes 6291464 | tf_op jit(solution)/shard_map/ppermute | solution.py:377
  402.9 272.8 %collective-permute-start.50 = (bf16[1024,2816]{1,0:T(8,128)(2,1)}, bf16[1024,2816]{1,0:T(8,128)(2,1)}, u32[]{:S(2)}, u32[]{:S(2)}) collective-permute-start(bf16[1024,2816]{1,0:T(8,128)(2,1)} %convolution_convert_fusion.2), channel_id=1, source_target_pairs={{0,2},{2,0},{4,6},{6,4},{8,10},{10,8},{12,14},{14,12},{16,18},{18,... | collective-permute-start | bytes 17301512 | tf_op jit(solution)/shard_map/ppermute | solution.py:420
  420.5 380.9 %collective-permute-start.35 = (bf16[1024,5632]{1,0:T(8,128)(2,1)}, bf16[1024,5632]{1,0:T(8,128)(2,1)}, u32[]{:S(2)}, u32[]{:S(2)}) collective-permute-start(bf16[1024,5632]{1,0:T(8,128)(2,1)} %convolution_convert_fusion), channel_id=1, source_target_pairs={{0,2},{2,0},{4,6},{6,4},{8,10},{10,8},{12,14},{14,12},{16,18},{18,... | collective-permute-start | bytes 34603016 | tf_op jit(solution)/shard_map/ppermute | solution.py:420
  561.8 53.8 %collective-permute-start.3 = (bf16[512,2048]{1,0:T(8,128)(2,1)}, bf16[512,2048]{1,0:T(8,128)(2,1)}, u32[]{:S(2)}, u32[]{:S(2)}) collective-permute-start(bf16[512,2048]{1,0:T(8,128)(2,1)} %add_convert_fusion), channel_id=1, source_target_pairs={{0,1},{1,0},{2,3},{3,2},{4,5},{5,4},{6,7},{7,6},{8,9},{9,8},{10,11... | collective-permute-start | bytes 6291464 | tf_op jit(solution)/shard_map/ppermute | solution.py:377
  563.2 51.7 %collective-permute-start.4 = (f32[128]{0:T(128)S(1)}, f32[128]{0:T(128)S(1)}, u32[]{:S(2)}, u32[]{:S(2)}) collective-permute-start(f32[128]{0:T(128)S(1)} %bitcast.142), channel_id=1, source_target_pairs={{0,1},{1,0},{2,3},{3,2},{4,5},{5,4},{6,7},{7,6},{8,9},{9,8},{10,11... | collective-permute-start | bytes 1544 | tf_op jit(solution)/shard_map/ppermute | solution.py:377
  582.3 41.6 %collective-permute-start.20 = (bf16[1024,1024]{0,1:T(8,128)(2,1)}, bf16[1024,1024]{0,1:T(8,128)(2,1)}, u32[]{:S(2)}, u32[]{:S(2)}) collective-permute-start(bf16[1024,1024]{0,1:T(8,128)(2,1)} %convolution_convert_fusion.6), channel_id=1, source_target_pairs={{0,2},{2,0},{4,6},{6,4},{8,10},{10,8},{12,14},{14,12},{16,18},{18,... | collective-permute-start | bytes 6291464 | tf_op jit(solution)/shard_map/ppermute | solution.py:420
  615.0 127.6 %collective-permute-start.5 = (bf16[1024,3072]{1,0:T(8,128)(2,1)}, bf16[1024,3072]{1,0:T(8,128)(2,1)}, u32[]{:S(2)}, u32[]{:S(2)}) collective-permute-start(bf16[1024,3072]{1,0:T(8,128)(2,1)} %convolution_convert_fusion.4), channel_id=1, source_target_pairs={{0,2},{2,0},{4,6},{6,4},{8,10},{10,8},{12,14},{14,12},{16,18},{18,... | collective-permute-start | bytes 18874376 | tf_op jit(solution)/shard_map/ppermute | solution.py:420
  620.4 16.6 %all-to-all-start = ((f32[16,1,2056]{2,1,0:T(1,128)}), f32[16,1,2056]{2,1,0:T(1,128)S(1)}, u32[]{:S(2)}, u32[]{:S(2)}) async-start(f32[16,1,2056]{2,1,0:T(1,128)} %copy.134), calls=%async_computation | async-start | bytes 278528 | tf_op jit(solution)/shard_map/all_to_all | solution.py:559
  679.4 9.9 %collective-permute-start.58 = (bf16[128,1408]{1,0:T(8,128)(2,1)S(1)}, bf16[128,1408]{1,0:T(8,128)(2,1)S(1)}, u32[]{:S(2)}, u32[]{:S(2)}) collective-permute-start(bf16[128,1408]{1,0:T(8,128)(2,1)S(1)} %add_convert_fusion.36), channel_id=1, source_target_pairs={{0,4},{2,6},{8,0},{10,2},{16,8},{18,10},{24,16},{26,18},{28,24},{3... | collective-permute-start | bytes 1081352 | tf_op jit(solution)/shard_map/ppermute | solution.py:414
  681.8 9.8 %collective-permute-start.51 = (bf16[128,1408]{1,0:T(8,128)(2,1)S(1)}, bf16[128,1408]{1,0:T(8,128)(2,1)S(1)}, u32[]{:S(2)}, u32[]{:S(2)}) collective-permute-start(bf16[128,1408]{1,0:T(8,128)(2,1)S(1)} %add_convert_fusion.43), channel_id=1, source_target_pairs={{0,8},{2,10},{8,16},{10,18},{16,24},{18,26},{24,28},{26,30},{28,20... | collective-permute-start | bytes 1081352 | tf_op jit(solution)/shard_map/ppermute | solution.py:414
  689.5 9.0 collective-permute-start.59
  691.8 8.9 collective-permute-start.52
  700.9 8.9 collective-permute-start.53
  707.3 8.9 collective-permute-start.61
  716.3 9.7 %collective-permute-start.62 = (bf16[128,1408]{1,0:T(8,128)(2,1)S(1)}, bf16[128,1408]{1,0:T(8,128)(2,1)S(1)}, u32[]{:S(2)}, u32[]{:S(2)}) collective-permute-start(bf16[128,1408]{1,0:T(8,128)(2,1)S(1)} %add_convert_fusion.32), channel_id=1, source_target_pairs={{0,4},{2,6},{8,0},{10,2},{16,8},{18,10},{24,16},{26,18},{28,24},{3... | collective-permute-start | bytes 1081352 | tf_op jit(solution)/shard_map/ppermute | solution.py:414
  718.8 9.8 %collective-permute-start.55 = (bf16[128,1408]{1,0:T(8,128)(2,1)S(1)}, bf16[128,1408]{1,0:T(8,128)(2,1)S(1)}, u32[]{:S(2)}, u32[]{:S(2)}) collective-permute-start(bf16[128,1408]{1,0:T(8,128)(2,1)S(1)} %add_convert_fusion.39), channel_id=1, source_target_pairs={{0,8},{2,10},{8,16},{10,18},{16,24},{18,26},{24,28},{26,30},{28,20... | collective-permute-start | bytes 1081352 | tf_op jit(solution)/shard_map/ppermute | solution.py:414
  736.4 12.2 %collective-permute-start.57 = (bf16[128,1408]{1,0:T(8,128)(2,1)S(1)}, bf16[128,1408]{1,0:T(8,128)(2,1)S(1)}, u32[]{:S(2)}, u32[]{:S(2)}) collective-permute-start(bf16[128,1408]{1,0:T(8,128)(2,1)S(1)} %add_convert_fusion.37), channel_id=1, source_target_pairs={{0,8},{2,10},{8,16},{10,18},{16,24},{18,26},{24,28},{26,30},{28,20... | collective-permute-start | bytes 1081352 | tf_op jit(solution)/shard_map/ppermute | solution.py:414
  746.4 11.5 %collective-permute-start.13 = (bf16[128,1536]{1,0:T(8,128)(2,1)S(1)}, bf16[128,1536]{1,0:T(8,128)(2,1)S(1)}, u32[]{:S(2)}, u32[]{:S(2)}) collective-permute-start(bf16[128,1536]{1,0:T(8,128)(2,1)S(1)} %add_convert_fusion.22), channel_id=1, source_target_pairs={{0,4},{2,6},{8,0},{10,2},{16,8},{18,10},{24,16},{26,18},{28,24},{3... | collective-permute-start | bytes 1179656 | tf_op jit(solution)/shard_map/ppermute | solution.py:414
  748.9 11.2 %collective-permute-start.6 = (bf16[128,1536]{1,0:T(8,128)(2,1)S(1)}, bf16[128,1536]{1,0:T(8,128)(2,1)S(1)}, u32[]{:S(2)}, u32[]{:S(2)}) collective-permute-start(bf16[128,1536]{1,0:T(8,128)(2,1)S(1)} %add_convert_fusion.29), channel_id=1, source_target_pairs={{0,8},{2,10},{8,16},{10,18},{16,24},{18,26},{24,28},{26,30},{28,20... | collective-permute-start | bytes 1179656 | tf_op jit(solution)/shard_map/ppermute | solution.py:414
  758.1 10.7 %collective-permute-start.14 = (bf16[128,1536]{1,0:T(8,128)(2,1)S(1)}, bf16[128,1536]{1,0:T(8,128)(2,1)S(1)}, u32[]{:S(2)}, u32[]{:S(2)}) collective-permute-start(bf16[128,1536]{1,0:T(8,128)(2,1)S(1)} %add_convert_fusion.21), channel_id=1, source_target_pairs={{0,4},{2,6},{8,0},{10,2},{16,8},{18,10},{24,16},{26,18},{28,24},{3... | collective-permute-start | bytes 1179656 | tf_op jit(solution)/shard_map/ppermute | solution.py:414
  760.3 10.4 %collective-permute-start.7 = (bf16[128,1536]{1,0:T(8,128)(2,1)S(1)}, bf16[128,1536]{1,0:T(8,128)(2,1)S(1)}, u32[]{:S(2)}, u32[]{:S(2)}) collective-permute-start(bf16[128,1536]{1,0:T(8,128)(2,1)S(1)} %add_convert_fusion.28), channel_id=1, source_target_pairs={{0,8},{2,10},{8,16},{10,18},{16,24},{18,26},{24,28},{26,30},{28,20... | collective-permute-start | bytes 1179656 | tf_op jit(solution)/shard_map/ppermute | solution.py:414
  768.9 9.8 %collective-permute-start.15 = (bf16[128,1536]{1,0:T(8,128)(2,1)S(1)}, bf16[128,1536]{1,0:T(8,128)(2,1)S(1)}, u32[]{:S(2)}, u32[]{:S(2)}) collective-permute-start(bf16[128,1536]{1,0:T(8,128)(2,1)S(1)} %add_convert_fusion.20), channel_id=1, source_target_pairs={{0,4},{2,6},{8,0},{10,2},{16,8},{18,10},{24,16},{26,18},{28,24},{3... | collective-permute-start | bytes 1179656 | tf_op jit(solution)/shard_map/ppermute | solution.py:414
  770.9 9.5 collective-permute-start.8
  778.9 8.9 collective-permute-start.16
  788.0 12.0 %collective-permute-start.17 = (bf16[128,1536]{1,0:T(8,128)(2,1)S(1)}, bf16[128,1536]{1,0:T(8,128)(2,1)S(1)}, u32[]{:S(2)}, u32[]{:S(2)}) collective-permute-start(bf16[128,1536]{1,0:T(8,128)(2,1)S(1)} %add_convert_fusion.18), channel_id=1, source_target_pairs={{0,4},{2,6},{8,0},{10,2},{16,8},{18,10},{24,16},{26,18},{28,24},{3... | collective-permute-start | bytes 1179656 | tf_op jit(solution)/shard_map/ppermute | solution.py:414
  789.3 24.3 %collective-permute-start.10 = (bf16[128,1536]{1,0:T(8,128)(2,1)S(1)}, bf16[128,1536]{1,0:T(8,128)(2,1)}, u32[]{:S(2)}, u32[]{:S(2)}) collective-permute-start(bf16[128,1536]{1,0:T(8,128)(2,1)S(1)} %add_convert_fusion.25), channel_id=1, source_target_pairs={{0,8},{2,10},{8,16},{10,18},{16,24},{18,26},{24,28},{26,30},{28,20... | collective-permute-start | bytes 1179656 | tf_op jit(solution)/shard_map/ppermute | solution.py:414
  800.1 34.4 %collective-permute-start.18 = (bf16[128,1536]{1,0:T(8,128)(2,1)S(1)}, bf16[128,1536]{1,0:T(8,128)(2,1)}, u32[]{:S(2)}, u32[]{:S(2)}) collective-permute-start(bf16[128,1536]{1,0:T(8,128)(2,1)S(1)} %add_convert_fusion.17), channel_id=1, source_target_pairs={{0,4},{2,6},{8,0},{10,2},{16,8},{18,10},{24,16},{26,18},{28,24},{3... | collective-permute-start | bytes 1179656 | tf_op jit(solution)/shard_map/ppermute | solution.py:414
  812.1 19.1 %collective-permute-start.43 = (bf16[128,2816]{1,0:T(8,128)(2,1)S(1)}, bf16[128,2816]{1,0:T(8,128)(2,1)S(1)}, u32[]{:S(2)}, u32[]{:S(2)}) collective-permute-start(bf16[128,2816]{1,0:T(8,128)(2,1)S(1)} %add_convert_fusion.8), channel_id=1, source_target_pairs={{0,4},{2,6},{8,0},{10,2},{16,8},{18,10},{24,16},{26,18},{28,24},{3... | collective-permute-start | bytes 2162696 | tf_op jit(solution)/shard_map/ppermute | solution.py:414
  815.0 37.1 %collective-permute-start.11 = (bf16[128,1536]{1,0:T(8,128)(2,1)S(1)}, bf16[128,1536]{1,0:T(8,128)(2,1)S(1)}, u32[]{:S(2)}, u32[]{:S(2)}) collective-permute-start(bf16[128,1536]{1,0:T(8,128)(2,1)S(1)} %add_convert_fusion.24), channel_id=1, source_target_pairs={{0,8},{2,10},{8,16},{10,18},{16,24},{18,26},{24,28},{26,30},{28,20... | collective-permute-start | bytes 1179656 | tf_op jit(solution)/shard_map/ppermute | solution.py:414
  817.3 25.3 %collective-permute-start.36 = (bf16[128,2816]{1,0:T(8,128)(2,1)S(1)}, bf16[128,2816]{1,0:T(8,128)(2,1)S(1)}, u32[]{:S(2)}, u32[]{:S(2)}) collective-permute-start(bf16[128,2816]{1,0:T(8,128)(2,1)S(1)} %add_convert_fusion.15), channel_id=1, source_target_pairs={{0,8},{2,10},{8,16},{10,18},{16,24},{18,26},{24,28},{26,30},{28,20... | collective-permute-start | bytes 2162696 | tf_op jit(solution)/shard_map/ppermute | solution.py:414
  832.9 15.8 %collective-permute-start.44 = (bf16[128,2816]{1,0:T(8,128)(2,1)S(1)}, bf16[128,2816]{1,0:T(8,128)(2,1)S(1)}, u32[]{:S(2)}, u32[]{:S(2)}) collective-permute-start(bf16[128,2816]{1,0:T(8,128)(2,1)S(1)} %add_convert_fusion.7), channel_id=1, source_target_pairs={{0,4},{2,6},{8,0},{10,2},{16,8},{18,10},{24,16},{26,18},{28,24},{3... | collective-permute-start | bytes 2162696 | tf_op jit(solution)/shard_map/ppermute | solution.py:414
  835.8 35.7 %collective-permute-start.19 = (bf16[128,1536]{1,0:T(8,128)(2,1)S(1)}, bf16[128,1536]{1,0:T(8,128)(2,1)S(1)}, u32[]{:S(2)}, u32[]{:S(2)}) collective-permute-start(bf16[128,1536]{1,0:T(8,128)(2,1)S(1)} %add_convert_fusion.16), channel_id=1, source_target_pairs={{0,4},{2,6},{8,0},{10,2},{16,8},{18,10},{24,16},{26,18},{28,24},{3... | collective-permute-start | bytes 1179656 | tf_op jit(solution)/shard_map/ppermute | solution.py:414
  844.0 17.9 %collective-permute-start.37 = (bf16[128,2816]{1,0:T(8,128)(2,1)S(1)}, bf16[128,2816]{1,0:T(8,128)(2,1)S(1)}, u32[]{:S(2)}, u32[]{:S(2)}) collective-permute-start(bf16[128,2816]{1,0:T(8,128)(2,1)S(1)} %add_convert_fusion.14), channel_id=1, source_target_pairs={{0,8},{2,10},{8,16},{10,18},{16,24},{18,26},{24,28},{26,30},{28,20... | collective-permute-start | bytes 2162696 | tf_op jit(solution)/shard_map/ppermute | solution.py:414
  850.4 17.7 %collective-permute-start.45 = (bf16[128,2816]{1,0:T(8,128)(2,1)S(1)}, bf16[128,2816]{1,0:T(8,128)(2,1)S(1)}, u32[]{:S(2)}, u32[]{:S(2)}) collective-permute-start(bf16[128,2816]{1,0:T(8,128)(2,1)S(1)} %add_convert_fusion.6), channel_id=1, source_target_pairs={{0,4},{2,6},{8,0},{10,2},{16,8},{18,10},{24,16},{26,18},{28,24},{3... | collective-permute-start | bytes 2162696 | tf_op jit(solution)/shard_map/ppermute | solution.py:414
  853.4 35.2 %collective-permute-start.12 = (bf16[128,1536]{1,0:T(8,128)(2,1)S(1)}, bf16[128,1536]{1,0:T(8,128)(2,1)S(1)}, u32[]{:S(2)}, u32[]{:S(2)}) collective-permute-start(bf16[128,1536]{1,0:T(8,128)(2,1)S(1)} %add_convert_fusion.23), channel_id=1, source_target_pairs={{0,8},{2,10},{8,16},{10,18},{16,24},{18,26},{24,28},{26,30},{28,20... | collective-permute-start | bytes 1179656 | tf_op jit(solution)/shard_map/ppermute | solution.py:414
  863.4 17.2 %collective-permute-start.38 = (bf16[128,2816]{1,0:T(8,128)(2,1)S(1)}, bf16[128,2816]{1,0:T(8,128)(2,1)S(1)}, u32[]{:S(2)}, u32[]{:S(2)}) collective-permute-start(bf16[128,2816]{1,0:T(8,128)(2,1)S(1)} %add_convert_fusion.13), channel_id=1, source_target_pairs={{0,8},{2,10},{8,16},{10,18},{16,24},{18,26},{24,28},{26,30},{28,20... | collective-permute-start | bytes 2162696 | tf_op jit(solution)/shard_map/ppermute | solution.py:414
  869.8 15.2 %collective-permute-start.46 = (bf16[128,2816]{1,0:T(8,128)(2,1)S(1)}, bf16[128,2816]{1,0:T(8,128)(2,1)S(1)}, u32[]{:S(2)}, u32[]{:S(2)}) collective-permute-start(bf16[128,2816]{1,0:T(8,128)(2,1)S(1)} %add_convert_fusion.5), channel_id=1, source_target_pairs={{0,4},{2,6},{8,0},{10,2},{16,8},{18,10},{24,16},{26,18},{28,24},{3... | collective-permute-start | bytes 2162696 | tf_op jit(solution)/shard_map/ppermute | solution.py:414
  881.9 16.2 %collective-permute-start.39 = (bf16[128,2816]{1,0:T(8,128)(2,1)S(1)}, bf16[128,2816]{1,0:T(8,128)(2,1)S(1)}, u32[]{:S(2)}, u32[]{:S(2)}) collective-permute-start(bf16[128,2816]{1,0:T(8,128)(2,1)S(1)} %add_convert_fusion.12), channel_id=1, source_target_pairs={{0,8},{2,10},{8,16},{10,18},{16,24},{18,26},{24,28},{26,30},{28,20... | collective-permute-start | bytes 2162696 | tf_op jit(solution)/shard_map/ppermute | solution.py:414
  886.6 14.8 %collective-permute-start.47 = (bf16[128,2816]{1,0:T(8,128)(2,1)S(1)}, bf16[128,2816]{1,0:T(8,128)(2,1)S(1)}, u32[]{:S(2)}, u32[]{:S(2)}) collective-permute-start(bf16[128,2816]{1,0:T(8,128)(2,1)S(1)} %add_convert_fusion.4), channel_id=1, source_target_pairs={{0,4},{2,6},{8,0},{10,2},{16,8},{18,10},{24,16},{26,18},{28,24},{3... | collective-permute-start | bytes 2162696 | tf_op jit(solution)/shard_map/ppermute | solution.py:414
  900.5 17.9 %collective-permute-start.40 = (bf16[128,2816]{1,0:T(8,128)(2,1)}, bf16[128,2816]{1,0:T(8,128)(2,1)}, u32[]{:S(2)}, u32[]{:S(2)}) collective-permute-start(bf16[128,2816]{1,0:T(8,128)(2,1)} %add_convert_fusion.11), channel_id=1, source_target_pairs={{0,8},{2,10},{8,16},{10,18},{16,24},{18,26},{24,28},{26,30},{28,20... | collective-permute-start | bytes 2162696 | tf_op jit(solution)/shard_map/ppermute | solution.py:414
  903.9 17.2 %collective-permute-start.48 = (bf16[128,2816]{1,0:T(8,128)(2,1)}, bf16[128,2816]{1,0:T(8,128)(2,1)}, u32[]{:S(2)}, u32[]{:S(2)}) collective-permute-start(bf16[128,2816]{1,0:T(8,128)(2,1)} %add_convert_fusion.3), channel_id=1, source_target_pairs={{0,4},{2,6},{8,0},{10,2},{16,8},{18,10},{24,16},{26,18},{28,24},{3... | collective-permute-start | bytes 2162696 | tf_op jit(solution)/shard_map/ppermute | solution.py:414
  921.1 11.6 %collective-permute-start.41 = (bf16[128,2816]{1,0:T(8,128)(2,1)}, bf16[128,2816]{1,0:T(8,128)(2,1)}, u32[]{:S(2)}, u32[]{:S(2)}) collective-permute-start(bf16[128,2816]{1,0:T(8,128)(2,1)} %add_convert_fusion.10), channel_id=1, source_target_pairs={{0,8},{2,10},{8,16},{10,18},{16,24},{18,26},{24,28},{26,30},{28,20... | collective-permute-start | bytes 2162696 | tf_op jit(solution)/shard_map/ppermute | solution.py:414
  923.7 11.6 %collective-permute-start.49 = (bf16[128,2816]{1,0:T(8,128)(2,1)}, bf16[128,2816]{1,0:T(8,128)(2,1)}, u32[]{:S(2)}, u32[]{:S(2)}) collective-permute-start(bf16[128,2816]{1,0:T(8,128)(2,1)} %add_convert_fusion.2), channel_id=1, source_target_pairs={{0,4},{2,6},{8,0},{10,2},{16,8},{18,10},{24,16},{26,18},{28,24},{3... | collective-permute-start | bytes 2162696 | tf_op jit(solution)/shard_map/ppermute | solution.py:414
  934.5 11.3 %collective-permute-start.42 = (bf16[128,2816]{1,0:T(8,128)(2,1)S(1)}, bf16[128,2816]{1,0:T(8,128)(2,1)S(1)}, u32[]{:S(2)}, u32[]{:S(2)}) collective-permute-start(bf16[128,2816]{1,0:T(8,128)(2,1)S(1)} %add_convert_fusion.9), channel_id=1, source_target_pairs={{0,8},{2,10},{8,16},{10,18},{16,24},{18,26},{24,28},{26,30},{28,20... | collective-permute-start | bytes 2162696 | tf_op jit(solution)/shard_map/ppermute | solution.py:414
  (77 other events, 999.7 us)
Sparse Core Ops, SparseCore 0:
  10.7 134.0 all-gather.3
  146.9 180.1 all-gather.5

commit v2 on v1

--- a/solution.py
+++ b/solution.py
@@ -75,9 +75,9 @@
     return jnp.sum(jnp.where(lanes == head, beta_ref[...], 0.0), axis=1, keepdims=True)
 
 
-def forward_kernel(heads, passes, proj_ref, beta_ref, conv_ref, gain_ref, segc_ref, segr_ref,
+def forward_kernel(heads, passes, first, proj_ref, beta_ref, conv_ref, gain_ref, segc_ref, segr_ref,
                    mixed_ref, out_ref, writes_ref, solve_ref, state_ref, q_scr, k_scr, v_scr):
-    group = pl.program_id(0)
+    group = first + pl.program_id(0)
     length = proj_ref.shape[0]
     chunks = length // CHUNK
     width = 128
@@ -168,11 +168,11 @@
                 state[h] = carry_last * state[h] + add
 
 
-def backward_kernel(heads, passes, proj_ref, beta_ref, conv_ref, gain_ref, segc_ref, segr_ref,
+def backward_kernel(heads, passes, first, proj_ref, beta_ref, conv_ref, gain_ref, segc_ref, segr_ref,
                     out_ref, writes_ref, solve_ref, state_ref, gmix_ref,
                     gproj_ref, gbeta_ref, gconv_ref, ggain_ref,
                     q_scr, k_scr, v_scr, gq_scr, gk_scr, gv_scr, do_scr):
-    group = pl.program_id(0)
+    group = first + pl.program_id(0)
     length = proj_ref.shape[0]
     chunks = length // CHUNK
     width = 128
@@ -181,7 +181,7 @@
     gates = [allowed_rows(seg_full, offset) for offset in (1, 2, 3)]
     gain = gain_ref[...]
 
-    @pl.when(group == 0)
+    @pl.when(pl.program_id(0) == 0)
     def _():
         gbeta_ref[...] = jnp.zeros_like(gbeta_ref)
         ggain_ref[...] = jnp.zeros_like(ggain_ref)
@@ -310,122 +310,382 @@
             gproj_ref[:, column : column + width] = gsignal.astype(BF16)
 
 
-def mixer_forward(projected, logits, conv, gain, seg_ids, heads, passes):
-    length, columns = projected.shape
-    groups = columns // (3 * heads * 128)
+def mixer_specs(length, wide, first):
+    fixed = lambda shape: pl.BlockSpec(shape, lambda g: (0,) * len(shape))
+    return [
+        pl.BlockSpec((length, 3 * wide), lambda g: (0, g + first)),
+        fixed((length, 128)),
+        pl.BlockSpec((3, 4, wide), lambda g: (0, 0, g + first)),
+        fixed((1, 128)),
+        fixed((length, 1)),
+        fixed((1, length)),
+    ]
+
+
+def mixer_forward(projected, logits, conv, gain, seg_ids, heads, passes, first, count):
+    length = projected.shape[0]
     wide = heads * 128
-    f32 = lambda: jax.ShapeDtypeStruct((length, groups * wide), F32)
+    f32 = jax.ShapeDtypeStruct((length, count * wide), F32)
     block = pl.BlockSpec((length, wide), lambda g: (0, g))
+    work = count * heads * length * 128
+    return pl.pallas_call(
+        functools.partial(forward_kernel, heads, passes, first),
+        grid=(count,),
+        in_specs=mixer_specs(length, wide, first),
+        out_specs=[block] * 5,
+        out_shape=[jax.ShapeDtypeStruct((length, count * wide), BF16), f32, f32, f32, f32],
+        scratch_shapes=[pltpu.VMEM((length, wide), F32)] * 3,
+        compiler_params=pltpu.CompilerParams(vmem_limit_bytes=48 * 2**20),
+        cost_estimate=pl.CostEstimate(flops=work * 30000, bytes_accessed=work * 30, transcendentals=work * 4),
+        name="mixer_forward",
+    )(projected, logits, conv, gain, seg_ids[:, None], seg_ids[None, :])
+
+
+def mixer_backward(projected, logits, conv, gain, seg_ids, saved, grad_mixed, heads, passes, first, count, base):
+    length = projected.shape[0]
+    wide = heads * 128
+    block = pl.BlockSpec((length, wide), lambda g: (0, g + first - base))
+    grads = pl.BlockSpec((length, wide), lambda g: (0, g + first))
     fixed = lambda shape: pl.BlockSpec(shape, lambda g: (0,) * len(shape))
+    work = count * heads * length * 128
     return pl.pallas_call(
-        functools.partial(forward_kernel, heads, passes),
-        grid=(groups,),
-        in_specs=[
+        functools.partial(backward_kernel, heads, passes, first),
+        grid=(count,),
+        in_specs=mixer_specs(length, wide, first) + [block] * 4 + [grads],
+        out_specs=[
             pl.BlockSpec((length, 3 * wide), lambda g: (0, g)),
             fixed((length, 128)),
             pl.BlockSpec((3, 4, wide), lambda g: (0, 0, g)),
             fixed((1, 128)),
-            fixed((length, 1)),
-            fixed((1, length)),
         ],
-        out_specs=[block] * 5,
-        out_shape=[jax.ShapeDtypeStruct((length, groups * wide), BF16), f32(), f32(), f32(), f32()],
-        scratch_shapes=[pltpu.VMEM((length, wide), F32)] * 3,
-        compiler_params=pltpu.CompilerParams(vmem_limit_bytes=56 * 2**20),
-        name="mixer_forward",
-    )(projected, logits, conv, gain, seg_ids[:, None], seg_ids[None, :])
-
-
-def mixer_backward(projected, logits, conv, gain, seg_ids, saved, grad_mixed, heads, passes):
-    length, columns = projected.shape
-    groups = columns // (3 * heads * 128)
-    wide = heads * 128
-    block = pl.BlockSpec((length, wide), lambda g: (0, g))
-    fixed = lambda shape: pl.BlockSpec(shape, lambda g: (0,) * len(shape))
-    triple = pl.BlockSpec((length, 3 * wide), lambda g: (0, g))
-    taps = pl.BlockSpec((3, 4, wide), lambda g: (0, 0, g))
-    return pl.pallas_call(
-        functools.partial(backward_kernel, heads, passes),
-        grid=(groups,),
-        in_specs=[triple, fixed((length, 128)), taps, fixed((1, 128)), fixed((length, 1)), fixed((1, length))] + [block] * 5,
-        out_specs=[triple, fixed((length, 128)), taps, fixed((1, 128))],
         out_shape=[
-            jax.ShapeDtypeStruct((length, columns), BF16),
+            jax.ShapeDtypeStruct((length, 3 * count * wide), BF16),
             jax.ShapeDtypeStruct((length, 128), F32),
-            jax.ShapeDtypeStruct((3, 4, groups * wide), F32),
+            jax.ShapeDtypeStruct((3, 4, count * wide), F32),
             jax.ShapeDtypeStruct((1, 128), F32),
         ],
         scratch_shapes=[pltpu.VMEM((length, wide), F32)] * 7,
-        compiler_params=pltpu.CompilerParams(vmem_limit_bytes=56 * 2**20),
+        compiler_params=pltpu.CompilerParams(vmem_limit_bytes=48 * 2**20),
+        cost_estimate=pl.CostEstimate(flops=work * 60000, bytes_accessed=work * 40, transcendentals=work * 8),
         name="mixer_backward",
     )(projected, logits, conv, gain, seg_ids[:, None], seg_ids[None, :], *saved, grad_mixed)
 
 
+LIMIT = 40 * 2**20
+
+
+def cost(flops, *arrays):
+    size = sum(a.size * a.dtype.itemsize for a in arrays)
+    return pl.CostEstimate(flops=flops, bytes_accessed=size, transcendentals=0)
+
+
+def whole(array):
+    return pl.BlockSpec(array.shape, lambda i: (0,) * array.ndim)
+
+
+def stacked(refs):
+    return jnp.concatenate([ref[...] for ref in refs], axis=0)
+
+
+def rows_kernel(count, left_ref, *refs):
+    out_ref = refs[count]
+    out_ref[...] = dot1(left_ref[...], stacked(refs[:count]), NN).astype(out_ref.dtype)
+
+
+def times_rows(left, blocks, start, columns, tile, kind):
+    rows = blocks[0].shape[0]
+    first = start // tile
+    out = jax.ShapeDtypeStruct((left.shape[0], columns), kind)
+    return pl.pallas_call(
+        functools.partial(rows_kernel, len(blocks)),
+        grid=(columns // tile,),
+        in_specs=[whole(left)]
+        + [pl.BlockSpec((rows, tile), lambda i: (0, first + i)) for _ in blocks],
+        out_specs=pl.BlockSpec((left.shape[0], tile), lambda i: (0, i)),
+        out_shape=out,
+        compiler_params=pltpu.CompilerParams(vmem_limit_bytes=LIMIT),
+        cost_estimate=cost(2 * left.size * columns, left, *blocks, out),
+        name="times_rows",
+    )(left, *blocks)
+
+
+def turned_kernel(count, extra, left_ref, *refs):
+    blocks, tail = refs[:count], refs[count : count + 2 * extra]
+    out_ref, total = refs[count + 2 * extra :]
+    step = pl.program_id(0)
+
+    @pl.when(step == 0)
+    def _():
+        total[...] = dot1(tail[0][...], tail[1][...], NT) if extra else jnp.zeros_like(total)
+
+    total[...] += dot1(left_ref[...], stacked(blocks), NT)
+
+    @pl.when(step == pl.num_programs(0) - 1)
+    def _():
+        out_ref[...] = total[...].astype(out_ref.dtype)
+
+
+def times_turned(left, blocks, start, tile, kind, plane=0, planes=1, extra=()):
+    rows = blocks[0].shape[0]
+    first = start // tile
+    length, depth = left.shape[-2:]
+    each = depth // tile
+    if left.ndim == 3:
+        spec = pl.BlockSpec((None, length, tile), lambda i: (plane + i // each, 0, i % each))
+    else:
+        spec = pl.BlockSpec((length, tile), lambda i: (0, i))
+    out = jax.ShapeDtypeStruct((length, rows * len(blocks)), kind)
+    return pl.pallas_call(
+        functools.partial(turned_kernel, len(blocks), len(extra) // 2),
+        grid=(planes * each,),
+        in_specs=[spec]
+        + [pl.BlockSpec((rows, tile), lambda i: (0, first + i)) for _ in blocks]
+        + [whole(a) for a in extra],
+        out_specs=whole(out),
+        out_shape=out,
+        scratch_shapes=[pltpu.VMEM(out.shape, F32)],
+        compiler_params=pltpu.CompilerParams(vmem_limit_bytes=LIMIT),
+        cost_estimate=cost(2 * planes * length * depth * out.shape[1], left, *blocks, out),
+        name="times_turned",
+    )(left, *blocks, *extra)
+
+
+def gated_kernel(count, normed_ref, cot_ref, *refs):
+    gate_refs, up_refs, down_refs = refs[:count], refs[count : 2 * count], refs[2 * count : 3 * count]
+    out_ref = refs[3 * count]
+    gate = dot1(normed_ref[...], stacked(gate_refs), NN)
+    up = dot1(normed_ref[...], stacked(up_refs), NN)
+    grad = dot1(cot_ref[...], stacked(down_refs), NN)
+    sig = jax.nn.sigmoid(gate)
+    out_ref[0] = (grad * up * sig * (1.0 + gate * (1.0 - sig))).astype(BF16)
+    silu = gate * sig
+    out_ref[1] = (grad * silu).astype(BF16)
+    out_ref[2] = (silu * up).astype(BF16)
+
+
+def gated_units(normed, cot, blocks, tile):
+    rows, columns = blocks[0].shape
+    units = columns // 3
+    each = units // tile
+    length = normed.shape[0]
+    out = jax.ShapeDtypeStruct((3, length, units), BF16)
+
+    def spec(which):
+        return pl.BlockSpec((rows, tile), lambda i: (0, which * each + i))
+
+    return pl.pallas_call(
+        functools.partial(gated_kernel, len(blocks)),
+        grid=(each,),
+        in_specs=[whole(normed), whole(cot)] + [spec(w) for w in range(3) for _ in blocks],
+        out_specs=pl.BlockSpec((3, length, tile), lambda i: (0, 0, i)),
+        out_shape=out,
+        compiler_params=pltpu.CompilerParams(vmem_limit_bytes=LIMIT),
+        cost_estimate=cost(6 * normed.size * units, normed, cot, *blocks, out),
+        name="gated_units",
+    )(normed, cot, *blocks, *blocks, *blocks)
+
+
+def weight_kernel(split, *refs):
+    out_ref, right_ref = refs[-1], refs[-2]
+    if len(refs) == 3:
+        out_ref[...] = dot1(refs[0][...], right_ref[...], NN).astype(BF16)
+        return
+    step = pl.program_id(0)
+
+    @pl.when(step < split)
+    def _():
+        out_ref[...] = dot1(refs[0][...], right_ref[...], NN).astype(BF16)
+
+    @pl.when(step >= split)
+    def _():
+        out_ref[...] = dot1(refs[1][...], right_ref[...], NN).astype(BF16)
+
+
+def weight_grads(lefts, half, right, tile, split=0):
+    features, length = lefts[0].shape
+    depth = right.shape[-1]
+    each = depth // tile
+    if right.ndim == 3:
+        columns = right.shape[0] * depth
+        spec = pl.BlockSpec((None, length, tile), lambda i: (i // each, 0, i % each))
+    else:
+        columns = depth
+        spec = pl.BlockSpec((length, tile), lambda i: (0, i))
+    out = jax.ShapeDtypeStruct((features // 2, columns), BF16)
+    return pl.pallas_call(
+        functools.partial(weight_kernel, split // tile),
+        grid=(columns // tile,),
+        in_specs=[pl.BlockSpec((features // 2, length), lambda i: (half, 0)) for _ in lefts] + [spec],
+        out_specs=pl.BlockSpec((features // 2, tile), lambda i: (0, i)),
+        out_shape=out,
+        compiler_params=pltpu.CompilerParams(vmem_limit_bytes=LIMIT),
+        cost_estimate=cost(features * length * columns, lefts[0], right, out),
+        name="weight_grads",
+    )(*lefts, right)
+
+
+def move_kernel(table_ref, in_ref, out_ref):
+    out_ref[...] = in_ref[...]
+
+
+def move_columns(value, table, width, inverse=False):
+    length, columns = value.shape
+    if width % 128:
+        parts = value.reshape(length, -1, width)
+        index = jnp.argsort(table) if inverse else table
+        return jnp.take(parts, index, axis=1).reshape(length, columns)
+    there = pl.BlockSpec((length, width), lambda i, t: (0, t[i]))
+    here = pl.BlockSpec((length, width), lambda i, t: (0, i))
+    return pl.pallas_call(
+        move_kernel,
+        grid_spec=pltpu.PrefetchScalarGridSpec(
+            num_scalar_prefetch=1,
+            grid=(columns // width,),
+            in_specs=[here if inverse else there],
+            out_specs=there if inverse else here,
+        ),
+        out_shape=jax.ShapeDtypeStruct(value.shape, value.dtype),
+        compiler_params=pltpu.CompilerParams(vmem_limit_bytes=LIMIT),
+        cost_estimate=cost(0, value, value),
+        name="move_columns",
+    )(table, value)
+
+
 HEADS_PER_STEP = 2
 PASSES = 3
-
-
-def matmul(left, right, dims, kind=F32):
-    return lax.dot_general(left, right, dims, preferred_element_type=F32).astype(kind)
-
-
-def ring_order(chips):
-    return [2 * i for i in range(chips // 2)] + [2 * i + 1 for i in reversed(range(chips // 2))]
+PORTIONS = 4
+
+
+class Box:
+    def __init__(self, value):
+        self.value = value
+
+
+def sync(*boxes):
+    values = lax.optimization_barrier(tuple(box.value for box in boxes))
+    for box, value in zip(boxes, values):
+        box.value = value
+
+
+class Ring:
+    def __init__(self, devices):
+        self.chips = chips = devices // 2
+        self.order = [2 * i for i in range(chips // 2)]
+        self.order += [2 * i + 1 for i in reversed(range(chips // 2))]
+        place = [self.order.index(c) for c in range(chips)]
+        index = lax.axis_index("dp")
+        chip, core = index // 2, index % 2
+        here = jnp.asarray(place, jnp.int32)[chip]
+        around = jnp.asarray(self.order, jnp.int32)[(here + jnp.arange(chips, dtype=jnp.int32)) % chips]
+        self.table = jnp.concatenate([2 * around + core, 2 * around + 1 - core])
+        self.core_swap = [(i, i ^ 1) for i in range(devices)]
+        self.hops = {}
+        for turn in (1, -1):
+            hops = []
+            for at, source in enumerate(self.order):
+                target = self.order[(at + turn) % chips]
+                hops += [(2 * source, 2 * target), (2 * source + 1, 2 * target + 1)]
+            self.hops[turn] = hops
+
+    def send(self, value, turn):
+        return Box(lax.ppermute(value, "dp", self.hops[turn]))
+
+    def swap(self, value):
+        return Box(lax.ppermute(value, "dp", self.core_swap))
+
+    def steps(self, portion):
+        total = self.chips // 2
+        return range(total * portion // PORTIONS + 1, total * (portion + 1) // PORTIONS + 1)
+
+
+class Gather:
+    def __init__(self, ring, own):
+        self.ring = ring
+        box = Box(own)
+        self.blocks = {(0, 0): [box]}
+        self.front = {1: box, -1: box}
+        self.fresh = [((0, 0), box)]
+        self.pending = [box]
+
+    def swap(self):
+        for (at, _), box in self.fresh:
+            other = self.ring.swap(box.value)
+            self.blocks.setdefault((at, 1), []).append(other)
+            self.pending.append(other)
+        self.fresh = []
+
+    def advance(self, portion):
+        chips = self.ring.chips
+        for step in self.ring.steps(portion):
+            for turn in (1, -1):
+                value = self.front[turn].value
+                if 2 * step == chips:
+                    half = value.shape[1] // 2
+                    value = value[:, :half] if turn == 1 else value[:, half:]
+                box = self.ring.send(value, turn)
+                key = (-turn * step % chips, 0)
+                self.blocks.setdefault(key, []).append(box)
+                self.front[turn] = box
+                self.fresh.append((key, box))
+                self.pending.append(box)
+
+    def boxes(self):
+        waiting, self.pending = self.pending, []
+        return waiting
+
+    def ordered(self):
+        out = []
+        for core in range(2):
+            for at in range(self.ring.chips):
+                parts = [box.value for box in self.blocks[at, core]]
+                out.append(parts[0] if len(parts) == 1 else jnp.concatenate(parts, axis=1))
+        most = 16
+        if len(out) > most:
+            many = len(out) // most
+            out = [jnp.concatenate(out[i * many : (i + 1) * many], axis=0) for i in range(most)]
+        return out
+
+
+class Scatter:
+    def __init__(self, ring, own, other):
+        self.ring = ring
+        self.own = Box(own)
+        self.other = ring.swap(other)
+        self.got = {1: None, -1: None}
+
+    def local(self, at):
+        rows = self.own.value.shape[0] // self.ring.chips
+        span = slice(at * rows, (at + 1) * rows)
+        return self.own.value[span].astype(F32) + self.other.value[span].astype(F32)
+
+    def advance(self, portion):
+        chips = self.ring.chips
+        for step in self.ring.steps(portion):
+            away = chips // 2 - step + 1
+            for turn in (1, -1):
+                total = self.local(turn * away % chips)
+                half = total.shape[1] // 2
+                if step == 1:
+                    total = total[:, :half] if turn == 1 else total[:, half:]
+                else:
+                    got = self.got[turn].value.astype(F32)
+                    if step == 2:
+                        near, far = total[:, :half], total[:, half:]
+                        parts = [near + got, far] if turn == 1 else [near, far + got]
+                        total = jnp.concatenate(parts, axis=1)
+                    else:
+                        total = total + got
+                self.got[turn] = self.ring.send(total.astype(BF16), turn)
+
+    def boxes(self):
+        return [box for box in self.got.values() if box is not None] + [self.own, self.other]
+
+    def result(self):
+        return self.local(0) + self.got[1].value.astype(F32) + self.got[-1].value.astype(F32)
 
 
 def swap_tensor(value):
     return lax.ppermute(value, "tensor", [(0, 1), (1, 0)])
-
-
-def pair_sum(part):
-    low = part.astype(BF16)
-    return low.astype(F32) + swap_tensor(low).astype(F32)
-
-
-def pair_split(rows, width, core):
-    blocks = rows.reshape(rows.shape[0], -1, 2, width)
-    own = lax.dynamic_index_in_dim(blocks, core, 2, keepdims=False)
-    other = lax.dynamic_index_in_dim(blocks, 1 - core, 2, keepdims=False)
-    flat = (rows.shape[0], -1)
-    return own.reshape(flat), other.reshape(flat)
-
-
-def ring_scatter(own, other, chip, forward):
-    chips = lax.axis_size("dp") // 2
-    rows = own.shape[0] // chips
-    order = ring_order(chips)
-    place = [order.index(c) for c in range(chips)]
-    table = jnp.asarray(order, jnp.int32)
-    here = jnp.asarray(place, jnp.int32)[chip]
-    turn = 1 if forward else -1
-    hops = []
-    for position, source in enumerate(order):
-        target = order[(position + turn) % chips]
-        hops += [(2 * source, 2 * target), (2 * source + 1, 2 * target + 1)]
-
-    def local(step):
-        at = table[(here - turn * (step + 1)) % chips] * rows
-        a = lax.dynamic_slice_in_dim(own, at, rows, 0)
-        b = lax.dynamic_slice_in_dim(other, at, rows, 0)
-        return a.astype(F32) + b.astype(F32)
-
-    total = local(0)
-    for step in range(1, chips):
-        moved = lax.ppermute(total.astype(BF16), "dp", hops)
-        total = local(step) + moved.astype(F32)
-    return total
-
-
-def scatter_grads(own, other, chip, core_swap):
-    other = lax.ppermute(other, "dp", core_swap)
-    half = own.shape[1] // 2
-    return jnp.concatenate(
-        [
-            ring_scatter(own[:, :half], other[:, :half], chip, True),
-            ring_scatter(own[:, half:], other[:, half:], chip, False),
-        ],
-        axis=1,
-    )
 
 
 def norm_back(values, scale, gain, grad):
@@ -433,6 +693,16 @@
     inner = jnp.mean(values * scaled, axis=-1, keepdims=True)
     gain_grad = jnp.sum(values * scale * grad, axis=0)
     return scale * scaled - values * (scale * scale * scale) * inner, gain_grad
+
+
+def matmul(left, right, dims):
+    return lax.dot_general(left, right, dims, preferred_element_type=F32)
+
+
+def unit_chunks(units):
+    tile = 256
+    cut = (units // tile + 1) // 2 * tile
+    return [(0, cut), (cut, units)]
 
 
 def body(
@@ -450,116 +720,233 @@
     seg_ids = segments[0]
     length = tokens.shape[0]
     devices = lax.axis_size("dp")
-    index = lax.axis_index("dp")
-    chip, core = index // 2, index % 2
-    core_swap = [(i, i ^ 1) for i in range(devices)]
+    ring = Ring(devices)
     rows, _, local_width = attn_weight.shape
     head_count = beta_weight.shape[1]
     piece = conv_weight.shape[3]
     units = mlp_weight.shape[2]
     groups = head_count // HEADS_PER_STEP
     wide = local_width // groups
-    model_width = rows * devices
+    qkv = 3 * local_width
     taps_size = conv_weight.size
-
-    small = jnp.concatenate(
-        [norm_gain, mlp_gain, beta_weight.reshape(-1), conv_weight.reshape(-1), out_gain]
-    ).astype(BF16)
-    small = lax.all_gather(small, "dp", axis=0)
+    chunks = unit_chunks(units)
+
     attn_low = attn_weight.astype(BF16)
     qkv_local = attn_low[:, :3].reshape(rows, 3, groups, wide).transpose(0, 2, 1, 3)
-    attn_local = jnp.concatenate([qkv_local.reshape(rows, 3 * local_width), attn_low[:, 3]], axis=1)
-    attn_mat = lax.all_gather(attn_local, "dp", axis=0, tiled=True)
-    mlp_local = mlp_weight.astype(BF16).reshape(rows, 3 * units)
-    mlp_mat = lax.all_gather(mlp_local, "dp", axis=0, tiled=True)
-    qkv_mat, out_mat = attn_mat[:, : 3 * local_width], attn_mat[:, 3 * local_width :]
-    gu_mat, down_mat = mlp_mat[:, : 2 * units], mlp_mat[:, 2 * units :]
+    attn = Gather(ring, jnp.concatenate([qkv_local.reshape(rows, qkv), attn_low[:, 3]], axis=1))
+    small = Box(
+        jnp.concatenate(
+            [norm_gain, mlp_gain, beta_weight.reshape(-1), conv_weight.reshape(-1), out_gain]
+        ).astype(BF16)
+    )
+
+    attn.advance(0)
+    small.value = lax.all_gather(small.value, "dp", axis=0)
+    inputs_low = Box(move_columns(tokens, ring.table, rows))
+    sync(*attn.boxes(), small, inputs_low)
+    attn.swap()
+    attn.advance(1)
+    cot = Box(move_columns(cotangent, ring.table, rows))
+    cot_turned = Box(cot.value.T)
+    sync(*attn.boxes(), cot, cot_turned)
+    attn.swap()
+    attn.advance(2)
+    mlp_low = mlp_weight.astype(BF16)
+    mlp = []
+    for low, high in chunks:
+        mlp.append(Gather(ring, mlp_low[:, :, low:high].reshape(rows, 3 * (high - low))))
+    inputs_f = inputs_low.value.astype(F32)
     at = [0, rows, 2 * rows, 2 * rows + rows * head_count]
-    gain_in = small[:, at[0] : at[1]].reshape(-1).astype(F32)
-    gain_mid = small[:, at[1] : at[2]].reshape(-1).astype(F32)
-    beta_mat = small[:, at[2] : at[3]].reshape(model_width, head_count)
+    gathered = small.value[ring.table]
+    gain_in = gathered[:, at[0] : at[1]].reshape(-1).astype(F32)
+    gain_mid = gathered[:, at[1] : at[2]].reshape(-1).astype(F32)
+    beta_mat = gathered[:, at[2] : at[3]].reshape(devices * rows, head_count)
     beta_pad = jnp.pad(beta_mat, ((0, 0), (0, 128 - head_count)))
-    taps = small[:, at[3] : at[3] + taps_size].reshape(devices, 3, 4, head_count, piece)
+    taps = small.value[:, at[3] : at[3] + taps_size].reshape(devices, 3, 4, head_count, piece)
     taps = taps.transpose(1, 2, 3, 0, 4).reshape(3, 4, local_width).astype(F32)
-    gain_heads = small[:, at[3] + taps_size :].reshape(1, -1).astype(F32)
-
-    inputs_f = tokens.astype(F32)
+    gain_heads = small.value[:, at[3] + taps_size :].reshape(1, -1).astype(F32)
     scale_in = lax.rsqrt(jnp.mean(inputs_f * inputs_f, axis=-1, keepdims=True) + 1e-05)
-    normed = (inputs_f * scale_in * gain_in).astype(BF16)
-    projected = matmul(normed, qkv_mat, NN)
-    logits = matmul(normed, beta_pad, NN)
-    mixed, *saved = mixer_forward(
-        projected, logits, taps, gain_heads, seg_ids, HEADS_PER_STEP, PASSES
-    )
-    hidden = inputs_f + pair_sum(matmul(mixed, out_mat, NT))
-
+    normed = Box((inputs_f * scale_in * gain_in).astype(BF16))
+    normed_turned = Box(normed.value.T)
+    logits = Box(matmul(normed.value, beta_pad, NN))
+    sync(*attn.boxes(), normed, normed_turned, logits, mlp[0].front[1], mlp[1].front[1])
+    attn.swap()
+    attn.advance(3)
+    sync(*attn.boxes(), *mlp[0].boxes())
+
+    attn.swap()
+    mlp[0].advance(0)
+    attn_blocks = attn.ordered()
+    projected = Box(times_rows(normed.value, attn_blocks, 0, qkv, 512, F32))
+    span = groups // 2
+    mixers = []
+    for call in range(2):
+        made = mixer_forward(
+            projected.value, logits.value, taps, gain_heads, seg_ids, HEADS_PER_STEP, PASSES, call * span, span
+        )
+        made = [Box(m) for m in made]
+        mixers.append(made)
+        if call == 0:
+            sync(*mlp[0].boxes(), projected, *made)
+            mlp[0].swap()
+            mlp[0].advance(1)
+    mixed = jnp.concatenate([mixers[0][0].value, mixers[1][0].value], axis=1)
+    part = Box(times_turned(mixed, attn_blocks, qkv, 512, BF16))
+    sync(*mlp[0].boxes(), part)
+    attended = part.value.astype(F32) + swap_tensor(part.value).astype(F32)
+    mlp[0].swap()
+    mlp[0].advance(2)
+    sync(*mlp[0].boxes())
+    mlp[0].swap()
+    mlp[0].advance(3)
+    mlp[1].advance(0)
+    sync(*mlp[0].boxes(), *mlp[1].boxes())
+    mlp[0].swap()
+    mlp[1].swap()
+    mlp[1].advance(1)
+
+    hidden = inputs_f + attended
     scale_mid = lax.rsqrt(jnp.mean(hidden * hidden, axis=-1, keepdims=True) + 1e-05)
     normed_mlp = (hidden * scale_mid * gain_mid).astype(BF16)
-    gate = matmul(normed_mlp, gu_mat[:, :units], NN)
-    up = matmul(normed_mlp, gu_mat[:, units:], NN)
-    gate_sig = jax.nn.sigmoid(gate)
-    activated = (gate * gate_sig * up).astype(BF16)
-    grad_act = matmul(cotangent, down_mat, NN)
-    grad_gate = (grad_act * up * gate_sig * (1.0 + gate * (1.0 - gate_sig))).astype(BF16)
-    grad_up = (grad_act * gate * gate_sig).astype(BF16)
-    grad_gu = jnp.concatenate([grad_gate, grad_up], axis=1)
-    down = pair_sum(matmul(activated, down_mat, NT))
-    result = (hidden + down).astype(BF16)
-
-    mlp_own, mlp_other = pair_split(normed_mlp, rows, core)
-    cot_own, cot_other = pair_split(cotangent, rows, core)
-    grad_gu_mat = scatter_grads(
-        matmul(mlp_own, grad_gu, TN, BF16), matmul(mlp_other, grad_gu, TN, BF16), chip, core_swap
+    blocks = [mlp[0].ordered()]
+    acts = [Box(gated_units(normed_mlp, cot.value, blocks[0], 256))]
+    mlp_turned = Box(normed_mlp.T)
+    sync(*mlp[1].boxes(), acts[0], mlp_turned)
+    mlp[1].swap()
+    mlp[1].advance(2)
+
+    def mlp_grads(which):
+        split = 2 * acts[which].value.shape[2]
+        lefts = (mlp_turned.value, cot_turned.value)
+        return [Box(weight_grads(lefts, half, acts[which].value, 256, split)) for half in (0, 1)]
+
+    own, other = mlp_grads(0)
+    sync(*mlp[1].boxes(), own, other)
+    mlp[1].swap()
+    mlp[1].advance(3)
+    sums = [Scatter(ring, own.value, other.value)]
+    sync(*mlp[1].boxes(), *sums[0].boxes())
+    mlp[1].swap()
+    sums[0].advance(0)
+    blocks.append(mlp[1].ordered())
+    acts.append(Box(gated_units(normed_mlp, cot.value, blocks[1], 256)))
+    sync(*sums[0].boxes(), *acts)
+    sums[0].advance(1)
+    parts = [
+        times_turned(acts[w].value, blocks[w], 0, 256, F32, plane=0, planes=2) for w in range(2)
+    ]
+    part = Box((parts[0] + parts[1]).astype(BF16))
+    sync(*sums[0].boxes(), part, acts[1])
+    grad_normed_mlp = part.value.astype(F32) + swap_tensor(part.value).astype(F32)
+    sums[0].advance(2)
+    own, other = mlp_grads(1)
+    sync(*sums[0].boxes(), own, other, *acts)
+    sums[0].advance(3)
+    sums.append(Scatter(ring, own.value, other.value))
+    parts = [
+        times_turned(acts[w].value, blocks[w], 2 * acts[w].value.shape[2], 256, F32, plane=2)
+        for w in range(2)
+    ]
+    down = Box((parts[0] + parts[1]).astype(BF16))
+    sync(*sums[0].boxes(), *sums[1].boxes(), down)
+    sums[1].advance(0)
+
+    grad_norm, grad_gain_mid = norm_back(hidden, scale_mid, gain_mid, grad_normed_mlp)
+    grad_hidden = cot.value.astype(F32) + grad_norm
+    grad_hidden_low = grad_hidden.astype(BF16)
+    grad_mixed = Box(times_rows(grad_hidden_low, attn_blocks, qkv, local_width, 512, F32))
+    hidden_turned = Box(grad_hidden_low.T)
+    sync(*sums[1].boxes(), grad_mixed, hidden_turned, down)
+    sums[1].advance(1)
+    down_sum = down.value.astype(F32) + swap_tensor(down.value).astype(F32)
+    result = (hidden + down_sum).astype(BF16)
+
+    def mixer_grads(call):
+        made = mixer_backward(
+            projected.value,
+            logits.value,
+            taps,
+            gain_heads,
+            seg_ids,
+            [m.value for m in mixers[call][1:]],
+            grad_mixed.value,
+            HEADS_PER_STEP,
+            PASSES,
+            call * span,
+            span,
+            call * span,
+        )
+        return [Box(m) for m in made]
+
+    back = [mixer_grads(0)]
+    sync(*sums[1].boxes(), back[0][0], grad_mixed)
+    sums[1].advance(2)
+
+    def attn_grads(half):
+        left = weight_grads((normed_turned.value,), half, back[0][0].value, 512)
+        right = weight_grads((hidden_turned.value,), half, mixed, 512)
+        return Box(jnp.concatenate([left, right], axis=1))
+
+    other, own = attn_grads(1), attn_grads(0)
+    first = Scatter(ring, own.value, other.value)
+    sync(*sums[1].boxes(), *first.boxes(), grad_mixed)
+    sums[1].advance(3)
+    first.advance(0)
+    back.append(mixer_grads(1))
+    sync(*sums[1].boxes(), *first.boxes(), back[1][0])
+    first.advance(1)
+    other, own = [Box(weight_grads((normed_turned.value,), h, back[1][0].value, 512)) for h in (1, 0)]
+    second = Scatter(ring, own.value, other.value)
+    grad_logits_low = (back[0][1].value + back[1][1].value).astype(BF16)
+    grad_proj = jnp.concatenate([back[0][0].value, back[1][0].value], axis=1)
+    part = Box(
+        times_turned(grad_proj, attn_blocks, 0, 512, BF16, extra=(grad_logits_low, beta_pad))
     )
-    grad_down_mat = scatter_grads(
-        matmul(cot_own, activated, TN, BF16), matmul(cot_other, activated, TN, BF16), chip, core_swap
-    )
-    mlp_grad = jnp.concatenate([grad_gu_mat, grad_down_mat], axis=1).reshape(rows, 3, units)
-    grad_normed_mlp = pair_sum(matmul(grad_gu, gu_mat, NT))
-    grad_norm, grad_gain_mid = norm_back(hidden, scale_mid, gain_mid, grad_normed_mlp)
-    grad_hidden = cotangent.astype(F32) + grad_norm
-    grad_hidden_low = grad_hidden.astype(BF16)
-
-    grad_mixed = matmul(grad_hidden_low, out_mat, NN)
-    grad_proj, grad_logits, grad_taps, grad_gain_heads = mixer_backward(
-        projected, logits, taps, gain_heads, seg_ids, saved, grad_mixed, HEADS_PER_STEP, PASSES
-    )
-    grad_logits_low = grad_logits.astype(BF16)
-    hid_own, hid_other = pair_split(grad_hidden_low, rows, core)
-    in_own, in_other = pair_split(normed, rows, core)
-    grad_out_mat = scatter_grads(
-        matmul(hid_own, mixed, TN, BF16), matmul(hid_other, mixed, TN, BF16), chip, core_swap
-    )
-    grad_qkv_mat = scatter_grads(
-        matmul(in_own, grad_proj, TN, BF16), matmul(in_other, grad_proj, TN, BF16), chip, core_swap
-    )
-    grad_qkv_mat = grad_qkv_mat.reshape(rows, groups, 3, wide).transpose(0, 2, 1, 3)
-    attn_grad = jnp.concatenate(
-        [grad_qkv_mat.reshape(rows, 3, local_width), grad_out_mat[:, None]], axis=1
-    )
-    grad_beta = matmul(normed, grad_logits_low, TN)[:, :head_count]
-    grad_normed = pair_sum(
-        matmul(grad_proj, qkv_mat, NT) + matmul(grad_logits_low, beta_pad, NT)
-    )
+    sync(*first.boxes(), *second.boxes(), part)
+    first.advance(2)
+    second.advance(0)
+    grad_normed = part.value.astype(F32) + swap_tensor(part.value).astype(F32)
+    grad_beta = matmul(normed.value, grad_logits_low, TN)[:, :head_count]
+    sync(*first.boxes(), *second.boxes())
+    first.advance(3)
+    second.advance(1)
+    sync(*first.boxes(), *second.boxes())
+    second.advance(2)
+    sync(*second.boxes())
+    second.advance(3)
+
     grad_first, grad_gain_in = norm_back(inputs_f, scale_in, gain_in, grad_normed)
     grad_inputs = grad_hidden + grad_first
 
-    grad_gain_heads = grad_gain_heads[0] + swap_tensor(grad_gain_heads[0])
+    grad_gain_heads = back[0][3].value[0] + back[1][3].value[0]
+    grad_gain_heads = grad_gain_heads + swap_tensor(grad_gain_heads)
+    grad_taps = jnp.concatenate([back[0][2].value, back[1][2].value], axis=2)
     grad_taps = grad_taps.reshape(3, 4, head_count, devices, piece).transpose(3, 0, 1, 2, 4)
-    packed = jnp.concatenate(
+    owner = jnp.argsort(ring.table)
+    by_feature = jnp.concatenate(
         [
             grad_gain_in.reshape(devices, -1),
             grad_gain_mid.reshape(devices, -1),
             grad_beta.reshape(devices, -1),
-            grad_taps.reshape(devices, -1),
-            grad_gain_heads.reshape(devices, -1),
         ],
         axis=1,
+    )[owner]
+    packed = jnp.concatenate(
+        [by_feature, grad_taps.reshape(devices, -1), grad_gain_heads.reshape(devices, -1)], axis=1
     )
     packed = jnp.sum(lax.all_to_all(packed, "dp", 0, 0, tiled=True), axis=0)
+
+    mlp_grad = jnp.concatenate([s.result().reshape(rows, 3, -1) for s in sums], axis=2)
+    first_sum, second_sum = first.result(), second.result()
+    each = qkv // 2
+    qkv_grad = jnp.concatenate([first_sum[:, :each], second_sum], axis=1)
+    qkv_grad = qkv_grad.reshape(rows, groups, 3, wide).transpose(0, 2, 1, 3)
+    attn_grad = jnp.concatenate(
+        [qkv_grad.reshape(rows, 3, local_width), first_sum[:, each:][:, None]], axis=1
+    )
     return (
-        result,
-        grad_inputs,
+        move_columns(result, ring.table, rows, inverse=True),
+        move_columns(grad_inputs, ring.table, rows, inverse=True),
         packed[at[0] : at[1]],
         attn_grad,
         packed[at[2] : at[3]].reshape(rows, head_count),

time: 974 us -> 863 us (0.89)
  Pallas kernels: 82.2 us -> 274 us
  waiting for transfers between devices: 374 us -> 192 us
  matrix products: 156 us -> 4.8 us
  other arithmetic: 87 us -> 123 us
  between operations: 36.1 us -> 2.91 us
  blocking collectives: 24.4 us -> 38.2 us
    pallas_call x2 -> x28, Pallas kernels: 82.2 us -> 274 us  [the longest x6 64.9 us: times_turned(): pl.pallas_call(functools.partial(turned_kernel, len(blocks), len(extra) /...]
    all_gather x2 -> x0, waiting for transfers between devices: 152 us -> none  [the longest x1 94.9 us: body(): attn_mat = lax.all_gather(attn_local, 'dp', axis=0, tiled=True)]
    dot_general x19 -> x1, matrix products: 155 us -> 3.09 us  [matmul(): return lax.dot_general(left, right, dims, preferred_element_type=F32)]
    ppermute x60 -> x87, waiting for transfers between devices: 175 us -> 114 us  [the longest x56 114 us: send(): return Box(lax.ppermute(value, 'dp', self.hops[turn]))]
    ppermute x5, waiting for transfers between devices: 46.4 us -> 77.6 us  [swap_tensor(): return lax.ppermute(value, 'tensor', [(0, 1), (1, 0)])]
    slice x9 -> x23, local copies, waits for them, and re-layouts: 35.1 us -> 14.6 us  [the longest x6 7.05 us: advance(): value = value[:, :half] if turn == 1 else value[:, half:]]
    dynamic_slice x5 -> x1, local copies, waits for them, and re-layouts: 20.3 us -> 0.59 us  [__init__(): here = jnp.asarray(place, jnp.int32)[chip]]
    optimization_barrier x0 -> x6, local copies, waits for them, and re-layouts: none -> 16.9 us  [sync(): values = lax.optimization_barrier(tuple((box.value for box in boxes)))]
  transfers between devices with their start and end apart: 68 -> 93, of which waited for: 39 -> 25; matrix products, arithmetic and copies ran while one was open for 31% -> 22% of each run, Pallas kernels for 8% -> 30%
where the time goes in v2:
time: 863 us; the launch traced here: 852 us
  Pallas kernels  274 us (32%)
  waiting for transfers between devices  192 us (22%)
  local copies, waits for them, and re-layouts  137 us (16%)
  other arithmetic  123 us (14%)
  starting transfers between devices  79.6 us (9%)
  blocking collectives  38.2 us (4%)
    ppermute x56, waiting for transfers between devices, send(): return Box(lax.ppermute(value, 'dp', self.hops[turn]))  114 us
    ppermute x5, waiting for transfers between devices, swap_tensor(): return lax.ppermute(value, 'tensor', [(0, 1), (1, 0)])  77.6 us
    unnamed x312, local copies, waits for them, and re-layouts  65.3 us
    pallas_call x6, Pallas kernels, times_turned(): pl.pallas_call(functools.partial(turned_kernel, len(blocks), len(extra) /...  64.9 us
    ppermute x56, starting transfers between devices, send(): return Box(lax.ppermute(value, 'dp', self.hops[turn]))  59.7 us
    pallas_call x10, Pallas kernels, weight_grads(): pl.pallas_call(functools.partial(weight_kernel, split // tile), grid=(col...  59.4 us
    pallas_call x2, Pallas kernels, mixer_backward(): pl.pallas_call(functools.partial(backward_kernel, heads, passes, first),...  53.2 us
    all_gather x1, blocking collectives, body(): small.value = lax.all_gather(small.value, 'dp', axis=0)  38.2 us
  transfers between devices with their start and end apart: 93, of which 25 were waited for; matrix products, arithmetic and copies ran while one was open for 22% of the time, Pallas kernels for 30%

profile of v2, /device:TPU:0, one launch (start us, length us, event | category | flops | bytes accessed | tf_op | source)
XLA Modules:
  0.0 851.8 jit_solution(18193138820932386413)
XLA Ops:
  8.9 38.2 %all-gather = bf16[16,1,2056]{2,1,0:T(2,128)(2,1)S(1)} all-gather(bf16[1,1,2056]{2,1,0:T(2,128)(2,1)S(1)} %bitcast.90), channel_id=1, replica_groups=mesh['dp'=16,'tensor'=2] {'dp'}, dimensions={0}, use_global_device_ids=true | all-gather | bytes 69904 | tf_op jit(solution)/shard_map/all_gather | solution.py:744
  64.5 3.9 copy.145
  75.5 3.8 collective-permute-done.5.refs_6_
  90.1 13.8 %collective-permute-done.10.refs_3_ = bf16[128,4096]{1,0:T(8,128)(2,1)S(1)} collective-permute-done((bf16[128,4096]{1,0:T(8,128)(2,1)}, bf16[128,4096]{1,0:T(8,128)(2,1)S(1)}, u32[]{:S(2)}, u32[]{:S(2)}) %collective-permute-start.10) | collective-permute-done | bytes 1048608 | tf_op jit(solution)/shard_map/ppermute | solution.py:591
  112.4 12.0 %collective-permute-done.13 = bf16[128,2048]{1,0:T(8,128)(2,1)} collective-permute-done((bf16[128,2048]{1,0:T(8,128)(2,1)}, bf16[128,2048]{1,0:T(8,128)(2,1)}, u32[]{:S(2)}, u32[]{:S(2)}) %collective-permute-start.13) | collective-permute-done | bytes 524320 | tf_op jit(solution)/shard_map/ppermute | solution.py:591
  140.6 12.1 %times_rows.2.proj_ref = f32[512,3072]{1,0:T(8,128)} custom-call(bf16[512,2048]{1,0:T(8,128)(2,1)} %fusion.2.left_ref, bf16[128,4096]{1,0:T(8,128)(2,1)S(1)} %copy-done.53, bf16[128,4096]{1,0:T(8,128)(2,1)} %collective-permute-done.1.refs_1_, bf16[128,4096]{1,0:T(8,128)(2,1)} %collective-permute-done.6.refs_2_, bf16[128,4096]{1,0:T(8,128)(2,1)S(1)} %copy-done.59, ...), custom_call_target="tpu_custom_call" | custom-call | flops 6442450944 | bytes 25165824 | tf_op jit(solution)/shard_map/times_rows/pallas_call | solution.py:399
  154.6 15.2 %mixer_forward.2 = (bf16[512,512]{1,0:T(8,128)(2,1)S(1)}, f32[512,512]{1,0:T(8,128)S(1)}, f32[512,512]{1,0:T(8,128)S(1)}, f32[512,512]{1,0:T(8,128)S(1)}, f32[512,512]{1,0:T(8,128)S(1)}) custom-call(f32[512,3072]{1,0:T(8,128)} %times_rows.2.proj_ref, f32[512,128]{1,0:T(8,128)S(1)} %copy-done.79, f32[3,4,1024]{2,1,0:T(4,128)S(1)} %copy-done.83, ...), custom_call_target="tpu_custom_call" | custom-call | flops 7864320000 | bytes 7864320 | tf_op jit(solution)/shard_map/mixer_forward/pallas_call | solution.py:331
  177.4 15.2 %mixer_forward.3 = (bf16[512,512]{1,0:T(8,128)(2,1)S(1)}, f32[512,512]{1,0:T(8,128)S(1)}, f32[512,512]{1,0:T(8,128)S(1)}, f32[512,512]{1,0:T(8,128)S(1)}, f32[512,512]{1,0:T(8,128)S(1)}) custom-call(f32[512,3072]{1,0:T(8,128)} %times_rows.2.proj_ref, f32[512,128]{1,0:T(8,128)S(1)} %copy-done.80, f32[3,4,1024]{2,1,0:T(4,128)S(1)} %copy-done.83, ...), custom_call_target="tpu_custom_call" | custom-call | flops 7864320000 | bytes 7864320 | tf_op jit(solution)/shard_map/mixer_forward/pallas_call | solution.py:331
  199.9 6.0 times_turned.6
  216.3 22.8 %collective-permute-done.27.refs_5_.refs_21_.refs_37_ = bf16[128,4608]{1,0:T(8,128)(2,1)} collective-permute-done((bf16[128,4608]{1,0:T(8,128)(2,1)}, bf16[128,4608]{1,0:T(8,128)(2,1)}, u32[]{:S(2)}, u32[]{:S(2)}) %collective-permute-start.27) | collective-permute-done | bytes 1179680 | tf_op jit(solution)/shard_map/ppermute | solution.py:591
  242.3 13.8 %collective-permute-done.24 = bf16[512,2048]{1,0:T(8,128)(2,1)} collective-permute-done((bf16[512,2048]{1,0:T(8,128)(2,1)}, bf16[512,2048]{1,0:T(8,128)(2,1)}, u32[]{:S(2)}, u32[]{:S(2)}) %collective-permute-start.24) | collective-permute-done | bytes 2097184 | tf_op jit(solution)/shard_map/ppermute | solution.py:688
  264.5 7.4 collective-permute-done.31
  286.8 16.4 %gated_units.2.refs_2_.left_ref = bf16[3,512,1536]{2,1,0:T(8,128)(2,1)} custom-call(bf16[512,2048]{1,0:T(8,128)(2,1)} %multiply_convert_fusion.normed_ref, bf16[512,2048]{1,0:T(8,128)(2,1)} %copy-done.7, bf16[128,4608]{1,0:T(8,128)(2,1)S(1)} %copy.147.refs_0_.refs_16_.refs_32_, bf16[128,4608]{1,0:T(8,128)(2,1)S(1)} %copy-done.21, ...), custom_call_target="tpu_custom_call" | custom-call | flops 9663676416 | bytes 27787264 | tf_op jit(solution)/shard_map/gated_units/pallas_call | solution.py:476
  308.3 3.9 copy.160.refs_0_
  316.1 12.4 %weight_grads.11 = bf16[1024,4608]{1,0:T(8,128)(2,1)} custom-call(bf16[2048,512]{1,0:T(8,128)(2,1)S(1)} %copy-done.5, bf16[2048,512]{1,0:T(8,128)(2,1)S(1)} %bitcast.68, bf16[3,512,1536]{2,1,0:T(8,128)(2,1)S(1)} %copy-done), custom_call_target="tpu_custom_call" | custom-call | flops 4831838208 | bytes 16252928 | tf_op jit(solution)/shard_map/weight_grads/pallas_call | solution.py:515
  328.5 12.2 %weight_grads.10 = bf16[1024,4608]{1,0:T(8,128)(2,1)} custom-call(bf16[2048,512]{1,0:T(8,128)(2,1)S(1)} %copy-done.5, bf16[2048,512]{1,0:T(8,128)(2,1)S(1)} %bitcast.69, bf16[3,512,1536]{2,1,0:T(8,128)(2,1)S(1)} %copy-done), custom_call_target="tpu_custom_call" | custom-call | flops 4831838208 | bytes 16252928 | tf_op jit(solution)/shard_map/weight_grads/pallas_call | solution.py:515
  345.6 11.5 %collective-permute-done.48 = bf16[128,1920]{1,0:T(8,128)(2,1)S(1)} collective-permute-done((bf16[128,1920]{1,0:T(8,128)(2,1)S(1)}, bf16[128,1920]{1,0:T(8,128)(2,1)S(1)}, u32[]{:S(2)}, u32[]{:S(2)}) %collective-permute-start.48) | collective-permute-done | bytes 491552 | tf_op jit(solution)/shard_map/ppermute | solution.py:591
  364.0 14.6 %gated_units.3.left_ref.refs_2_ = bf16[3,512,1280]{2,1,0:T(8,128)(2,1)} custom-call(bf16[512,2048]{1,0:T(8,128)(2,1)} %multiply_convert_fusion.normed_ref, bf16[512,2048]{1,0:T(8,128)(2,1)} %copy-done.7, bf16[128,3840]{1,0:T(8,128)(2,1)} %copy.156.refs_0_.refs_16_.refs_32_, bf16[128,3840]{1,0:T(8,128)(2,1)S(1)} %copy-done.37, ...), custom_call_target="tpu_custom_call" | custom-call | flops 8053063680 | bytes 23855104 | tf_op jit(solution)/shard_map/gated_units/pallas_call | solution.py:476
  381.2 14.8 %times_turned.7 = f32[512,2048]{1,0:T(8,128)} custom-call(bf16[3,512,1536]{2,1,0:T(8,128)(2,1)} %gated_units.2.refs_2_.left_ref, bf16[128,4608]{1,0:T(8,128)(2,1)S(1)} %copy.147.refs_0_.refs_16_.refs_32_, bf16[128,4608]{1,0:T(8,128)(2,1)S(1)} %copy-done.22, bf16[128,4608]{1,0:T(8,128)(2,1)} %collective-permute-done.23.refs_2_.refs_18_.refs_34_, ...), custom_call_target="tpu_custom_call" | custom-call | flops 6442450944 | bytes 27787264 | tf_op jit(solution)/shard_map/times_turned/pallas_call | solution.py:438
  404.2 13.1 %times_turned.8 = f32[512,2048]{1,0:T(8,128)} custom-call(bf16[3,512,1280]{2,1,0:T(8,128)(2,1)} %gated_units.3.left_ref.refs_2_, bf16[128,3840]{1,0:T(8,128)(2,1)} %copy.156.refs_0_.refs_16_.refs_32_, bf16[128,3840]{1,0:T(8,128)(2,1)S(1)} %copy-done.37, bf16[128,3840]{1,0:T(8,128)(2,1)} %collective-permute-done.39.refs_2_.refs_18_.refs_34_, ...), custom_call_target="tpu_custom_call" | custom-call | flops 5368709120 | bytes 23855104 | tf_op jit(solution)/shard_map/times_turned/pallas_call | solution.py:438
  417.3 4.1 add_convert_fusion.2
  421.5 6.6 collective-permute-done.56
  436.8 10.6 %weight_grads.13 = bf16[1024,3840]{1,0:T(8,128)(2,1)} custom-call(bf16[2048,512]{1,0:T(8,128)(2,1)S(1)} %copy-done.6, bf16[2048,512]{1,0:T(8,128)(2,1)S(1)} %bitcast.70, bf16[3,512,1280]{2,1,0:T(8,128)(2,1)S(1)} %copy-done.3), custom_call_target="tpu_custom_call" | custom-call | flops 4026531840 | bytes 13893632 | tf_op jit(solution)/shard_map/weight_grads/pallas_call | solution.py:515
  447.4 10.6 %weight_grads.12 = bf16[1024,3840]{1,0:T(8,128)(2,1)} custom-call(bf16[2048,512]{1,0:T(8,128)(2,1)S(1)} %copy-done.6, bf16[2048,512]{1,0:T(8,128)(2,1)S(1)} %bitcast.71, bf16[3,512,1280]{2,1,0:T(8,128)(2,1)S(1)} %copy-done.3), custom_call_target="tpu_custom_call" | custom-call | flops 4026531840 | bytes 13893632 | tf_op jit(solution)/shard_map/weight_grads/pallas_call | solution.py:515
  468.0 5.7 add_convert_fusion.3
  475.8 8.4 times_turned.10
  484.3 9.3 %times_turned.9 = f32[512,2048]{1,0:T(8,128)} custom-call(bf16[3,512,1536]{2,1,0:T(8,128)(2,1)} %gated_units.2.refs_2_.left_ref, bf16[128,4608]{1,0:T(8,128)(2,1)S(1)} %copy.147.refs_0_.refs_16_.refs_32_, bf16[128,4608]{1,0:T(8,128)(2,1)S(1)} %copy-done.23, bf16[128,4608]{1,0:T(8,128)(2,1)} %collective-permute-done.23.refs_2_.refs_18_.refs_34_, ...), custom_call_target="tpu_custom_call" | custom-call | flops 3221225472 | bytes 27787264 | tf_op jit(solution)/shard_map/times_turned/pallas_call | solution.py:438
  493.6 4.3 add_convert_fusion.1
  497.9 16.9 %collective-permute-done.64 = bf16[512,2048]{1,0:T(8,128)(2,1)} collective-permute-done((bf16[512,2048]{1,0:T(8,128)(2,1)}, bf16[512,2048]{1,0:T(8,128)(2,1)}, u32[]{:S(2)}, u32[]{:S(2)}) %collective-permute-start.64) | collective-permute-done | bytes 2097184 | tf_op jit(solution)/shard_map/ppermute | solution.py:688
  522.8 5.0 fusion.28
  527.8 5.8 times_rows.3.gmix_ref
  540.6 3.9 copy.173.refs_0_
  549.6 26.5 %mixer_backward.2 = (bf16[512,1536]{1,0:T(8,128)(2,1)}, f32[512,128]{1,0:T(8,128)S(1)}, f32[3,4,512]{2,1,0:T(4,128)S(1)}, f32[1,128]{1,0:T(1,128)S(1)}) custom-call(f32[512,3072]{1,0:T(8,128)} %times_rows.2.proj_ref, f32[512,128]{1,0:T(8,128)S(1)} %copy-done.81, f32[3,4,1024]{2,1,0:T(4,128)S(1)} %copy-done.84, f32[1,128]{1,0:T(1,128)S(1)} %reshape.351.gain_ref, ...), custom_call_target="tpu_custom_call" | custom-call | flops 15728640000 | bytes 10485760 | tf_op jit(solution)/shard_map/mixer_backward/pallas_call | solution.py:351
  588.5 4.3 convert_add_fusion.3
  600.4 4.8 add_convert_fusion.10
  612.7 22.7 %collective-permute-done.65 = bf16[512,2048]{1,0:T(8,128)(2,1)} collective-permute-done((bf16[512,2048]{1,0:T(8,128)(2,1)}, bf16[512,2048]{1,0:T(8,128)(2,1)}, u32[]{:S(2)}, u32[]{:S(2)}) %collective-permute-start.65) | collective-permute-done | bytes 2097184 | tf_op jit(solution)/shard_map/ppermute | solution.py:688
  638.1 6.2 move_columns.6
  654.6 26.7 %mixer_backward.3 = (bf16[512,1536]{1,0:T(8,128)(2,1)}, f32[512,128]{1,0:T(8,128)S(1)}, f32[3,4,512]{2,1,0:T(4,128)S(1)}, f32[1,128]{1,0:T(1,128)S(1)}) custom-call(f32[512,3072]{1,0:T(8,128)} %times_rows.2.proj_ref, f32[512,128]{1,0:T(8,128)S(1)} %copy-done.82, f32[3,4,1024]{2,1,0:T(4,128)S(1)} %copy-done.85, f32[1,128]{1,0:T(1,128)S(1)} %reshape.351.gain_ref, ...), custom_call_target="tpu_custom_call" | custom-call | flops 15728640000 | bytes 10485760 | tf_op jit(solution)/shard_map/mixer_backward/pallas_call | solution.py:351
  699.2 13.3 %times_turned.11 = bf16[512,2048]{1,0:T(8,128)(2,1)} custom-call(bf16[512,3072]{1,0:T(8,128)(2,1)} %pad_maximum_fusion.3.left_ref, bf16[128,4096]{1,0:T(8,128)(2,1)S(1)} %copy-done.54, bf16[128,4096]{1,0:T(8,128)(2,1)} %collective-permute-done.1.refs_1_, bf16[128,4096]{1,0:T(8,128)(2,1)} %collective-permute-done.6.refs_2_, bf16[128,4096]{1,0:T(8,128)(2,1)S(1)} %copy-done.61, ...), custom_call_target="tpu_custom_call" | custom-call | flops 6442450944 | bytes 22020096 | tf_op jit(solution)/shard_map/times_turned/pallas_call | solution.py:438
  729.3 7.7 collective-permute-done.82
  756.5 11.3 %collective-permute-done.84 = bf16[128,2560]{1,0:T(8,128)(2,1)} collective-permute-done((bf16[128,2560]{1,0:T(8,128)(2,1)}, bf16[128,2560]{1,0:T(8,128)(2,1)}, u32[]{:S(2)}, u32[]{:S(2)}) %collective-permute-start.84) | collective-permute-done | bytes 655392 | tf_op jit(solution)/shard_map/ppermute | solution.py:591
  772.2 4.0 pad_maximum_fusion.2
  776.2 5.7 copy.190
  802.7 24.3 %collective-permute-done.78 = bf16[512,2048]{1,0:T(8,128)(2,1)} collective-permute-done((bf16[512,2048]{1,0:T(8,128)(2,1)}, bf16[512,2048]{1,0:T(8,128)(2,1)}, u32[]{:S(2)}, u32[]{:S(2)}) %collective-permute-start.78) | collective-permute-done | bytes 2097184 | tf_op jit(solution)/shard_map/ppermute | solution.py:688
  827.0 3.9 fusion.3
  832.5 5.4 all-to-all-start
  837.9 4.3 fusion.7.in_ref
  842.2 6.7 move_columns.7
  (640 shorter events, 316.7 us)
Async XLA Ops:
  5.3 47.4 %collective-permute-start = (bf16[128,4096]{1,0:T(8,128)(2,1)S(1)}, bf16[128,4096]{1,0:T(8,128)(2,1)}, u32[]{:S(2)}, u32[]{:S(2)}) collective-permute-start(bf16[128,4096]{1,0:T(8,128)(2,1)S(1)} %pad_maximum_fusion.8.refs_0_), channel_id=1, source_target_pairs={{0,8},{2,10},{8,16},{10,18},{16,24},{18,26},{24,28},{26,30},{28,20... | collective-permute-start | bytes 3145736 | tf_op jit(solution)/shard_map/ppermute | solution.py:591
  8.4 44.4 %collective-permute-start.1 = (bf16[128,4096]{1,0:T(8,128)(2,1)S(1)}, bf16[128,4096]{1,0:T(8,128)(2,1)}, u32[]{:S(2)}, u32[]{:S(2)}) collective-permute-start(bf16[128,4096]{1,0:T(8,128)(2,1)S(1)} %pad_maximum_fusion.8.refs_0_), channel_id=1, source_target_pairs={{0,4},{2,6},{8,0},{10,2},{16,8},{18,10},{24,16},{26,18},{28,24},{3... | collective-permute-start | bytes 3145736 | tf_op jit(solution)/shard_map/ppermute | solution.py:591
  53.7 25.5 %collective-permute-start.5 = (bf16[128,4096]{1,0:T(8,128)(2,1)}, bf16[128,4096]{1,0:T(8,128)(2,1)}, u32[]{:S(2)}, u32[]{:S(2)}) collective-permute-start(bf16[128,4096]{1,0:T(8,128)(2,1)} %collective-permute-done.refs_7_), channel_id=1, source_target_pairs={{0,8},{2,10},{8,16},{10,18},{16,24},{18,26},{24,28},{26,30},{28,20... | collective-permute-start | bytes 3145736 | tf_op jit(solution)/shard_map/ppermute | solution.py:591
  53.8 25.5 %collective-permute-start.6 = (bf16[128,4096]{1,0:T(8,128)(2,1)}, bf16[128,4096]{1,0:T(8,128)(2,1)}, u32[]{:S(2)}, u32[]{:S(2)}) collective-permute-start(bf16[128,4096]{1,0:T(8,128)(2,1)} %collective-permute-done.1.refs_1_), channel_id=1, source_target_pairs={{0,4},{2,6},{8,0},{10,2},{16,8},{18,10},{24,16},{26,18},{28,24},{3... | collective-permute-start | bytes 3145736 | tf_op jit(solution)/shard_map/ppermute | solution.py:591
  79.3 24.6 %collective-permute-start.10 = (bf16[128,4096]{1,0:T(8,128)(2,1)}, bf16[128,4096]{1,0:T(8,128)(2,1)S(1)}, u32[]{:S(2)}, u32[]{:S(2)}) collective-permute-start(bf16[128,4096]{1,0:T(8,128)(2,1)} %collective-permute-done.6.refs_2_), channel_id=1, source_target_pairs={{0,4},{2,6},{8,0},{10,2},{16,8},{18,10},{24,16},{26,18},{28,24},{3... | collective-permute-start | bytes 3145736 | tf_op jit(solution)/shard_map/ppermute | solution.py:591
  81.6 25.4 %collective-permute-start.9 = (bf16[128,4096]{1,0:T(8,128)(2,1)}, bf16[128,4096]{1,0:T(8,128)(2,1)}, u32[]{:S(2)}, u32[]{:S(2)}) collective-permute-start(bf16[128,4096]{1,0:T(8,128)(2,1)} %collective-permute-done.5.refs_6_), channel_id=1, source_target_pairs={{0,8},{2,10},{8,16},{10,18},{16,24},{18,26},{24,28},{26,30},{28,20... | collective-permute-start | bytes 3145736 | tf_op jit(solution)/shard_map/ppermute | solution.py:591
  133.8 40.0 %collective-permute-start.16 = (bf16[128,4608]{1,0:T(8,128)(2,1)S(1)}, bf16[128,4608]{1,0:T(8,128)(2,1)S(1)}, u32[]{:S(2)}, u32[]{:S(2)}) collective-permute-start(bf16[128,4608]{1,0:T(8,128)(2,1)S(1)} %copy.147.refs_0_.refs_16_.refs_32_), channel_id=1, source_target_pairs={{0,8},{2,10},{8,16},{10,18},{16,24},{18,26},{24,28},{26,30},{28,20... | collective-permute-start | bytes 3538952 | tf_op jit(solution)/shard_map/ppermute | solution.py:591
  134.1 39.6 %collective-permute-start.17 = (bf16[128,4608]{1,0:T(8,128)(2,1)S(1)}, bf16[128,4608]{1,0:T(8,128)(2,1)S(1)}, u32[]{:S(2)}, u32[]{:S(2)}) collective-permute-start(bf16[128,4608]{1,0:T(8,128)(2,1)S(1)} %copy.147.refs_0_.refs_16_.refs_32_), channel_id=1, source_target_pairs={{0,4},{2,6},{8,0},{10,2},{16,8},{18,10},{24,16},{26,18},{28,24},{3... | collective-permute-start | bytes 3538952 | tf_op jit(solution)/shard_map/ppermute | solution.py:591
  136.4 69.5 %collective-permute-start.15 = (bf16[128,4608]{1,0:T(8,128)(2,1)S(1)}, bf16[128,4608]{1,0:T(8,128)(2,1)S(1)}, u32[]{:S(2)}, u32[]{:S(2)}) collective-permute-start(bf16[128,4608]{1,0:T(8,128)(2,1)S(1)} %copy.147.refs_0_.refs_16_.refs_32_), channel_id=1, source_target_pairs={{0,2},{2,0},{4,6},{6,4},{8,10},{10,8},{12,14},{14,12},{16,18},{18,... | collective-permute-start | bytes 3538952 | tf_op jit(solution)/shard_map/ppermute | solution.py:594
  173.8 33.1 %collective-permute-start.20 = (bf16[128,4608]{1,0:T(8,128)(2,1)S(1)}, bf16[128,4608]{1,0:T(8,128)(2,1)}, u32[]{:S(2)}, u32[]{:S(2)}) collective-permute-start(bf16[128,4608]{1,0:T(8,128)(2,1)S(1)} %collective-permute-done.16.refs_7_.refs_23_.refs_39_), channel_id=1, source_target_pairs={{0,2},{2,0},{4,6},{6,4},{8,10},{10,8},{12,14},{14,12},{16,18},{18,... | collective-permute-start | bytes 3538952 | tf_op jit(solution)/shard_map/ppermute | solution.py:594
  174.4 33.6 %collective-permute-start.22 = (bf16[128,4608]{1,0:T(8,128)(2,1)S(1)}, bf16[128,4608]{1,0:T(8,128)(2,1)}, u32[]{:S(2)}, u32[]{:S(2)}) collective-permute-start(bf16[128,4608]{1,0:T(8,128)(2,1)S(1)} %collective-permute-done.16.refs_7_.refs_23_.refs_39_), channel_id=1, source_target_pairs={{0,8},{2,10},{8,16},{10,18},{16,24},{18,26},{24,28},{26,30},{28,20... | collective-permute-start | bytes 3538952 | tf_op jit(solution)/shard_map/ppermute | solution.py:591
  174.7 32.3 %collective-permute-start.21 = (bf16[128,4608]{1,0:T(8,128)(2,1)S(1)}, bf16[128,4608]{1,0:T(8,128)(2,1)S(1)}, u32[]{:S(2)}, u32[]{:S(2)}) collective-permute-start(bf16[128,4608]{1,0:T(8,128)(2,1)S(1)} %collective-permute-done.17.refs_1_.refs_17_.refs_33_), channel_id=1, source_target_pairs={{0,2},{2,0},{4,6},{6,4},{8,10},{10,8},{12,14},{14,12},{16,18},{18,... | collective-permute-start | bytes 3538952 | tf_op jit(solution)/shard_map/ppermute | solution.py:594
  174.7 33.3 %collective-permute-start.23 = (bf16[128,4608]{1,0:T(8,128)(2,1)S(1)}, bf16[128,4608]{1,0:T(8,128)(2,1)}, u32[]{:S(2)}, u32[]{:S(2)}) collective-permute-start(bf16[128,4608]{1,0:T(8,128)(2,1)S(1)} %collective-permute-done.17.refs_1_.refs_17_.refs_33_), channel_id=1, source_target_pairs={{0,4},{2,6},{8,0},{10,2},{16,8},{18,10},{24,16},{26,18},{28,24},{3... | collective-permute-start | bytes 3538952 | tf_op jit(solution)/shard_map/ppermute | solution.py:591
  208.0 48.1 %collective-permute-start.24 = (bf16[512,2048]{1,0:T(8,128)(2,1)}, bf16[512,2048]{1,0:T(8,128)(2,1)}, u32[]{:S(2)}, u32[]{:S(2)}) collective-permute-start(bf16[512,2048]{1,0:T(8,128)(2,1)} %times_turned.6), channel_id=1, source_target_pairs={{0,1},{1,0},{2,3},{3,2},{4,5},{5,4},{6,7},{7,6},{8,9},{9,8},{10,11... | collective-permute-start | bytes 6291464 | tf_op jit(solution)/shard_map/ppermute | solution.py:688
  210.0 29.2 %collective-permute-start.27 = (bf16[128,4608]{1,0:T(8,128)(2,1)}, bf16[128,4608]{1,0:T(8,128)(2,1)}, u32[]{:S(2)}, u32[]{:S(2)}) collective-permute-start(bf16[128,4608]{1,0:T(8,128)(2,1)} %collective-permute-done.22.refs_6_.refs_22_.refs_38_), channel_id=1, source_target_pairs={{0,8},{2,10},{8,16},{10,18},{16,24},{18,26},{24,28},{26,30},{28,20... | collective-permute-start | bytes 3538952 | tf_op jit(solution)/shard_map/ppermute | solution.py:591
  210.3 29.2 %collective-permute-start.28 = (bf16[128,4608]{1,0:T(8,128)(2,1)}, bf16[128,4608]{1,0:T(8,128)(2,1)}, u32[]{:S(2)}, u32[]{:S(2)}) collective-permute-start(bf16[128,4608]{1,0:T(8,128)(2,1)} %collective-permute-done.23.refs_2_.refs_18_.refs_34_), channel_id=1, source_target_pairs={{0,4},{2,6},{8,0},{10,2},{16,8},{18,10},{24,16},{26,18},{28,24},{3... | collective-permute-start | bytes 3538952 | tf_op jit(solution)/shard_map/ppermute | solution.py:591
  214.3 46.8 %collective-permute-start.33 = (bf16[128,3840]{1,0:T(8,128)(2,1)}, bf16[128,3840]{1,0:T(8,128)(2,1)}, u32[]{:S(2)}, u32[]{:S(2)}) collective-permute-start(bf16[128,3840]{1,0:T(8,128)(2,1)} %copy.154), channel_id=1, source_target_pairs={{0,8},{2,10},{8,16},{10,18},{16,24},{18,26},{24,28},{26,30},{28,20... | collective-permute-start | bytes 2949128 | tf_op jit(solution)/shard_map/ppermute | solution.py:591
  214.6 49.9 %collective-permute-start.34 = (bf16[128,3840]{1,0:T(8,128)(2,1)}, bf16[128,3840]{1,0:T(8,128)(2,1)S(1)}, u32[]{:S(2)}, u32[]{:S(2)}) collective-permute-start(bf16[128,3840]{1,0:T(8,128)(2,1)} %copy.154), channel_id=1, source_target_pairs={{0,4},{2,6},{8,0},{10,2},{16,8},{18,10},{24,16},{26,18},{28,24},{3... | collective-permute-start | bytes 2949128 | tf_op jit(solution)/shard_map/ppermute | solution.py:591
  239.5 35.9 %collective-permute-start.29 = (bf16[128,4608]{1,0:T(8,128)(2,1)}, bf16[128,4608]{1,0:T(8,128)(2,1)S(1)}, u32[]{:S(2)}, u32[]{:S(2)}) collective-permute-start(bf16[128,4608]{1,0:T(8,128)(2,1)} %collective-permute-done.27.refs_5_.refs_21_.refs_37_), channel_id=1, source_target_pairs={{0,2},{2,0},{4,6},{6,4},{8,10},{10,8},{12,14},{14,12},{16,18},{18,... | collective-permute-start | bytes 3538952 | tf_op jit(solution)/shard_map/ppermute | solution.py:594
  240.6 34.8 %collective-permute-start.30 = (bf16[128,4608]{1,0:T(8,128)(2,1)}, bf16[128,4608]{1,0:T(8,128)(2,1)S(1)}, u32[]{:S(2)}, u32[]{:S(2)}) collective-permute-start(bf16[128,4608]{1,0:T(8,128)(2,1)} %collective-permute-done.28.refs_3_.refs_19_.refs_35_), channel_id=1, source_target_pairs={{0,2},{2,0},{4,6},{6,4},{8,10},{10,8},{12,14},{14,12},{16,18},{18,... | collective-permute-start | bytes 3538952 | tf_op jit(solution)/shard_map/ppermute | solution.py:594
  276.5 27.7 %collective-permute-start.36 = (bf16[128,3840]{1,0:T(8,128)(2,1)}, bf16[128,3840]{1,0:T(8,128)(2,1)}, u32[]{:S(2)}, u32[]{:S(2)}) collective-permute-start(bf16[128,3840]{1,0:T(8,128)(2,1)} %collective-permute-done.33.refs_7_.refs_23_.refs_39_), channel_id=1, source_target_pairs={{0,2},{2,0},{4,6},{6,4},{8,10},{10,8},{12,14},{14,12},{16,18},{18,... | collective-permute-start | bytes 2949128 | tf_op jit(solution)/shard_map/ppermute | solution.py:594
  276.5 28.7 %collective-permute-start.38 = (bf16[128,3840]{1,0:T(8,128)(2,1)}, bf16[128,3840]{1,0:T(8,128)(2,1)}, u32[]{:S(2)}, u32[]{:S(2)}) collective-permute-start(bf16[128,3840]{1,0:T(8,128)(2,1)} %collective-permute-done.33.refs_7_.refs_23_.refs_39_), channel_id=1, source_target_pairs={{0,8},{2,10},{8,16},{10,18},{16,24},{18,26},{24,28},{26,30},{28,20... | collective-permute-start | bytes 2949128 | tf_op jit(solution)/shard_map/ppermute | solution.py:591
  279.8 24.4 %collective-permute-start.37 = (bf16[128,3840]{1,0:T(8,128)(2,1)}, bf16[128,3840]{1,0:T(8,128)(2,1)S(1)}, u32[]{:S(2)}, u32[]{:S(2)}) collective-permute-start(bf16[128,3840]{1,0:T(8,128)(2,1)} %copy-done.36), channel_id=1, source_target_pairs={{0,2},{2,0},{4,6},{6,4},{8,10},{10,8},{12,14},{14,12},{16,18},{18,... | collective-permute-start | bytes 2949128 | tf_op jit(solution)/shard_map/ppermute | solution.py:594
  281.6 24.2 %collective-permute-start.39 = (bf16[128,3840]{1,0:T(8,128)(2,1)}, bf16[128,3840]{1,0:T(8,128)(2,1)}, u32[]{:S(2)}, u32[]{:S(2)}) collective-permute-start(bf16[128,3840]{1,0:T(8,128)(2,1)} %copy-done.36), channel_id=1, source_target_pairs={{0,4},{2,6},{8,0},{10,2},{16,8},{18,10},{24,16},{26,18},{28,24},{3... | collective-permute-start | bytes 2949128 | tf_op jit(solution)/shard_map/ppermute | solution.py:591
  305.8 35.0 %collective-permute-start.42 = (bf16[128,3840]{1,0:T(8,128)(2,1)}, bf16[128,3840]{1,0:T(8,128)(2,1)}, u32[]{:S(2)}, u32[]{:S(2)}) collective-permute-start(bf16[128,3840]{1,0:T(8,128)(2,1)} %collective-permute-done.38.refs_6_.refs_22_.refs_38_), channel_id=1, source_target_pairs={{0,2},{2,0},{4,6},{6,4},{8,10},{10,8},{12,14},{14,12},{16,18},{18,... | collective-permute-start | bytes 2949128 | tf_op jit(solution)/shard_map/ppermute | solution.py:594
  305.8 35.0 %collective-permute-start.43 = (bf16[128,3840]{1,0:T(8,128)(2,1)}, bf16[128,3840]{1,0:T(8,128)(2,1)}, u32[]{:S(2)}, u32[]{:S(2)}) collective-permute-start(bf16[128,3840]{1,0:T(8,128)(2,1)} %collective-permute-done.39.refs_2_.refs_18_.refs_34_), channel_id=1, source_target_pairs={{0,2},{2,0},{4,6},{6,4},{8,10},{10,8},{12,14},{14,12},{16,18},{18,... | collective-permute-start | bytes 2949128 | tf_op jit(solution)/shard_map/ppermute | solution.py:594
  306.3 34.5 %collective-permute-start.44 = (bf16[128,3840]{1,0:T(8,128)(2,1)}, bf16[128,3840]{1,0:T(8,128)(2,1)}, u32[]{:S(2)}, u32[]{:S(2)}) collective-permute-start(bf16[128,3840]{1,0:T(8,128)(2,1)} %collective-permute-done.38.refs_6_.refs_22_.refs_38_), channel_id=1, source_target_pairs={{0,8},{2,10},{8,16},{10,18},{16,24},{18,26},{24,28},{26,30},{28,20... | collective-permute-start | bytes 2949128 | tf_op jit(solution)/shard_map/ppermute | solution.py:591
  307.3 33.4 %collective-permute-start.45 = (bf16[128,3840]{1,0:T(8,128)(2,1)}, bf16[128,3840]{1,0:T(8,128)(2,1)}, u32[]{:S(2)}, u32[]{:S(2)}) collective-permute-start(bf16[128,3840]{1,0:T(8,128)(2,1)} %collective-permute-done.39.refs_2_.refs_18_.refs_34_), channel_id=1, source_target_pairs={{0,4},{2,6},{8,0},{10,2},{16,8},{18,10},{24,16},{26,18},{28,24},{3... | collective-permute-start | bytes 2949128 | tf_op jit(solution)/shard_map/ppermute | solution.py:591
  400.4 27.7 %collective-permute-start.56 = (bf16[128,4608]{1,0:T(8,128)(2,1)S(1)}, bf16[128,4608]{1,0:T(8,128)(2,1)S(1)}, u32[]{:S(2)}, u32[]{:S(2)}) collective-permute-start(bf16[128,4608]{1,0:T(8,128)(2,1)S(1)} %pad_maximum_fusion.7), channel_id=1, source_target_pairs={{0,4},{2,6},{8,0},{10,2},{16,8},{18,10},{24,16},{26,18},{28,24},{3... | collective-permute-start | bytes 3538952 | tf_op jit(solution)/shard_map/ppermute | solution.py:591
  403.3 28.2 %collective-permute-start.55 = (bf16[128,4608]{1,0:T(8,128)(2,1)}, bf16[128,4608]{1,0:T(8,128)(2,1)S(1)}, u32[]{:S(2)}, u32[]{:S(2)}) collective-permute-start(bf16[128,4608]{1,0:T(8,128)(2,1)} %pad_maximum_fusion.6), channel_id=1, source_target_pairs={{0,8},{2,10},{8,16},{10,18},{16,24},{18,26},{24,28},{26,30},{28,20... | collective-permute-start | bytes 3538952 | tf_op jit(solution)/shard_map/ppermute | solution.py:591
  434.7 26.7 %collective-permute-start.57 = (bf16[128,4608]{1,0:T(8,128)(2,1)S(1)}, bf16[128,4608]{1,0:T(8,128)(2,1)S(1)}, u32[]{:S(2)}, u32[]{:S(2)}) collective-permute-start(bf16[128,4608]{1,0:T(8,128)(2,1)S(1)} %get-tuple-element.391), channel_id=1, source_target_pairs={{0,8},{2,10},{8,16},{10,18},{16,24},{18,26},{24,28},{26,30},{28,20... | collective-permute-start | bytes 3538952 | tf_op jit(solution)/shard_map/ppermute | solution.py:591
  435.0 26.5 %collective-permute-start.58 = (bf16[128,4608]{1,0:T(8,128)(2,1)S(1)}, bf16[128,4608]{1,0:T(8,128)(2,1)S(1)}, u32[]{:S(2)}, u32[]{:S(2)}) collective-permute-start(bf16[128,4608]{1,0:T(8,128)(2,1)S(1)} %get-tuple-element.390), channel_id=1, source_target_pairs={{0,4},{2,6},{8,0},{10,2},{16,8},{18,10},{24,16},{26,18},{28,24},{3... | collective-permute-start | bytes 3538952 | tf_op jit(solution)/shard_map/ppermute | solution.py:591
  463.4 55.1 %collective-permute-start.61 = (bf16[1024,3840]{1,0:T(8,128)(2,1)}, bf16[1024,3840]{1,0:T(8,128)(2,1)}, u32[]{:S(2)}, u32[]{:S(2)}) collective-permute-start(bf16[1024,3840]{1,0:T(8,128)(2,1)} %weight_grads.13), channel_id=1, source_target_pairs={{0,2},{2,0},{4,6},{6,4},{8,10},{10,8},{12,14},{14,12},{16,18},{18,... | collective-permute-start | bytes 23592968 | tf_op jit(solution)/shard_map/ppermute | solution.py:594
  466.4 48.4 %collective-permute-start.64 = (bf16[512,2048]{1,0:T(8,128)(2,1)}, bf16[512,2048]{1,0:T(8,128)(2,1)}, u32[]{:S(2)}, u32[]{:S(2)}) collective-permute-start(bf16[512,2048]{1,0:T(8,128)(2,1)} %add_convert_fusion.2), channel_id=1, source_target_pairs={{0,1},{1,0},{2,3},{3,2},{4,5},{5,4},{6,7},{7,6},{8,9},{9,8},{10,11... | collective-permute-start | bytes 6291464 | tf_op jit(solution)/shard_map/ppermute | solution.py:688
  473.6 44.9 %collective-permute-start.59 = (bf16[128,4608]{1,0:T(8,128)(2,1)}, bf16[128,4608]{1,0:T(8,128)(2,1)}, u32[]{:S(2)}, u32[]{:S(2)}) collective-permute-start(bf16[128,4608]{1,0:T(8,128)(2,1)} %get-tuple-element.389), channel_id=1, source_target_pairs={{0,8},{2,10},{8,16},{10,18},{16,24},{18,26},{24,28},{26,30},{28,20... | collective-permute-start | bytes 3538952 | tf_op jit(solution)/shard_map/ppermute | solution.py:591
  474.0 44.6 %collective-permute-start.60 = (bf16[128,4608]{1,0:T(8,128)(2,1)}, bf16[128,4608]{1,0:T(8,128)(2,1)}, u32[]{:S(2)}, u32[]{:S(2)}) collective-permute-start(bf16[128,4608]{1,0:T(8,128)(2,1)} %get-tuple-element.388), channel_id=1, source_target_pairs={{0,4},{2,6},{8,0},{10,2},{16,8},{18,10},{24,16},{26,18},{28,24},{3... | collective-permute-start | bytes 3538952 | tf_op jit(solution)/shard_map/ppermute | solution.py:591
  537.3 38.8 %collective-permute-start.67 = (bf16[128,3840]{1,0:T(8,128)(2,1)}, bf16[128,3840]{1,0:T(8,128)(2,1)}, u32[]{:S(2)}, u32[]{:S(2)}) collective-permute-start(bf16[128,3840]{1,0:T(8,128)(2,1)} %pad_maximum_fusion.10), channel_id=1, source_target_pairs={{0,4},{2,6},{8,0},{10,2},{16,8},{18,10},{24,16},{26,18},{28,24},{3... | collective-permute-start | bytes 2949128 | tf_op jit(solution)/shard_map/ppermute | solution.py:591
  540.2 35.9 %collective-permute-start.66 = (bf16[128,3840]{1,0:T(8,128)(2,1)}, bf16[128,3840]{1,0:T(8,128)(2,1)}, u32[]{:S(2)}, u32[]{:S(2)}) collective-permute-start(bf16[128,3840]{1,0:T(8,128)(2,1)} %pad_maximum_fusion.9), channel_id=1, source_target_pairs={{0,8},{2,10},{8,16},{10,18},{16,24},{18,26},{24,28},{26,30},{28,20... | collective-permute-start | bytes 2949128 | tf_op jit(solution)/shard_map/ppermute | solution.py:591
  583.2 61.1 %collective-permute-start.70 = (bf16[1024,2560]{1,0:T(8,128)(2,1)}, bf16[1024,2560]{1,0:T(8,128)(2,1)}, u32[]{:S(2)}, u32[]{:S(2)}) collective-permute-start(bf16[1024,2560]{1,0:T(8,128)(2,1)} %pad_maximum_fusion.1), channel_id=1, source_target_pairs={{0,2},{2,0},{4,6},{6,4},{8,10},{10,8},{12,14},{14,12},{16,18},{18,... | collective-permute-start | bytes 15728648 | tf_op jit(solution)/shard_map/ppermute | solution.py:594
  587.0 48.4 %collective-permute-start.65 = (bf16[512,2048]{1,0:T(8,128)(2,1)}, bf16[512,2048]{1,0:T(8,128)(2,1)}, u32[]{:S(2)}, u32[]{:S(2)}) collective-permute-start(bf16[512,2048]{1,0:T(8,128)(2,1)} %add_convert_fusion.1), channel_id=1, source_target_pairs={{0,1},{1,0},{2,3},{3,2},{4,5},{5,4},{6,7},{7,6},{8,9},{9,8},{10,11... | collective-permute-start | bytes 6291464 | tf_op jit(solution)/shard_map/ppermute | solution.py:688
  605.2 39.1 %collective-permute-start.68 = (bf16[128,3840]{1,0:T(8,128)(2,1)}, bf16[128,3840]{1,0:T(8,128)(2,1)S(1)}, u32[]{:S(2)}, u32[]{:S(2)}) collective-permute-start(bf16[128,3840]{1,0:T(8,128)(2,1)} %get-tuple-element.397), channel_id=1, source_target_pairs={{0,8},{2,10},{8,16},{10,18},{16,24},{18,26},{24,28},{26,30},{28,20... | collective-permute-start | bytes 2949128 | tf_op jit(solution)/shard_map/ppermute | solution.py:591
  606.0 38.3 %collective-permute-start.69 = (bf16[128,3840]{1,0:T(8,128)(2,1)}, bf16[128,3840]{1,0:T(8,128)(2,1)S(1)}, u32[]{:S(2)}, u32[]{:S(2)}) collective-permute-start(bf16[128,3840]{1,0:T(8,128)(2,1)} %get-tuple-element.396), channel_id=1, source_target_pairs={{0,4},{2,6},{8,0},{10,2},{16,8},{18,10},{24,16},{26,18},{28,24},{3... | collective-permute-start | bytes 2949128 | tf_op jit(solution)/shard_map/ppermute | solution.py:591
  646.6 36.5 %collective-permute-start.73 = (bf16[128,1280]{1,0:T(8,128)(2,1)}, bf16[128,1280]{1,0:T(8,128)(2,1)S(1)}, u32[]{:S(2)}, u32[]{:S(2)}) collective-permute-start(bf16[128,1280]{1,0:T(8,128)(2,1)} %get-tuple-element.417), channel_id=1, source_target_pairs={{0,8},{2,10},{8,16},{10,18},{16,24},{18,26},{24,28},{26,30},{28,20... | collective-permute-start | bytes 983048 | tf_op jit(solution)/shard_map/ppermute | solution.py:591
  647.5 35.6 %collective-permute-start.74 = (bf16[128,1280]{1,0:T(8,128)(2,1)}, bf16[128,1280]{1,0:T(8,128)(2,1)}, u32[]{:S(2)}, u32[]{:S(2)}) collective-permute-start(bf16[128,1280]{1,0:T(8,128)(2,1)} %get-tuple-element.416), channel_id=1, source_target_pairs={{0,4},{2,6},{8,0},{10,2},{16,8},{18,10},{24,16},{26,18},{28,24},{3... | collective-permute-start | bytes 983048 | tf_op jit(solution)/shard_map/ppermute | solution.py:591
  652.6 30.6 %collective-permute-start.71 = (bf16[128,3840]{1,0:T(8,128)(2,1)}, bf16[128,3840]{1,0:T(8,128)(2,1)S(1)}, u32[]{:S(2)}, u32[]{:S(2)}) collective-permute-start(bf16[128,3840]{1,0:T(8,128)(2,1)} %get-tuple-element.395), channel_id=1, source_target_pairs={{0,8},{2,10},{8,16},{10,18},{16,24},{18,26},{24,28},{26,30},{28,20... | collective-permute-start | bytes 2949128 | tf_op jit(solution)/shard_map/ppermute | solution.py:591
  653.6 29.5 %collective-permute-start.72 = (bf16[128,3840]{1,0:T(8,128)(2,1)S(1)}, bf16[128,3840]{1,0:T(8,128)(2,1)S(1)}, u32[]{:S(2)}, u32[]{:S(2)}) collective-permute-start(bf16[128,3840]{1,0:T(8,128)(2,1)S(1)} %get-tuple-element.394), channel_id=1, source_target_pairs={{0,4},{2,6},{8,0},{10,2},{16,8},{18,10},{24,16},{26,18},{28,24},{3... | collective-permute-start | bytes 2949128 | tf_op jit(solution)/shard_map/ppermute | solution.py:591
  687.5 25.0 %collective-permute-start.77 = (bf16[1024,1536]{1,0:T(8,128)(2,1)S(1)}, bf16[1024,1536]{1,0:T(8,128)(2,1)}, u32[]{:S(2)}, u32[]{:S(2)}) collective-permute-start(bf16[1024,1536]{1,0:T(8,128)(2,1)S(1)} %weight_grads.19), channel_id=1, source_target_pairs={{0,2},{2,0},{4,6},{6,4},{8,10},{10,8},{12,14},{14,12},{16,18},{18,... | collective-permute-start | bytes 9437192 | tf_op jit(solution)/shard_map/ppermute | solution.py:594
  781.9 45.1 %collective-permute-start.78 = (bf16[512,2048]{1,0:T(8,128)(2,1)}, bf16[512,2048]{1,0:T(8,128)(2,1)}, u32[]{:S(2)}, u32[]{:S(2)}) collective-permute-start(bf16[512,2048]{1,0:T(8,128)(2,1)} %times_turned.11), channel_id=1, source_target_pairs={{0,1},{1,0},{2,3},{3,2},{4,5},{5,4},{6,7},{7,6},{8,9},{9,8},{10,11... | collective-permute-start | bytes 6291464 | tf_op jit(solution)/shard_map/ppermute | solution.py:688
  (194 other events, 2357.3 us)

commit v3 on v1

--- a/solution.py
+++ b/solution.py
@@ -75,9 +75,9 @@
     return jnp.sum(jnp.where(lanes == head, beta_ref[...], 0.0), axis=1, keepdims=True)
 
 
-def forward_kernel(heads, passes, proj_ref, beta_ref, conv_ref, gain_ref, segc_ref, segr_ref,
+def forward_kernel(heads, passes, first, proj_ref, beta_ref, conv_ref, gain_ref, segc_ref, segr_ref,
                    mixed_ref, out_ref, writes_ref, solve_ref, state_ref, q_scr, k_scr, v_scr):
-    group = pl.program_id(0)
+    group = first + pl.program_id(0)
     length = proj_ref.shape[0]
     chunks = length // CHUNK
     width = 128
@@ -168,11 +168,11 @@
                 state[h] = carry_last * state[h] + add
 
 
-def backward_kernel(heads, passes, proj_ref, beta_ref, conv_ref, gain_ref, segc_ref, segr_ref,
+def backward_kernel(heads, passes, first, proj_ref, beta_ref, conv_ref, gain_ref, segc_ref, segr_ref,
                     out_ref, writes_ref, solve_ref, state_ref, gmix_ref,
                     gproj_ref, gbeta_ref, gconv_ref, ggain_ref,
                     q_scr, k_scr, v_scr, gq_scr, gk_scr, gv_scr, do_scr):
-    group = pl.program_id(0)
+    group = first + pl.program_id(0)
     length = proj_ref.shape[0]
     chunks = length // CHUNK
     width = 128
@@ -181,7 +181,7 @@
     gates = [allowed_rows(seg_full, offset) for offset in (1, 2, 3)]
     gain = gain_ref[...]
 
-    @pl.when(group == 0)
+    @pl.when(pl.program_id(0) == 0)
     def _():
         gbeta_ref[...] = jnp.zeros_like(gbeta_ref)
         ggain_ref[...] = jnp.zeros_like(ggain_ref)
@@ -310,122 +310,694 @@
             gproj_ref[:, column : column + width] = gsignal.astype(BF16)
 
 
-def mixer_forward(projected, logits, conv, gain, seg_ids, heads, passes):
-    length, columns = projected.shape
-    groups = columns // (3 * heads * 128)
+def mixer_specs(length, wide, first):
+    fixed = lambda shape: pl.BlockSpec(shape, lambda g: (0,) * len(shape))
+    return [
+        pl.BlockSpec((length, 3 * wide), lambda g: (0, g + first)),
+        fixed((length, 128)),
+        pl.BlockSpec((3, 4, wide), lambda g: (0, 0, g + first)),
+        fixed((1, 128)),
+        fixed((length, 1)),
+        fixed((1, length)),
+    ]
+
+
+def mixer_forward(projected, logits, conv, gain, seg_ids, heads, passes, first, count):
+    length = projected.shape[0]
     wide = heads * 128
-    f32 = lambda: jax.ShapeDtypeStruct((length, groups * wide), F32)
+    f32 = jax.ShapeDtypeStruct((length, count * wide), F32)
     block = pl.BlockSpec((length, wide), lambda g: (0, g))
+    return pl.pallas_call(
+        functools.partial(forward_kernel, heads, passes, first),
+        grid=(count,),
+        in_specs=mixer_specs(length, wide, first),
+        out_specs=[block] * 5,
+        out_shape=[jax.ShapeDtypeStruct((length, count * wide), BF16), f32, f32, f32, f32],
+        scratch_shapes=[pltpu.VMEM((length, wide), F32)] * 3,
+        compiler_params=pltpu.CompilerParams(vmem_limit_bytes=48 * 2**20),
+        cost_estimate=pl.CostEstimate(flops=1000, bytes_accessed=1000, transcendentals=0),
+        name="mixer_forward",
+    )(projected, logits, conv, gain, seg_ids[:, None], seg_ids[None, :])
+
+
+def mixer_backward(projected, logits, conv, gain, seg_ids, saved, grad_mixed, heads, passes, first, count, base):
+    length = projected.shape[0]
+    wide = heads * 128
+    block = pl.BlockSpec((length, wide), lambda g: (0, g + first - base))
+    grads = pl.BlockSpec((length, wide), lambda g: (0, g + first))
     fixed = lambda shape: pl.BlockSpec(shape, lambda g: (0,) * len(shape))
     return pl.pallas_call(
-        functools.partial(forward_kernel, heads, passes),
-        grid=(groups,),
-        in_specs=[
+        functools.partial(backward_kernel, heads, passes, first),
+        grid=(count,),
+        in_specs=mixer_specs(length, wide, first) + [block] * 4 + [grads],
+        out_specs=[
             pl.BlockSpec((length, 3 * wide), lambda g: (0, g)),
             fixed((length, 128)),
             pl.BlockSpec((3, 4, wide), lambda g: (0, 0, g)),
             fixed((1, 128)),
-            fixed((length, 1)),
-            fixed((1, length)),
         ],
-        out_specs=[block] * 5,
-        out_shape=[jax.ShapeDtypeStruct((length, groups * wide), BF16), f32(), f32(), f32(), f32()],
-        scratch_shapes=[pltpu.VMEM((length, wide), F32)] * 3,
-        compiler_params=pltpu.CompilerParams(vmem_limit_bytes=56 * 2**20),
-        name="mixer_forward",
-    )(projected, logits, conv, gain, seg_ids[:, None], seg_ids[None, :])
-
-
-def mixer_backward(projected, logits, conv, gain, seg_ids, saved, grad_mixed, heads, passes):
-    length, columns = projected.shape
-    groups = columns // (3 * heads * 128)
-    wide = heads * 128
-    block = pl.BlockSpec((length, wide), lambda g: (0, g))
-    fixed = lambda shape: pl.BlockSpec(shape, lambda g: (0,) * len(shape))
-    triple = pl.BlockSpec((length, 3 * wide), lambda g: (0, g))
-    taps = pl.BlockSpec((3, 4, wide), lambda g: (0, 0, g))
-    return pl.pallas_call(
-        functools.partial(backward_kernel, heads, passes),
-        grid=(groups,),
-        in_specs=[triple, fixed((length, 128)), taps, fixed((1, 128)), fixed((length, 1)), fixed((1, length))] + [block] * 5,
-        out_specs=[triple, fixed((length, 128)), taps, fixed((1, 128))],
         out_shape=[
-            jax.ShapeDtypeStruct((length, columns), BF16),
+            jax.ShapeDtypeStruct((length, 3 * count * wide), BF16),
             jax.ShapeDtypeStruct((length, 128), F32),
-            jax.ShapeDtypeStruct((3, 4, groups * wide), F32),
+            jax.ShapeDtypeStruct((3, 4, count * wide), F32),
             jax.ShapeDtypeStruct((1, 128), F32),
         ],
         scratch_shapes=[pltpu.VMEM((length, wide), F32)] * 7,
-        compiler_params=pltpu.CompilerParams(vmem_limit_bytes=56 * 2**20),
+        compiler_params=pltpu.CompilerParams(vmem_limit_bytes=48 * 2**20),
+        cost_estimate=pl.CostEstimate(flops=1000, bytes_accessed=1000, transcendentals=0),
         name="mixer_backward",
     )(projected, logits, conv, gain, seg_ids[:, None], seg_ids[None, :], *saved, grad_mixed)
 
 
+LIMIT = 48 * 2**20
+
+
+def whole(array):
+    return pl.BlockSpec(array.shape, lambda *_: (0,) * array.ndim)
+
+
+def call(kernel, grid, in_specs, out_specs, out_shape, name, table, *operands, scratch=()):
+    return pl.pallas_call(
+        kernel,
+        grid_spec=pltpu.PrefetchScalarGridSpec(
+            num_scalar_prefetch=1,
+            grid=grid,
+            in_specs=in_specs,
+            out_specs=out_specs,
+            scratch_shapes=scratch,
+        ),
+        out_shape=out_shape,
+        compiler_params=pltpu.CompilerParams(vmem_limit_bytes=LIMIT),
+        cost_estimate=pl.CostEstimate(flops=1000, bytes_accessed=1000, transcendentals=0),
+        name=name,
+    )(table, *operands)
+
+
+IN_PLACE = pl.BlockSpec(memory_space=pl.ANY)
+
+
+def lanes_at(place, width):
+    return pl.ds(pl.multiple_of(place * width, width), width)
+
+
+def column_tiles(blocks, starts, tile, table_ref, hold, sems):
+    rows = blocks[0].shape[0]
+    step, count = pl.program_id(0), pl.num_programs(0)
+
+    def copies(at):
+        slot = lax.rem(at, 2)
+        for w, start in enumerate(starts):
+            columns = pl.ds(pl.multiple_of(start + at * tile, 128), tile)
+            for r, block in enumerate(blocks):
+                yield pltpu.make_async_copy(
+                    block.at[:, columns],
+                    hold.at[slot, w, lanes_at(table_ref[r], rows), :],
+                    sems.at[slot, w, r],
+                )
+
+    @pl.when(step == 0)
+    def _():
+        for copy in copies(step):
+            copy.start()
+
+    @pl.when(step + 1 < count)
+    def _():
+        for copy in copies(step + 1):
+            copy.start()
+
+    for copy in copies(step):
+        copy.wait()
+    return lax.rem(step, 2)
+
+
+def tile_scratch(blocks, ranges, tile):
+    rows, count = blocks[0].shape[0], len(blocks)
+    return [
+        pltpu.VMEM((2, ranges, rows * count, tile), BF16),
+        pltpu.SemaphoreType.DMA((2, ranges, count)),
+    ]
+
+
+def rows_kernel(count, start, tile, table_ref, left_ref, *refs):
+    blocks, (out_ref, hold, sems) = refs[:count], refs[count:]
+    slot = column_tiles(blocks, [start], tile, table_ref, hold, sems)
+    out_ref[...] = dot1(left_ref[...], hold[slot, 0], NN).astype(out_ref.dtype)
+
+
+def times_rows(left, blocks, table, start, columns, tile, kind):
+    return call(
+        functools.partial(rows_kernel, len(blocks), start, tile),
+        (columns // tile,),
+        [whole(left)] + [IN_PLACE] * len(blocks),
+        pl.BlockSpec((left.shape[0], tile), lambda i, t: (0, i)),
+        jax.ShapeDtypeStruct((left.shape[0], columns), kind),
+        "times_rows",
+        table,
+        left,
+        *blocks,
+        scratch=tile_scratch(blocks, 1, tile),
+    )
+
+
+def gated_kernel(table_ref, normed_ref, cot_ref, gate_ref, up_ref, down_ref, out_ref):
+    gate = dot1(normed_ref[...], gate_ref[...], NN)
+    up = dot1(normed_ref[...], up_ref[...], NN)
+    grad = dot1(cot_ref[...], down_ref[...], NN)
+    sig = jax.nn.sigmoid(gate)
+    silu = gate * sig
+    out_ref[0] = (grad * up * sig * (1.0 + gate * (1.0 - sig))).astype(BF16)
+    out_ref[1] = (grad * silu).astype(BF16)
+    out_ref[2] = (silu * up).astype(BF16)
+
+
+def gated_units(normed, cot, mat, table, tile):
+    width, columns = mat.shape
+    units = columns // 3
+    each = units // tile
+    length = normed.shape[0]
+
+    def spec(which):
+        return pl.BlockSpec((width, tile), lambda i, t: (0, which * each + i))
+
+    return call(
+        gated_kernel,
+        (each,),
+        [whole(normed), whole(cot)] + [spec(w) for w in range(3)],
+        pl.BlockSpec((3, length, tile), lambda i, t: (0, 0, i)),
+        jax.ShapeDtypeStruct((3, length, units), BF16),
+        "gated_units",
+        table,
+        normed,
+        cot,
+        mat,
+        mat,
+        mat,
+    )
+
+
+def units_kernel(terms, plus, table_ref, *refs):
+    out_ref = refs[-1]
+    total = refs[2 * terms][...] if plus else None
+    for n in range(terms):
+        part = dot1(refs[n][...], refs[terms + n][...], NT)
+        total = part if total is None else total + part
+    out_ref[...] = total.astype(out_ref.dtype)
+
+
+def units_turned(terms, tile, kind, table, plus=None):
+    acts, mats, act_specs, mat_specs = [], [], [], []
+    for act, plane, mat in terms:
+        length, units = act.shape[1:]
+        width = mat.shape[0]
+        acts.append(act)
+        mats.append(mat)
+        act_specs.append(pl.BlockSpec((None, length, units), lambda i, t, p=plane: (p, 0, 0)))
+        mat_specs.append(pl.BlockSpec((tile, units), lambda i, t, p=plane: (i, p)))
+    column = pl.BlockSpec((length, tile), lambda i, t: (0, i))
+    more = [] if plus is None else [plus]
+    return call(
+        functools.partial(units_kernel, len(terms), len(more)),
+        (width // tile,),
+        act_specs + mat_specs + [column for _ in more],
+        column,
+        jax.ShapeDtypeStruct((length, width), kind),
+        "units_turned",
+        table,
+        *acts,
+        *mats,
+        *more,
+    )
+
+
+def turned_kernel(plan, extra, table_ref, *refs):
+    lefts = refs[: sum(len(pieces) for _, _, _, pieces in plan)]
+    refs = refs[len(lefts) :]
+    blocks = []
+    for count, _, _, _ in plan:
+        blocks.append(refs[:count])
+        refs = refs[count:]
+    tail, refs = refs[:extra], refs[extra:]
+    out_ref, sems, holds = refs[0], refs[1], refs[2:]
+    step, last = pl.program_id(0), pl.num_programs(0) - 1
+    rows = blocks[0][0].shape[0]
+    count = len(blocks[0])
+
+    def copies(r):
+        for g, (_, start, width, _) in enumerate(plan):
+            yield pltpu.make_async_copy(
+                blocks[g][r].at[:, start : start + width],
+                holds[g].at[r // 2 % 2, r % 2 * rows : (r % 2 + 1) * rows, :],
+                sems.at[g, r // 2 % 2, r % 2],
+            )
+
+    for r in range(count):
+        if r < 2:
+
+            @pl.when(step == 0)
+            def _():
+                for copy in copies(r):
+                    copy.start()
+
+        else:
+
+            @pl.when(step + 1 == r // 2)
+            def _():
+                for copy in copies(r):
+                    copy.start()
+
+    for r in range(count):
+
+        @pl.when(step == r // 2)
+        def _():
+            for copy in copies(r):
+                copy.wait()
+
+    slot = lax.rem(step, 2)
+    total, at = None, 0
+    for g, (_, _, _, pieces) in enumerate(plan):
+        low = 0
+        for plane in pieces:
+            left = lefts[at][plane] if plane is not None else lefts[at][...]
+            high = low + left.shape[1]
+            part = dot1(left, holds[g][slot, :, low:high], NT)
+            total = part if total is None else total + part
+            low, at = high, at + 1
+    for k in range(2):
+        place = table_ref[2 * step + k]
+        piece = total[:, k * rows : (k + 1) * rows]
+        if extra:
+            piece = piece + dot1(tail[0][...], tail[1][lanes_at(place, rows), :], NT)
+        out_ref[:, lanes_at(place, rows)] = piece.astype(BF16)
+
+
+def times_turned(groups, table, extra=()):
+    plan, lefts, left_specs, blocks = [], [], [], []
+    for pieces, own_blocks, start in groups:
+        width, planes = 0, []
+        for piece in pieces:
+            if isinstance(piece, tuple):
+                piece, plane = piece
+                planes.append(0)
+                left_specs.append(
+                    pl.BlockSpec((1,) + piece.shape[1:], lambda i, t, plane=plane: (plane, 0, 0))
+                )
+            else:
+                planes.append(None)
+                left_specs.append(whole(piece))
+            lefts.append(piece)
+            width += piece.shape[-1]
+        plan.append((len(own_blocks), start, width, planes))
+        blocks += own_blocks
+    rows, count = groups[0][1][0].shape[0], plan[0][0]
+    length = lefts[0].shape[-2]
+    out = jax.ShapeDtypeStruct((length, rows * count), BF16)
+    return call(
+        functools.partial(turned_kernel, plan, len(extra)),
+        (count // 2,),
+        left_specs + [IN_PLACE] * len(blocks) + [whole(a) for a in extra],
+        whole(out),
+        out,
+        "times_turned",
+        table,
+        *lefts,
+        *blocks,
+        *extra,
+        scratch=[pltpu.SemaphoreType.DMA((len(plan), 2, 2))]
+        + [pltpu.VMEM((2, 2 * rows, width), BF16) for _, _, width, _ in plan],
+    )
+
+
+def weight_kernel(cuts, which, plus, table_ref, *refs):
+    pairs = len(cuts) - 1
+    lefts, rights, out_ref, turned = refs[:pairs], refs[pairs : 2 * pairs], refs[-2], refs[-1]
+    step = pl.program_id(0)
+    block = 128
+    for n in range(pairs):
+
+        @pl.when(step == cuts[n])
+        def _():
+            for at in range(turned.shape[0] // block):
+                if which is None:
+                    lanes = slice(at * block, (at + 1) * block)
+                else:
+                    lanes = lanes_at(2 * at + table_ref[which], block)
+                turned[at * block : (at + 1) * block, :] = lefts[n][:, lanes].T
+
+        @pl.when((step >= cuts[n]) & (step < cuts[n + 1]))
+        def _():
+            product = dot1(turned[...], rights[n][...], NN)
+            if plus:
+                product = product + refs[2 * pairs][...].reshape(product.shape).astype(F32)
+            out_ref[...] = product.astype(BF16).reshape(out_ref.shape)
+
+
+def weight_grads(pairs, tile, rows, cores, which, plus=None):
+    length, features = pairs[0][0].shape
+    chips = features // (2 * rows)
+    inside = rows % 128 == 0
+    cuts, lefts, rights, specs = [0], [], [], []
+    for left, right, plane, planes in pairs:
+        if not inside:
+            left = left.reshape(length, chips, 2, rows)
+            left = lax.dynamic_index_in_dim(left, cores[which], 2, keepdims=False)
+            left = left.reshape(length, chips * rows)
+        each = right.shape[-1] // tile
+        low, most = cuts[-1], planes * each - 1
+        if right.ndim == 3:
+            spec = pl.BlockSpec(
+                (None, length, tile),
+                lambda i, t, low=low, most=most, plane=plane, each=each: (
+                    plane + jnp.clip(i - low, 0, most) // each,
+                    0,
+                    jnp.clip(i - low, 0, most) % each,
+                ),
+            )
+        else:
+            spec = pl.BlockSpec(
+                (length, tile), lambda i, t, low=low, most=most: (0, jnp.clip(i - low, 0, most))
+            )
+        lefts.append(left)
+        rights.append(right)
+        specs.append(spec)
+        cuts.append(low + most + 1)
+    place = pl.BlockSpec((chips, rows, tile), lambda i, t: (0, 0, i))
+    more = [] if plus is None else [plus]
+    return call(
+        functools.partial(weight_kernel, cuts, which if inside else None, len(more)),
+        (cuts[-1],),
+        [whole(left) for left in lefts] + specs + [place for _ in more],
+        place,
+        jax.ShapeDtypeStruct((chips, rows, cuts[-1] * tile), BF16),
+        "weight_grads",
+        cores,
+        *lefts,
+        *rights,
+        *more,
+        scratch=[pltpu.VMEM((chips * rows, length), BF16)],
+    )
+
+
+def hop_tile(half):
+    for parts in (2, 3, 1):
+        if half % (128 * parts) == 0:
+            return half // parts
+    return 128
+
+
+def hop_kernel(kind, each, table_ref, *refs):
+    step = pl.program_id(0)
+    for d in range(2):
+        total = refs[d][...]
+        if kind == "first":
+            refs[2 + d][...] = total
+        elif kind == "middle":
+            refs[4 + d][...] = (total.astype(F32) + refs[2 + d][...].astype(F32)).astype(BF16)
+        else:
+            mine = (step < each) if d == 0 else (step >= each)
+
+            @pl.when(mine)
+            def _():
+                refs[4 + d][...] = (total.astype(F32) + refs[2 + d][...].astype(F32)).astype(BF16)
+
+            @pl.when(jnp.logical_not(mine))
+            def _():
+                refs[4 + d][...] = total
+
+
+def ring_hop(kind, own, got, table, ahead, behind):
+    chips, rows, columns = own.shape
+    half = columns // 2
+    tile = hop_tile(half)
+    each = half // tile
+
+    def term(place, offset=0):
+        return pl.BlockSpec((None, rows, tile), lambda i, t: (t[place], 0, i + offset))
+
+    flat = pl.BlockSpec((rows, tile), lambda i, t: (0, i))
+    if kind == "first":
+        specs = [term(ahead), term(behind, each)]
+        steps, width = each, half
+    else:
+        specs = [term(ahead), term(behind)]
+        steps, width = 2 * each, columns
+        if kind == "middle":
+            specs += [flat, flat]
+        else:
+            specs += [
+                pl.BlockSpec((rows, tile), lambda i, t: (0, jnp.minimum(i, each - 1))),
+                pl.BlockSpec((rows, tile), lambda i, t: (0, jnp.maximum(i - each, 0))),
+            ]
+    return call(
+        functools.partial(hop_kernel, kind, each),
+        (steps,),
+        specs,
+        [flat, flat],
+        [jax.ShapeDtypeStruct((rows, width), BF16)] * 2,
+        "ring_hop",
+        table,
+        own,
+        own,
+        *got,
+    )
+
+
+def landed(refs):
+    return refs[0][...].astype(F32) + refs[1][...].astype(F32) + refs[2][...].astype(F32)
+
+
+def units_result_kernel(table_ref, *refs):
+    low = 0
+    for n in range(0, len(refs) - 1, 3):
+        total = landed(refs[n : n + 3])
+        refs[-1][:, low : low + total.shape[1]] = total
+        low += total.shape[1]
+
+
+def units_result(sums, table):
+    operands, specs, units = [], [], 0
+    for own, ahead, behind in sums:
+        _, rows, columns = own.shape
+        units += columns // 3
+        term = pl.BlockSpec((None, rows, columns // 3), lambda i, t: (t[0], 0, i))
+        flat = pl.BlockSpec((rows, columns // 3), lambda i, t: (0, i))
+        operands += [own, ahead, behind]
+        specs += [term, flat, flat]
+    return call(
+        units_result_kernel,
+        (3,),
+        specs,
+        pl.BlockSpec((None, rows, units), lambda i, t: (i, 0, 0)),
+        jax.ShapeDtypeStruct((3, rows, units), F32),
+        "units_result",
+        table,
+        *operands,
+    )
+
+
+def mixer_result_kernel(wide, table_ref, *refs):
+    out_ref = refs[-1]
+    group = 0
+    for n in range(0, len(refs) - 1, 3):
+        total = landed(refs[n : n + 3])
+        columns = total.shape[1]
+        low = 0
+        while columns - low >= 3 * wide and (n > 0 or columns - low > out_ref.shape[2]):
+            for p in range(3):
+                out_ref[:, p, group * wide : (group + 1) * wide] = total[:, low : low + wide]
+                low += wide
+            group += 1
+        if low < columns:
+            out_ref[:, 3, :] = total[:, low:]
+
+
+def mixer_result(sums, wide, local_width, table):
+    operands, specs = [], []
+    step = 32
+    for own, ahead, behind in sums:
+        _, rows, columns = own.shape
+        term = pl.BlockSpec((None, step, columns), lambda i, t: (t[0], i, 0))
+        flat = pl.BlockSpec((step, columns), lambda i, t: (i, 0))
+        operands += [own, ahead, behind]
+        specs += [term, flat, flat]
+    return call(
+        functools.partial(mixer_result_kernel, wide),
+        (rows // step,),
+        specs,
+        pl.BlockSpec((step, 4, local_width), lambda i, t: (i, 0, 0)),
+        jax.ShapeDtypeStruct((rows, 4, local_width), F32),
+        "mixer_result",
+        table,
+        *operands,
+    )
+
+
+def pack_kernel(wide, in_ref, out_ref):
+    low = 0
+    for group in range(in_ref.shape[2] // wide):
+        for p in range(3):
+            out_ref[:, low : low + wide] = in_ref[:, p, group * wide : (group + 1) * wide].astype(BF16)
+            low += wide
+    out_ref[:, low:] = in_ref[:, 3, :].astype(BF16)
+
+
+def pack_mixer(weights, wide):
+    rows, _, width = weights.shape
+    step = 32
+    return pl.pallas_call(
+        functools.partial(pack_kernel, wide),
+        grid=(rows // step,),
+        in_specs=[pl.BlockSpec((step, 4, width), lambda i: (i, 0, 0))],
+        out_specs=pl.BlockSpec((step, 4 * width), lambda i: (i, 0)),
+        out_shape=jax.ShapeDtypeStruct((rows, 4 * width), BF16),
+        cost_estimate=pl.CostEstimate(flops=1000, bytes_accessed=1000, transcendentals=0),
+        name="pack_mixer",
+    )(weights)
+
+
 HEADS_PER_STEP = 2
 PASSES = 3
-
-
-def matmul(left, right, dims, kind=F32):
-    return lax.dot_general(left, right, dims, preferred_element_type=F32).astype(kind)
-
-
-def ring_order(chips):
-    return [2 * i for i in range(chips // 2)] + [2 * i + 1 for i in reversed(range(chips // 2))]
+PORTIONS = 4
+
+
+class Box:
+    def __init__(self, value):
+        self.value = value
+
+
+def sync(*boxes):
+    values = lax.optimization_barrier(tuple(box.value for box in boxes))
+    for box, value in zip(boxes, values):
+        box.value = value
+
+
+class Ring:
+    def __init__(self, devices):
+        self.chips = chips = devices // 2
+        self.order = [2 * i for i in range(chips // 2)]
+        self.order += [2 * i + 1 for i in reversed(range(chips // 2))]
+        place = [self.order.index(c) for c in range(chips)]
+        index = lax.axis_index("dp")
+        chip, core = index // 2, index % 2
+        here = jnp.asarray(place, jnp.int32)[chip]
+        self.around = jnp.asarray(self.order, jnp.int32)[(here + jnp.arange(chips, dtype=jnp.int32)) % chips]
+        self.cores = jnp.stack([core, 1 - core]).astype(jnp.int32)
+        self.table = jnp.concatenate([2 * self.around + core, 2 * self.around + 1 - core])
+        self.core_swap = [(i, i ^ 1) for i in range(devices)]
+        self.hops = {}
+        for turn in (1, -1):
+            hops = []
+            for at, source in enumerate(self.order):
+                target = self.order[(at + turn) % chips]
+                hops += [(2 * source, 2 * target), (2 * source + 1, 2 * target + 1)]
+            self.hops[turn] = hops
+
+    def send(self, value, turn):
+        return Box(lax.ppermute(value, "dp", self.hops[turn]))
+
+    def swap(self, value):
+        return Box(lax.ppermute(value, "dp", self.core_swap))
+
+    def steps(self, portion):
+        total = self.chips // 2
+        return range(total * portion // PORTIONS + 1, total * (portion + 1) // PORTIONS + 1)
+
+
+class Gather:
+    def __init__(self, ring, own):
+        self.ring = ring
+        box = Box(own)
+        self.blocks = {(0, 0): [box]}
+        self.front = {1: box, -1: box}
+        self.fresh = [((0, 0), box)]
+        self.pending = [box]
+
+    def swap(self, boxes=None):
+        if boxes is None:
+            boxes, self.fresh = self.fresh, []
+        for (at, _), box in boxes:
+            other = self.ring.swap(box.value)
+            self.blocks.setdefault((at, 1), []).append(other)
+            self.pending.append(other)
+
+    def advance(self, portion):
+        chips = self.ring.chips
+        came, self.fresh = self.fresh, []
+        for step in self.ring.steps(portion):
+            for turn in (1, -1):
+                value = self.front[turn].value
+                if 2 * step == chips:
+                    half = value.shape[1] // 2
+                    value = value[:, :half] if turn == 1 else value[:, half:]
+                box = self.ring.send(value, turn)
+                key = (-turn * step % chips, 0)
+                self.blocks.setdefault(key, []).append(box)
+                self.front[turn] = box
+                self.fresh.append((key, box))
+                self.pending.append(box)
+        self.swap(came)
+
+    def boxes(self):
+        waiting, self.pending = self.pending, []
+        return waiting
+
+    def ordered(self):
+        out = []
+        for core in range(2):
+            for at in range(self.ring.chips):
+                parts = [box.value for box in self.blocks[at, core]]
+                out.append(parts[0] if len(parts) == 1 else jnp.concatenate(parts, axis=1))
+        return out
+
+
+class Scatter:
+    def __init__(self, ring, grads):
+        self.ring = ring
+        self.grads = grads
+        self.other = Box(grads(1, None))
+        self.own = None
+        self.got = []
+
+    def swap(self):
+        self.other = self.ring.swap(self.other.value)
+
+    def join(self):
+        self.own = Box(self.grads(0, self.other.value))
+
+    def advance(self, portion):
+        chips = self.ring.chips
+        for step in self.ring.steps(portion):
+            away = chips // 2 - step + 1
+            kind = {1: "first", 2: "second"}.get(step, "middle")
+            got = [box.value for box in self.got]
+            out = ring_hop(kind, self.own.value, got, self.ring.around, away, chips - away)
+            self.got = [self.ring.send(out[0], 1), self.ring.send(out[1], -1)]
+
+    def boxes(self):
+        return [self.other if self.own is None else self.own] + self.got
+
+    def parts(self):
+        return [self.own.value, self.got[0].value, self.got[1].value]
+
+
+class Exchange:
+    def __init__(self, part, pieces):
+        self.part = part
+        blocks = part.shape[0] // 32
+        self.cuts = [32 * (blocks * i // pieces) for i in range(pieces + 1)]
+        self.got = []
+
+    def advance(self):
+        at = len(self.got)
+        self.got.append(Box(swap_tensor(self.part[self.cuts[at] : self.cuts[at + 1]])))
+        return self.got[-1]
+
+    def result(self):
+        other = jnp.concatenate([box.value for box in self.got], axis=0)
+        return self.part.astype(F32) + other.astype(F32)
 
 
 def swap_tensor(value):
     return lax.ppermute(value, "tensor", [(0, 1), (1, 0)])
-
-
-def pair_sum(part):
-    low = part.astype(BF16)
-    return low.astype(F32) + swap_tensor(low).astype(F32)
-
-
-def pair_split(rows, width, core):
-    blocks = rows.reshape(rows.shape[0], -1, 2, width)
-    own = lax.dynamic_index_in_dim(blocks, core, 2, keepdims=False)
-    other = lax.dynamic_index_in_dim(blocks, 1 - core, 2, keepdims=False)
-    flat = (rows.shape[0], -1)
-    return own.reshape(flat), other.reshape(flat)
-
-
-def ring_scatter(own, other, chip, forward):
-    chips = lax.axis_size("dp") // 2
-    rows = own.shape[0] // chips
-    order = ring_order(chips)
-    place = [order.index(c) for c in range(chips)]
-    table = jnp.asarray(order, jnp.int32)
-    here = jnp.asarray(place, jnp.int32)[chip]
-    turn = 1 if forward else -1
-    hops = []
-    for position, source in enumerate(order):
-        target = order[(position + turn) % chips]
-        hops += [(2 * source, 2 * target), (2 * source + 1, 2 * target + 1)]
-
-    def local(step):
-        at = table[(here - turn * (step + 1)) % chips] * rows
-        a = lax.dynamic_slice_in_dim(own, at, rows, 0)
-        b = lax.dynamic_slice_in_dim(other, at, rows, 0)
-        return a.astype(F32) + b.astype(F32)
-
-    total = local(0)
-    for step in range(1, chips):
-        moved = lax.ppermute(total.astype(BF16), "dp", hops)
-        total = local(step) + moved.astype(F32)
-    return total
-
-
-def scatter_grads(own, other, chip, core_swap):
-    other = lax.ppermute(other, "dp", core_swap)
-    half = own.shape[1] // 2
-    return jnp.concatenate(
-        [
-            ring_scatter(own[:, :half], other[:, :half], chip, True),
-            ring_scatter(own[:, half:], other[:, half:], chip, False),
-        ],
-        axis=1,
-    )
 
 
 def norm_back(values, scale, gain, grad):
@@ -433,6 +1005,20 @@
     inner = jnp.mean(values * scaled, axis=-1, keepdims=True)
     gain_grad = jnp.sum(values * scale * grad, axis=0)
     return scale * scaled - values * (scale * scale * scale) * inner, gain_grad
+
+
+def matmul(left, right, dims):
+    return lax.dot_general(left, right, dims, preferred_element_type=F32)
+
+
+def even_blocks(matrix):
+    return [matrix[i : i + 128] for i in range(0, matrix.shape[0], 128)]
+
+
+def unit_chunks(units):
+    tile = 256
+    cut = units // tile * 3 // 4 * tile
+    return [(0, cut), (cut, units)]
 
 
 def body(
@@ -450,101 +1036,207 @@
     seg_ids = segments[0]
     length = tokens.shape[0]
     devices = lax.axis_size("dp")
-    index = lax.axis_index("dp")
-    chip, core = index // 2, index % 2
-    core_swap = [(i, i ^ 1) for i in range(devices)]
+    ring = Ring(devices)
     rows, _, local_width = attn_weight.shape
     head_count = beta_weight.shape[1]
     piece = conv_weight.shape[3]
     units = mlp_weight.shape[2]
+    width = rows * devices
     groups = head_count // HEADS_PER_STEP
     wide = local_width // groups
-    model_width = rows * devices
+    qkv = 3 * local_width
     taps_size = conv_weight.size
-
+    chunks = unit_chunks(units)
+
+    attn_local = pack_mixer(attn_weight, wide)
     small = jnp.concatenate(
         [norm_gain, mlp_gain, beta_weight.reshape(-1), conv_weight.reshape(-1), out_gain]
     ).astype(BF16)
-    small = lax.all_gather(small, "dp", axis=0)
-    attn_low = attn_weight.astype(BF16)
-    qkv_local = attn_low[:, :3].reshape(rows, 3, groups, wide).transpose(0, 2, 1, 3)
-    attn_local = jnp.concatenate([qkv_local.reshape(rows, 3 * local_width), attn_low[:, 3]], axis=1)
-    attn_mat = lax.all_gather(attn_local, "dp", axis=0, tiled=True)
-    mlp_local = mlp_weight.astype(BF16).reshape(rows, 3 * units)
-    mlp_mat = lax.all_gather(mlp_local, "dp", axis=0, tiled=True)
-    qkv_mat, out_mat = attn_mat[:, : 3 * local_width], attn_mat[:, 3 * local_width :]
-    gu_mat, down_mat = mlp_mat[:, : 2 * units], mlp_mat[:, 2 * units :]
+    small = jnp.broadcast_to(small, (devices,) + small.shape)
+    mlp_low = mlp_weight.astype(BF16)
+    mlp_local = [
+        Box(mlp_low[:, :, low:high].reshape(rows, 3 * (high - low))) for low, high in chunks
+    ]
+
+    in_ring = rows % 128 == 0
+    if in_ring:
+        attn = Gather(ring, attn_local)
+        attn.advance(0)
+    small = Box(lax.all_to_all(small, "dp", 0, 0, tiled=True))
+    if in_ring:
+        sync(*attn.boxes())
+        attn.advance(1)
     at = [0, rows, 2 * rows, 2 * rows + rows * head_count]
+    small = small.value
     gain_in = small[:, at[0] : at[1]].reshape(-1).astype(F32)
     gain_mid = small[:, at[1] : at[2]].reshape(-1).astype(F32)
-    beta_mat = small[:, at[2] : at[3]].reshape(model_width, head_count)
-    beta_pad = jnp.pad(beta_mat, ((0, 0), (0, 128 - head_count)))
+    beta_mat = small[:, at[2] : at[3]].reshape(width, head_count)
+    beta_pad = Box(jnp.pad(beta_mat, ((0, 0), (0, 128 - head_count))))
     taps = small[:, at[3] : at[3] + taps_size].reshape(devices, 3, 4, head_count, piece)
-    taps = taps.transpose(1, 2, 3, 0, 4).reshape(3, 4, local_width).astype(F32)
-    gain_heads = small[:, at[3] + taps_size :].reshape(1, -1).astype(F32)
-
+    taps = Box(taps.transpose(1, 2, 3, 0, 4).reshape(3, 4, local_width).astype(F32))
+    gain_heads = Box(small[:, at[3] + taps_size :].reshape(1, -1).astype(F32))
     inputs_f = tokens.astype(F32)
     scale_in = lax.rsqrt(jnp.mean(inputs_f * inputs_f, axis=-1, keepdims=True) + 1e-05)
-    normed = (inputs_f * scale_in * gain_in).astype(BF16)
-    projected = matmul(normed, qkv_mat, NN)
-    logits = matmul(normed, beta_pad, NN)
+    normed = Box((inputs_f * scale_in * gain_in).astype(BF16))
+    logits = Box(matmul(normed.value, beta_pad.value, NN))
+    if in_ring:
+        sync(*attn.boxes(), normed, logits, taps, gain_heads, beta_pad)
+        attn.advance(2)
+        sync(*attn.boxes(), normed, *mlp_local)
+        attn.advance(3)
+        sync(*attn.boxes(), normed, mlp_local[1])
+        attn.swap()
+        attn_blocks = attn.ordered()
+        table = ring.table
+    else:
+        attn_blocks = even_blocks(lax.all_gather(attn_local, "dp", axis=0, tiled=True))
+        table = jnp.arange(width // 128, dtype=jnp.int32)
+    mats = [lax.all_gather(mlp_local[0].value, "dp", axis=0, tiled=True)]
+
+    projected = Box(times_rows(normed.value, attn_blocks, table, 0, qkv, 512, F32))
+    sync(projected, mlp_local[1])
+    mats.append(lax.all_gather(mlp_local[1].value, "dp", axis=0, tiled=True))
     mixed, *saved = mixer_forward(
-        projected, logits, taps, gain_heads, seg_ids, HEADS_PER_STEP, PASSES
-    )
-    hidden = inputs_f + pair_sum(matmul(mixed, out_mat, NT))
-
+        projected.value,
+        logits.value,
+        taps.value,
+        gain_heads.value,
+        seg_ids,
+        HEADS_PER_STEP,
+        PASSES,
+        0,
+        groups,
+    )
+    part = times_turned([([mixed], attn_blocks, qkv)], table)
+    hidden = inputs_f + part.astype(F32) + swap_tensor(part).astype(F32)
     scale_mid = lax.rsqrt(jnp.mean(hidden * hidden, axis=-1, keepdims=True) + 1e-05)
     normed_mlp = (hidden * scale_mid * gain_mid).astype(BF16)
-    gate = matmul(normed_mlp, gu_mat[:, :units], NN)
-    up = matmul(normed_mlp, gu_mat[:, units:], NN)
-    gate_sig = jax.nn.sigmoid(gate)
-    activated = (gate * gate_sig * up).astype(BF16)
-    grad_act = matmul(cotangent, down_mat, NN)
-    grad_gate = (grad_act * up * gate_sig * (1.0 + gate * (1.0 - gate_sig))).astype(BF16)
-    grad_up = (grad_act * gate * gate_sig).astype(BF16)
-    grad_gu = jnp.concatenate([grad_gate, grad_up], axis=1)
-    down = pair_sum(matmul(activated, down_mat, NT))
-    result = (hidden + down).astype(BF16)
-
-    mlp_own, mlp_other = pair_split(normed_mlp, rows, core)
-    cot_own, cot_other = pair_split(cotangent, rows, core)
-    grad_gu_mat = scatter_grads(
-        matmul(mlp_own, grad_gu, TN, BF16), matmul(mlp_other, grad_gu, TN, BF16), chip, core_swap
-    )
-    grad_down_mat = scatter_grads(
-        matmul(cot_own, activated, TN, BF16), matmul(cot_other, activated, TN, BF16), chip, core_swap
-    )
-    mlp_grad = jnp.concatenate([grad_gu_mat, grad_down_mat], axis=1).reshape(rows, 3, units)
-    grad_normed_mlp = pair_sum(matmul(grad_gu, gu_mat, NT))
-    grad_norm, grad_gain_mid = norm_back(hidden, scale_mid, gain_mid, grad_normed_mlp)
+
+    def mlp_grads(which):
+        act = acts[which].value
+        size = act.shape[2]
+        pairs = [(normed_mlp, act, 0, 2), (cotangent, act, 2, 1)]
+        tile = size // 2 if size % 512 == 0 else size
+
+        def grads(half, plus):
+            return weight_grads(pairs, tile, rows, ring.cores, half, plus)
+
+        return grads
+
+    acts = [Box(gated_units(normed_mlp, cotangent, mats[0], table, 256))]
+    sync(*acts)
+    sums = [Scatter(ring, mlp_grads(0))]
+    sync(*acts, *sums[0].boxes())
+    sums[0].swap()
+    act = acts[0].value
+    part = Box(units_turned([(act, p, mats[0]) for p in range(2)], 256, F32, table))
+    sync(part, *acts, *sums[0].boxes())
+    sums[0].join()
+    sync(part, *acts, *sums[0].boxes())
+    sums[0].advance(0)
+    acts.append(Box(gated_units(normed_mlp, cotangent, mats[1], table, 256)))
+    sync(part, *acts, *sums[0].boxes())
+    sums[0].advance(1)
+    act = acts[1].value
+    part = Box(units_turned([(act, p, mats[1]) for p in range(2)], 256, BF16, table, plus=part.value))
+    sync(part, *acts, *sums[0].boxes())
+    exchange = Exchange(part.value, 3)
+    sums[0].advance(2)
+    sums.append(Scatter(ring, mlp_grads(1)))
+    sync(exchange.advance(), *acts, *sums[0].boxes(), *sums[1].boxes())
+    sums[0].advance(3)
+    sums[1].swap()
+    down = Box(units_turned([(a.value, 2, mat) for a, mat in zip(acts, mats)], 256, BF16, table))
+    sync(exchange.advance(), down, *acts, *sums[0].boxes(), *sums[1].boxes())
+    sums[1].join()
+    sync(*sums[1].boxes())
+    sums[1].advance(0)
+    sync(exchange.advance(), *sums[1].boxes())
+    sums[1].advance(1)
+
+    grad_norm, grad_gain_mid = norm_back(hidden, scale_mid, gain_mid, exchange.result())
     grad_hidden = cotangent.astype(F32) + grad_norm
     grad_hidden_low = grad_hidden.astype(BF16)
-
-    grad_mixed = matmul(grad_hidden_low, out_mat, NN)
-    grad_proj, grad_logits, grad_taps, grad_gain_heads = mixer_backward(
-        projected, logits, taps, gain_heads, seg_ids, saved, grad_mixed, HEADS_PER_STEP, PASSES
-    )
-    grad_logits_low = grad_logits.astype(BF16)
-    hid_own, hid_other = pair_split(grad_hidden_low, rows, core)
-    in_own, in_other = pair_split(normed, rows, core)
-    grad_out_mat = scatter_grads(
-        matmul(hid_own, mixed, TN, BF16), matmul(hid_other, mixed, TN, BF16), chip, core_swap
-    )
-    grad_qkv_mat = scatter_grads(
-        matmul(in_own, grad_proj, TN, BF16), matmul(in_other, grad_proj, TN, BF16), chip, core_swap
-    )
-    grad_qkv_mat = grad_qkv_mat.reshape(rows, groups, 3, wide).transpose(0, 2, 1, 3)
-    attn_grad = jnp.concatenate(
-        [grad_qkv_mat.reshape(rows, 3, local_width), grad_out_mat[:, None]], axis=1
-    )
-    grad_beta = matmul(normed, grad_logits_low, TN)[:, :head_count]
-    grad_normed = pair_sum(
-        matmul(grad_proj, qkv_mat, NT) + matmul(grad_logits_low, beta_pad, NT)
-    )
+    grad_mixed = Box(
+        times_rows(grad_hidden_low, attn_blocks, table, qkv, local_width, 512, F32)
+    )
+    sync(*sums[1].boxes(), grad_mixed, down)
+    sums[1].advance(2)
+    down = Exchange(down.value, 3)
+
+    def mixer_grads(first, count):
+        made = mixer_backward(
+            projected.value,
+            logits.value,
+            taps.value,
+            gain_heads.value,
+            seg_ids,
+            saved,
+            grad_mixed.value,
+            HEADS_PER_STEP,
+            PASSES,
+            first,
+            count,
+            0,
+        )
+        return [Box(m) for m in made]
+
+    half = groups // 2
+    back = [mixer_grads(0, half)]
+    sync(down.advance(), *sums[1].boxes(), back[0][0], grad_mixed)
+    sums[1].advance(3)
+
+    def early_grads(which, plus):
+        pairs = [(normed.value, back[0][0].value, 0, 1), (grad_hidden_low, mixed, 0, 1)]
+        return weight_grads(pairs, 512, rows, ring.cores, which, plus)
+
+    first = Scatter(ring, early_grads)
+    sync(*sums[1].boxes(), *first.boxes(), grad_mixed)
+    first.swap()
+    back.append(mixer_grads(half, half // 2))
+    sync(down.advance(), back[1][0], grad_mixed, *first.boxes())
+    first.join()
+    sync(grad_mixed, *first.boxes())
+    first.advance(0)
+    back.append(mixer_grads(half + half // 2, half - half // 2))
+    sync(down.advance(), back[2][0], *first.boxes())
+    first.advance(1)
+    grad_logits_low = sum(b[1].value for b in back).astype(BF16)
+    lefts = [b[0].value for b in back]
+    part = Box(times_turned([(lefts, attn_blocks, 0)], table, extra=(grad_logits_low, beta_pad.value)))
+    sync(part, back[1][0], back[2][0], *first.boxes())
+    exchange = Exchange(part.value, 3)
+    first.advance(2)
+
+    def late_grads(which, plus):
+        pairs = [(normed.value, b[0].value, 0, 1) for b in back[1:]]
+        return weight_grads(pairs, back[1][0].value.shape[1], rows, ring.cores, which, plus)
+
+    second = Scatter(ring, late_grads)
+    sync(exchange.advance(), back[1][0], back[2][0], *first.boxes(), *second.boxes())
+    first.advance(3)
+    second.swap()
+    grad_beta = Box(matmul(normed.value, grad_logits_low, TN)[:, :head_count])
+    mlp_grad = Box(units_result([s.parts() for s in sums], ring.around))
+    sync(exchange.advance(), grad_beta, mlp_grad, *first.boxes(), *second.boxes())
+    second.join()
+    second.advance(0)
+    result = Box((hidden + down.result()).astype(BF16))
+    sync(exchange.advance(), result, *first.boxes(), *second.boxes())
+    second.advance(1)
+    grad_normed = exchange.result()
+    grad_beta = grad_beta.value
+    sync(*second.boxes())
+    second.advance(2)
+    sync(*second.boxes())
+    second.advance(3)
+
     grad_first, grad_gain_in = norm_back(inputs_f, scale_in, gain_in, grad_normed)
     grad_inputs = grad_hidden + grad_first
 
-    grad_gain_heads = grad_gain_heads[0] + swap_tensor(grad_gain_heads[0])
+    grad_gain_heads = sum(b[3].value[0] for b in back)
+    grad_gain_heads = grad_gain_heads + swap_tensor(grad_gain_heads)
+    grad_taps = jnp.concatenate([b[2].value for b in back], axis=2)
     grad_taps = grad_taps.reshape(3, 4, head_count, devices, piece).transpose(3, 0, 1, 2, 4)
     packed = jnp.concatenate(
         [
@@ -557,8 +1249,9 @@
         axis=1,
     )
     packed = jnp.sum(lax.all_to_all(packed, "dp", 0, 0, tiled=True), axis=0)
+    attn_grad = mixer_result([first.parts(), second.parts()], wide, local_width, ring.around)
     return (
-        result,
+        result.value,
         grad_inputs,
         packed[at[0] : at[1]],
         attn_grad,
@@ -566,7 +1259,7 @@
         packed[at[3] : at[3] + taps_size].reshape(conv_weight.shape),
         packed[at[3] + taps_size :],
         packed[at[1] : at[2]],
-        mlp_grad,
+        mlp_grad.value.transpose(1, 0, 2),
     )
 
 

time: 974 us -> 773 us (0.79)
  Pallas kernels: 82.2 us -> 328 us
  matrix products: 156 us -> 2.46 us
  waiting for transfers between devices: 374 us -> 221 us
  local copies, waits for them, and re-layouts: 136 us -> 78.8 us
  other arithmetic: 87 us -> 48.5 us
  blocking collectives: 24.4 us -> 0 us
  between operations: 36.1 us -> 15.6 us
    pallas_call x2 -> x40, Pallas kernels: 82.2 us -> 328 us  [the longest x35 240 us: call(): pl.pallas_call(kernel, grid_spec=pltpu.PrefetchScalarGridSpec(num_scalar_...]
    dot_general x19 -> x2, matrix products: 155 us -> 2.46 us  [matmul(): return lax.dot_general(left, right, dims, preferred_element_type=F32)]
    all_gather x2, waiting for transfers between devices: 152 us -> 0.01 us  [the longest x1 0.01 us: body(): mats = [lax.all_gather(mlp_local[0].value, 'dp', axis=0, tiled=True)]]
    convert_element_type x60 -> x5, other arithmetic: 47 us -> 7.38 us  [the longest x1 5.14 us: body(): result = Box((hidden + down.result()).astype(BF16))]
    ppermute x60 -> x53, waiting for transfers between devices: 175 us -> 147 us  [the longest x40 144 us: send(): return Box(lax.ppermute(value, 'dp', self.hops[turn]))]
    all_gather x1 -> x0, blocking collectives: 24.4 us -> none  [body(): small = lax.all_gather(small, 'dp', axis=0)]
    slice x10 -> x11, local copies, waits for them, and re-layouts: 35.2 us -> 13.5 us  [the longest x6 8.52 us: advance(): self.part[self.cuts[at]:self.cuts[at + 1]]]
    dynamic_slice x5 -> x1, local copies, waits for them, and re-layouts: 20.3 us -> 0.58 us  [__init__(): here = jnp.asarray(place, jnp.int32)[chip]]
  transfers between devices with their start and end apart: 68 -> 68, of which waited for: 39 -> 32; matrix products, arithmetic and copies ran while one was open for 31% -> 13% of each run, Pallas kernels for 8% -> 39%
where the time goes in v3:
time: 773 us; the launch traced here: 762 us
  Pallas kernels  328 us (42%)
  waiting for transfers between devices  221 us (29%)
  local copies, waits for them, and re-layouts  78.8 us (10%)
  starting transfers between devices  68.1 us (9%)
  other arithmetic  48.5 us (6%)
  between operations  15.6 us (2%)
    pallas_call x35, Pallas kernels, call(): pl.pallas_call(kernel, grid_spec=pltpu.PrefetchScalarGridSpec(num_scalar_...  240 us
    ppermute x40, waiting for transfers between devices, send(): return Box(lax.ppermute(value, 'dp', self.hops[turn]))  144 us
    ppermute x11, waiting for transfers between devices, swap_tensor(): return lax.ppermute(value, 'tensor', [(0, 1), (1, 0)])  61.7 us
    pallas_call x3, Pallas kernels, mixer_backward(): pl.pallas_call(functools.partial(backward_kernel, heads, passes, first),...  53.1 us
    ppermute x40, starting transfers between devices, send(): return Box(lax.ppermute(value, 'dp', self.hops[turn]))  43.1 us
    unnamed x194, local copies, waits for them, and re-layouts  37.3 us
    pallas_call x1, Pallas kernels, mixer_forward(): pl.pallas_call(functools.partial(forward_kernel, heads, passes, first), g...  29.7 us
  transfers between devices with their start and end apart: 68, of which 32 were waited for; matrix products, arithmetic and copies ran while one was open for 13% of the time, Pallas kernels for 39%

profile of v3, /device:TPU:0, one launch (start us, length us, event | category | flops | bytes accessed | tf_op | source)
XLA Modules:
  0.0 762.5 jit_solution(16069898653353883108)
XLA Ops:
  7.2 4.7 pack_mixer.1.refs_0_.refs_1_.refs_3_
  22.0 6.5 all-to-all-start
  29.6 13.0 %all-to-all-done = bf16[16,2,1028]{2,1,0:T(2,128)(2,1)S(1)} async-done(((bf16[16,2,1028]{2,1,0:T(2,128)(2,1)}), bf16[16,2,1028]{2,1,0:T(2,128)(2,1)S(1)}, u32[]{:S(2)}, u32[]{:S(2)}) %all-to-all-start) | async-done | bytes 65824 | tf_op jit(solution)/shard_map/all_to_all | solution.py:1065
  51.3 19.6 %collective-permute-done.3.refs_6_.refs_7_.refs_9_ = bf16[128,4096]{1,0:T(8,128)(2,1)} collective-permute-done((bf16[128,4096]{1,0:T(8,128)(2,1)}, bf16[128,4096]{1,0:T(8,128)(2,1)}, u32[]{:S(2)}, u32[]{:S(2)}) %collective-permute-start.3) | collective-permute-done | bytes 1048608 | tf_op jit(solution)/shard_map/ppermute | solution.py:895
  81.5 15.2 %collective-permute-done.7.refs_5_.refs_6_.refs_8_ = bf16[128,4096]{1,0:T(8,128)(2,1)} collective-permute-done((bf16[128,4096]{1,0:T(8,128)(2,1)}, bf16[128,4096]{1,0:T(8,128)(2,1)}, u32[]{:S(2)}, u32[]{:S(2)}) %collective-permute-start.7) | collective-permute-done | bytes 1048608 | tf_op jit(solution)/shard_map/ppermute | solution.py:895
  108.1 20.3 %collective-permute-done.11 = bf16[128,2048]{1,0:T(8,128)(2,1)} collective-permute-done((bf16[128,2048]{1,0:T(8,128)(2,1)}, bf16[128,2048]{1,0:T(8,128)(2,1)}, u32[]{:S(2)}, u32[]{:S(2)}) %collective-permute-start.11) | collective-permute-done | bytes 524320 | tf_op jit(solution)/shard_map/ppermute | solution.py:895
  136.1 14.0 %times_rows.2.proj_ref = f32[512,3072]{1,0:T(8,128)} custom-call(s32[16]{0:T(128)S(1)} %pad_add_fusion.table_ref, bf16[512,2048]{1,0:T(8,128)(2,1)} %copy-done.4, bf16[128,4096]{1,0:T(8,128)(2,1)S(1)} %copy-done.13, bf16[128,4096]{1,0:T(8,128)(2,1)S(1)} %copy-done.25, bf16[128,4096]{1,0:T(8,128)(2,1)} %collective-permute-done.4.refs_2_.refs_3_.refs_5_, ...), custom_call_target="tpu_custom_call" | custom-call | flops 1000 | bytes 1000 | tf_op jit(solution)/shard_map/times_rows/pallas_call | solution.py:380
  153.5 29.7 %mixer_forward.1 = (bf16[512,1024]{1,0:T(8,128)(2,1)S(1)}, f32[512,1024]{1,0:T(8,128)S(1)}, f32[512,1024]{1,0:T(8,128)S(1)}, f32[512,1024]{1,0:T(8,128)}, f32[512,1024]{1,0:T(8,128)}) custom-call(f32[512,3072]{1,0:T(8,128)} %times_rows.2.proj_ref, f32[512,128]{1,0:T(8,128)S(1)} %copy-done.35, f32[3,4,1024]{2,1,0:T(4,128)S(1)} %reshape.211.conv_ref, ...), custom_call_target="tpu_custom_call" | custom-call | flops 1000 | bytes 1000 | tf_op jit(solution)/shard_map/mixer_forward/pallas_call | solution.py:330
  185.9 8.3 %times_turned.2 = bf16[512,2048]{1,0:T(8,128)(2,1)} custom-call(s32[16]{0:T(128)S(1)} %pad_add_fusion.table_ref, bf16[512,1024]{1,0:T(8,128)(2,1)S(1)} %get-tuple-element.209.refs_0_.refs_3_, bf16[128,4096]{1,0:T(8,128)(2,1)S(1)} %copy-done.13, bf16[128,4096]{1,0:T(8,128)(2,1)S(1)} %copy-done.26, ...), custom_call_target="tpu_custom_call" | custom-call | flops 1000 | bytes 1000 | tf_op jit(solution)/shard_map/times_turned/pallas_call | solution.py:380
  195.9 46.4 %collective-permute-done.17 = bf16[512,2048]{1,0:T(8,128)(2,1)S(1)} collective-permute-done((bf16[512,2048]{1,0:T(8,128)(2,1)}, bf16[512,2048]{1,0:T(8,128)(2,1)S(1)}, u32[]{:S(2)}, u32[]{:S(2)}) %collective-permute-start.17) | collective-permute-done | bytes 2097184 | tf_op jit(solution)/shard_map/ppermute | solution.py:1000
  242.3 5.2 multiply_reduce_fusion.2
  247.5 4.4 multiply_convert_fusion.normed_ref.refs_0_
  253.5 19.3 %gated_units.2.refs_2_.refs_3_.refs_0_.refs_1_ = bf16[3,512,2048]{2,1,0:T(8,128)(2,1)} custom-call(s32[16]{0:T(128)S(1)} %pad_add_fusion.table_ref, bf16[512,2048]{1,0:T(8,128)(2,1)S(1)} %copy-done.9, bf16[512,2048]{1,0:T(8,128)(2,1)S(1)} %copy-done.8, bf16[2048,6144]{1,0:T(8,128)(2,1)} %all-gather.3.cloned.1.call-done.gate_ref.up_ref.down_ref.refs_2_.refs_3_, ...), custom_call_target="tpu_custom_call" | custom-call | flops 1000 | bytes 1000 | tf_op jit(solution)/shard_map/gated_units/pallas_call | solution.py:380
  272.9 13.5 %weight_grads.8 = bf16[8,128,6144]{2,1,0:T(8,128)(2,1)} custom-call(s32[2]{0:T(128)S(1)} %pad_add_fusion.1.table_ref, bf16[512,2048]{1,0:T(8,128)(2,1)S(1)} %copy-done.9, bf16[512,2048]{1,0:T(8,128)(2,1)S(1)} %copy-done.8, bf16[3,512,2048]{2,1,0:T(8,128)(2,1)} %gated_units.2.refs_2_.refs_3_.refs_0_.refs_1_, ...), custom_call_target="tpu_custom_call" | custom-call | flops 1000 | bytes 1000 | tf_op jit(solution)/shard_map/weight_grads/pallas_call | solution.py:380
  286.3 15.0 %units_turned.3.refs_4_ = f32[512,2048]{1,0:T(8,128)S(1)} custom-call(s32[16]{0:T(128)S(1)} %pad_add_fusion.table_ref, bf16[3,512,2048]{2,1,0:T(8,128)(2,1)} %gated_units.2.refs_2_.refs_3_.refs_0_.refs_1_, bf16[3,512,2048]{2,1,0:T(8,128)(2,1)} %gated_units.2.refs_2_.refs_3_.refs_0_.refs_1_, ...), custom_call_target="tpu_custom_call" | custom-call | flops 1000 | bytes 1000 | tf_op jit(solution)/shard_map/units_turned/pallas_call | solution.py:380
  305.8 16.0 %weight_grads.9.refs_0_.refs_1_ = bf16[8,128,6144]{2,1,0:T(8,128)(2,1)} custom-call(s32[2]{0:T(128)S(1)} %pad_add_fusion.1.table_ref, bf16[512,2048]{1,0:T(8,128)(2,1)S(1)} %copy-done.10, bf16[512,2048]{1,0:T(8,128)(2,1)S(1)} %copy-done.8, bf16[3,512,2048]{2,1,0:T(8,128)(2,1)} %gated_units.2.refs_2_.refs_3_.refs_0_.refs_1_, ...), custom_call_target="tpu_custom_call" | custom-call | flops 1000 | bytes 1000 | tf_op jit(solution)/shard_map/weight_grads/pallas_call | solution.py:380
  328.4 9.3 %gated_units.3.refs_0_.refs_1_.refs_2_.refs_3_ = bf16[3,512,768]{2,1,0:T(8,128)(2,1)} custom-call(s32[16]{0:T(128)S(1)} %pad_add_fusion.table_ref, bf16[512,2048]{1,0:T(8,128)(2,1)S(1)} %copy-done.11, bf16[512,2048]{1,0:T(8,128)(2,1)S(1)} %copy-done.8, bf16[2048,2304]{1,0:T(8,128)(2,1)} %all-gather.5.cloned.1.call-done.gate_ref.up_ref.down_ref.refs_2_.refs_3_, ...), custom_call_target="tpu_custom_call" | custom-call | flops 1000 | bytes 1000 | tf_op jit(solution)/shard_map/gated_units/pallas_call | solution.py:380
  337.7 7.1 collective-permute-done.19.refs_2_
  345.7 4.1 ring_hop.17
  351.9 9.2 %units_turned.4 = bf16[512,2048]{1,0:T(8,128)(2,1)S(1)} custom-call(s32[16]{0:T(128)S(1)} %pad_add_fusion.table_ref, bf16[3,512,768]{2,1,0:T(8,128)(2,1)S(1)} %copy-done.6, bf16[3,512,768]{2,1,0:T(8,128)(2,1)S(1)} %copy-done.6, bf16[2048,2304]{1,0:T(8,128)(2,1)} %all-gather.5.cloned.1.call-done.gate_ref.up_ref.down_ref.refs_2_.refs_3_, ...), custom_call_target="tpu_custom_call" | custom-call | flops 1000 | bytes 1000 | tf_op jit(solution)/shard_map/units_turned/pallas_call | solution.py:380
  361.0 24.2 %collective-permute-done.21.refs_2_ = bf16[128,6144]{1,0:T(8,128)(2,1)S(1)} collective-permute-done((bf16[128,6144]{1,0:T(8,128)(2,1)S(1)}, bf16[128,6144]{1,0:T(8,128)(2,1)S(1)}, u32[]{:S(2)}, u32[]{:S(2)}) %collective-permute-start.21) | collective-permute-done | bytes 1572896 | tf_op jit(solution)/shard_map/ppermute | solution.py:895
  385.7 4.8 ring_hop.18
  395.0 7.3 weight_grads.10
  402.3 5.3 collective-permute-done.25
  407.6 17.4 %collective-permute-done.26.refs_2_ = bf16[128,6144]{1,0:T(8,128)(2,1)S(1)} collective-permute-done((bf16[128,6144]{1,0:T(8,128)(2,1)}, bf16[128,6144]{1,0:T(8,128)(2,1)S(1)}, u32[]{:S(2)}, u32[]{:S(2)}) %collective-permute-start.26) | collective-permute-done | bytes 1572896 | tf_op jit(solution)/shard_map/ppermute | solution.py:895
  426.8 4.8 ring_hop.19
  437.9 11.6 %units_turned.5 = bf16[512,2048]{1,0:T(8,128)(2,1)S(1)} custom-call(s32[16]{0:T(128)S(1)} %pad_add_fusion.table_ref, bf16[3,512,2048]{2,1,0:T(8,128)(2,1)} %gated_units.2.refs_2_.refs_3_.refs_0_.refs_1_, bf16[3,512,768]{2,1,0:T(8,128)(2,1)S(1)} %copy-done.7, bf16[2048,6144]{1,0:T(8,128)(2,1)} %all-gather.3.cloned.1.call-done.gate_ref.up_ref.down_ref.refs_2_.refs_3_, ...), custom_call_target="tpu_custom_call" | custom-call | flops 1000 | bytes 1000 | tf_op jit(solution)/shard_map/units_turned/pallas_call | solution.py:380
  452.7 16.0 %collective-permute-done.28.refs_1_ = bf16[128,6144]{1,0:T(8,128)(2,1)S(1)} collective-permute-done((bf16[128,6144]{1,0:T(8,128)(2,1)}, bf16[128,6144]{1,0:T(8,128)(2,1)S(1)}, u32[]{:S(2)}, u32[]{:S(2)}) %collective-permute-start.28) | collective-permute-done | bytes 1572896 | tf_op jit(solution)/shard_map/ppermute | solution.py:895
  469.9 8.3 %weight_grads.11.refs_0_.refs_1_.refs_3_ = bf16[8,128,2304]{2,1,0:T(8,128)(2,1)} custom-call(s32[2]{0:T(128)S(1)} %pad_add_fusion.1.table_ref, bf16[512,2048]{1,0:T(8,128)(2,1)S(1)} %copy-done.12, bf16[512,2048]{1,0:T(8,128)(2,1)S(1)} %copy-done.8, bf16[3,512,768]{2,1,0:T(8,128)(2,1)} %gated_units.3.refs_0_.refs_1_.refs_2_.refs_3_, ...), custom_call_target="tpu_custom_call" | custom-call | flops 1000 | bytes 1000 | tf_op jit(solution)/shard_map/weight_grads/pallas_call | solution.py:380
  483.5 5.4 collective-permute-done.31.refs_2_
  496.0 4.9 multiply_reduce_fusion
  500.8 7.1 fusion.20
  508.0 7.6 times_rows.3.gmix_ref
  523.3 26.5 %mixer_backward.3 = (bf16[512,1536]{1,0:T(8,128)(2,1)S(1)}, f32[512,128]{1,0:T(8,128)S(1)}, f32[3,4,512]{2,1,0:T(4,128)S(1)}, f32[1,128]{1,0:T(1,128)S(1)}) custom-call(f32[512,3072]{1,0:T(8,128)} %times_rows.2.proj_ref, f32[512,128]{1,0:T(8,128)S(1)} %copy-done.36, f32[3,4,1024]{2,1,0:T(4,128)S(1)} %reshape.211.conv_ref, f32[1,128]{1,0:T(1,128)S(1)} %reshape.212.gain_ref, ...), custom_call_target="tpu_custom_call" | custom-call | flops 1000 | bytes 1000 | tf_op jit(solution)/shard_map/mixer_backward/pallas_call | solution.py:349
  558.4 8.5 %weight_grads.12 = bf16[8,128,2560]{2,1,0:T(8,128)(2,1)} custom-call(s32[2]{0:T(128)S(1)} %pad_add_fusion.1.table_ref, bf16[512,2048]{1,0:T(8,128)(2,1)S(1)} %copy-done.5, bf16[512,2048]{1,0:T(8,128)(2,1)} %get-tuple-element.399.left_ref.refs_1_, bf16[512,1536]{1,0:T(8,128)(2,1)S(1)} %copy-done.30, bf16[512,1024]{1,0:T(8,128)(2,1)S(1)} %copy-done.32), custom_call_target="tpu_custom_call" | custom-call | flops 1000 | bytes 1000 | tf_op jit(solution)/shard_map/weight_grads/pallas_call | solution.py:380
  571.4 13.3 %mixer_backward.4 = (bf16[512,768]{1,0:T(8,128)(2,1)S(1)}, f32[512,128]{1,0:T(8,128)S(1)}, f32[3,4,256]{2,1,0:T(4,128)S(1)}, f32[1,128]{1,0:T(1,128)S(1)}) custom-call(f32[512,3072]{1,0:T(8,128)} %times_rows.2.proj_ref, f32[512,128]{1,0:T(8,128)S(1)} %copy-done.36, f32[3,4,1024]{2,1,0:T(4,128)S(1)} %reshape.211.conv_ref, f32[1,128]{1,0:T(1,128)S(1)} %reshape.212.gain_ref, ...), custom_call_target="tpu_custom_call" | custom-call | flops 1000 | bytes 1000 | tf_op jit(solution)/shard_map/mixer_backward/pallas_call | solution.py:349
  585.7 9.6 %weight_grads.13.refs_0_.refs_1_ = bf16[8,128,2560]{2,1,0:T(8,128)(2,1)} custom-call(s32[2]{0:T(128)S(1)} %pad_add_fusion.1.table_ref, bf16[512,2048]{1,0:T(8,128)(2,1)S(1)} %copy-done.5, bf16[512,2048]{1,0:T(8,128)(2,1)} %get-tuple-element.399.left_ref.refs_1_, bf16[512,1536]{1,0:T(8,128)(2,1)S(1)} %copy-done.30, bf16[512,1024]{1,0:T(8,128)(2,1)S(1)} %copy-done.32, ...), custom_call_target="tpu_custom_call" | custom-call | flops 1000 | bytes 1000 | tf_op jit(solution)/shard_map/weight_grads/pallas_call | solution.py:380
  600.7 13.3 %mixer_backward.5 = (bf16[512,768]{1,0:T(8,128)(2,1)S(1)}, f32[512,128]{1,0:T(8,128)S(1)}, f32[3,4,256]{2,1,0:T(4,128)S(1)}, f32[1,128]{1,0:T(1,128)S(1)}) custom-call(f32[512,3072]{1,0:T(8,128)} %times_rows.2.proj_ref, f32[512,128]{1,0:T(8,128)S(1)} %copy-done.36, f32[3,4,1024]{2,1,0:T(4,128)S(1)} %reshape.211.conv_ref, f32[1,128]{1,0:T(1,128)S(1)} %reshape.212.gain_ref, ...), custom_call_target="tpu_custom_call" | custom-call | flops 1000 | bytes 1000 | tf_op jit(solution)/shard_map/mixer_backward/pallas_call | solution.py:349
  619.5 13.5 %times_turned.3 = bf16[512,2048]{1,0:T(8,128)(2,1)} custom-call(s32[16]{0:T(128)S(1)} %pad_add_fusion.table_ref, bf16[512,1536]{1,0:T(8,128)(2,1)} %copy-done.29, bf16[512,768]{1,0:T(8,128)(2,1)S(1)} %get-tuple-element.324.refs_1_.refs_2_, bf16[512,768]{1,0:T(8,128)(2,1)S(1)} %get-tuple-element.325.refs_2_.refs_3_, bf16[128,4096]{1,0:T(8,128)(2,1)S(1)} %copy-done.14, ...), custom_call_target="tpu_custom_call" | custom-call | flops 1000 | bytes 1000 | tf_op jit(solution)/shard_map/times_turned/pallas_call | solution.py:380
  642.3 4.4 weight_grads.14
  646.8 4.4 collective-permute-done.49
  656.5 4.1 ring_hop.27
  663.4 4.9 units_result.1
  683.7 5.8 weight_grads.15.refs_0_.refs_1_.refs_3_
  695.6 5.1 add_convert_fusion
  722.8 4.2 all-to-all-start.1
  735.4 6.4 fusion.8
  750.4 4.8 mixer_result.1
  (402 shorter events, 212.5 us)
Async XLA Ops:
  11.9 33.4 %collective-permute-start = (bf16[128,4096]{1,0:T(8,128)(2,1)}, bf16[128,4096]{1,0:T(8,128)(2,1)}, u32[]{:S(2)}, u32[]{:S(2)}) collective-permute-start(bf16[128,4096]{1,0:T(8,128)(2,1)} %pack_mixer.1.refs_0_.refs_1_.refs_3_), channel_id=1, source_target_pairs={{0,8},{2,10},{8,16},{10,18},{16,24},{18,26},{24,28},{26,30},{28,20... | collective-permute-start | bytes 3145736 | tf_op jit(solution)/shard_map/ppermute | solution.py:895
  14.9 30.4 %collective-permute-start.1 = (bf16[128,4096]{1,0:T(8,128)(2,1)}, bf16[128,4096]{1,0:T(8,128)(2,1)S(1)}, u32[]{:S(2)}, u32[]{:S(2)}) collective-permute-start(bf16[128,4096]{1,0:T(8,128)(2,1)} %pack_mixer.1.refs_0_.refs_1_.refs_3_), channel_id=1, source_target_pairs={{0,4},{2,6},{8,0},{10,2},{16,8},{18,10},{24,16},{26,18},{28,24},{3... | collective-permute-start | bytes 3145736 | tf_op jit(solution)/shard_map/ppermute | solution.py:895
  14.9 30.4 %collective-permute-start.2 = (bf16[128,4096]{1,0:T(8,128)(2,1)}, bf16[128,4096]{1,0:T(8,128)(2,1)}, u32[]{:S(2)}, u32[]{:S(2)}) collective-permute-start(bf16[128,4096]{1,0:T(8,128)(2,1)} %pack_mixer.1.refs_0_.refs_1_.refs_3_), channel_id=1, source_target_pairs={{0,2},{2,0},{4,6},{6,4},{8,10},{10,8},{12,14},{14,12},{16,18},{18,... | collective-permute-start | bytes 3145736 | tf_op jit(solution)/shard_map/ppermute | solution.py:898
  22.0 20.6 %all-to-all-start = ((bf16[16,2,1028]{2,1,0:T(2,128)(2,1)}), bf16[16,2,1028]{2,1,0:T(2,128)(2,1)S(1)}, u32[]{:S(2)}, u32[]{:S(2)}) async-start(bf16[16,2,1028]{2,1,0:T(2,128)(2,1)} %reshape.223), calls=%async_computation | async-start | bytes 147456 | tf_op jit(solution)/shard_map/all_to_all | solution.py:1065
  28.5 223.4 %all-gather.3.cloned.1.call-start = ((), (), s32[]{:S(2)}) async-start(), calls=%async_computation.2 | async-start | bytes 26738688 | tf_op jit(solution)/shard_map/all_gather | solution.py:1094
  45.3 25.5 %collective-permute-start.3 = (bf16[128,4096]{1,0:T(8,128)(2,1)}, bf16[128,4096]{1,0:T(8,128)(2,1)}, u32[]{:S(2)}, u32[]{:S(2)}) collective-permute-start(bf16[128,4096]{1,0:T(8,128)(2,1)} %collective-permute-done.refs_7_.refs_8_.refs_10_), channel_id=1, source_target_pairs={{0,8},{2,10},{8,16},{10,18},{16,24},{18,26},{24,28},{26,30},{28,20... | collective-permute-start | bytes 3145736 | tf_op jit(solution)/shard_map/ppermute | solution.py:895
  45.9 25.7 %collective-permute-start.5 = (bf16[128,4096]{1,0:T(8,128)(2,1)}, bf16[128,4096]{1,0:T(8,128)(2,1)S(1)}, u32[]{:S(2)}, u32[]{:S(2)}) collective-permute-start(bf16[128,4096]{1,0:T(8,128)(2,1)} %collective-permute-done.refs_7_.refs_8_.refs_10_), channel_id=1, source_target_pairs={{0,2},{2,0},{4,6},{6,4},{8,10},{10,8},{12,14},{14,12},{16,18},{18,... | collective-permute-start | bytes 3145736 | tf_op jit(solution)/shard_map/ppermute | solution.py:898
  45.9 25.7 %collective-permute-start.4 = (bf16[128,4096]{1,0:T(8,128)(2,1)S(1)}, bf16[128,4096]{1,0:T(8,128)(2,1)}, u32[]{:S(2)}, u32[]{:S(2)}) collective-permute-start(bf16[128,4096]{1,0:T(8,128)(2,1)S(1)} %collective-permute-done.1.refs_1_.refs_2_.refs_4_), channel_id=1, source_target_pairs={{0,4},{2,6},{8,0},{10,2},{16,8},{18,10},{24,16},{26,18},{28,24},{3... | collective-permute-start | bytes 3145736 | tf_op jit(solution)/shard_map/ppermute | solution.py:895
  47.4 24.1 %collective-permute-start.6 = (bf16[128,4096]{1,0:T(8,128)(2,1)S(1)}, bf16[128,4096]{1,0:T(8,128)(2,1)S(1)}, u32[]{:S(2)}, u32[]{:S(2)}) collective-permute-start(bf16[128,4096]{1,0:T(8,128)(2,1)S(1)} %collective-permute-done.1.refs_1_.refs_2_.refs_4_), channel_id=1, source_target_pairs={{0,2},{2,0},{4,6},{6,4},{8,10},{10,8},{12,14},{14,12},{16,18},{18,... | collective-permute-start | bytes 3145736 | tf_op jit(solution)/shard_map/ppermute | solution.py:898
  71.6 25.2 %collective-permute-start.7 = (bf16[128,4096]{1,0:T(8,128)(2,1)}, bf16[128,4096]{1,0:T(8,128)(2,1)}, u32[]{:S(2)}, u32[]{:S(2)}) collective-permute-start(bf16[128,4096]{1,0:T(8,128)(2,1)} %collective-permute-done.3.refs_6_.refs_7_.refs_9_), channel_id=1, source_target_pairs={{0,8},{2,10},{8,16},{10,18},{16,24},{18,26},{24,28},{26,30},{28,20... | collective-permute-start | bytes 3145736 | tf_op jit(solution)/shard_map/ppermute | solution.py:895
  72.8 24.7 %collective-permute-start.8 = (bf16[128,4096]{1,0:T(8,128)(2,1)}, bf16[128,4096]{1,0:T(8,128)(2,1)S(1)}, u32[]{:S(2)}, u32[]{:S(2)}) collective-permute-start(bf16[128,4096]{1,0:T(8,128)(2,1)} %collective-permute-done.4.refs_2_.refs_3_.refs_5_), channel_id=1, source_target_pairs={{0,4},{2,6},{8,0},{10,2},{16,8},{18,10},{24,16},{26,18},{28,24},{3... | collective-permute-start | bytes 3145736 | tf_op jit(solution)/shard_map/ppermute | solution.py:895
  74.0 23.5 %collective-permute-start.9 = (bf16[128,4096]{1,0:T(8,128)(2,1)}, bf16[128,4096]{1,0:T(8,128)(2,1)}, u32[]{:S(2)}, u32[]{:S(2)}) collective-permute-start(bf16[128,4096]{1,0:T(8,128)(2,1)} %collective-permute-done.3.refs_6_.refs_7_.refs_9_), channel_id=1, source_target_pairs={{0,2},{2,0},{4,6},{6,4},{8,10},{10,8},{12,14},{14,12},{16,18},{18,... | collective-permute-start | bytes 3145736 | tf_op jit(solution)/shard_map/ppermute | solution.py:898
  74.0 23.5 %collective-permute-start.10 = (bf16[128,4096]{1,0:T(8,128)(2,1)}, bf16[128,4096]{1,0:T(8,128)(2,1)}, u32[]{:S(2)}, u32[]{:S(2)}) collective-permute-start(bf16[128,4096]{1,0:T(8,128)(2,1)} %collective-permute-done.4.refs_2_.refs_3_.refs_5_), channel_id=1, source_target_pairs={{0,2},{2,0},{4,6},{6,4},{8,10},{10,8},{12,14},{14,12},{16,18},{18,... | collective-permute-start | bytes 3145736 | tf_op jit(solution)/shard_map/ppermute | solution.py:898
  100.6 226.2 %all-gather.5.cloned.1.call-start = ((), (), s32[]{:S(2)}) async-start(), calls=%async_computation.3 | async-start | bytes 10027008 | tf_op jit(solution)/shard_map/all_gather | solution.py:1098
  100.6 29.8 %collective-permute-start.13 = (bf16[128,4096]{1,0:T(8,128)(2,1)}, bf16[128,4096]{1,0:T(8,128)(2,1)S(1)}, u32[]{:S(2)}, u32[]{:S(2)}) collective-permute-start(bf16[128,4096]{1,0:T(8,128)(2,1)} %collective-permute-done.7.refs_5_.refs_6_.refs_8_), channel_id=1, source_target_pairs={{0,2},{2,0},{4,6},{6,4},{8,10},{10,8},{12,14},{14,12},{16,18},{18,... | collective-permute-start | bytes 3145736 | tf_op jit(solution)/shard_map/ppermute | solution.py:898
  100.7 29.8 %collective-permute-start.14 = (bf16[128,4096]{1,0:T(8,128)(2,1)S(1)}, bf16[128,4096]{1,0:T(8,128)(2,1)}, u32[]{:S(2)}, u32[]{:S(2)}) collective-permute-start(bf16[128,4096]{1,0:T(8,128)(2,1)S(1)} %collective-permute-done.8.refs_3_.refs_4_.refs_6_), channel_id=1, source_target_pairs={{0,2},{2,0},{4,6},{6,4},{8,10},{10,8},{12,14},{14,12},{16,18},{18,... | collective-permute-start | bytes 3145736 | tf_op jit(solution)/shard_map/ppermute | solution.py:898
  103.9 24.5 %collective-permute-start.11 = (bf16[128,2048]{1,0:T(8,128)(2,1)}, bf16[128,2048]{1,0:T(8,128)(2,1)}, u32[]{:S(2)}, u32[]{:S(2)}) collective-permute-start(bf16[128,2048]{1,0:T(8,128)(2,1)} %slice.86), channel_id=1, source_target_pairs={{0,8},{2,10},{8,16},{10,18},{16,24},{18,26},{24,28},{26,30},{28,20... | collective-permute-start | bytes 1572872 | tf_op jit(solution)/shard_map/ppermute | solution.py:895
  105.1 25.4 %collective-permute-start.12 = (bf16[128,2048]{1,0:T(8,128)(2,1)}, bf16[128,2048]{1,0:T(8,128)(2,1)}, u32[]{:S(2)}, u32[]{:S(2)}) collective-permute-start(bf16[128,2048]{1,0:T(8,128)(2,1)} %slice.87), channel_id=1, source_target_pairs={{0,4},{2,6},{8,0},{10,2},{16,8},{18,10},{24,16},{26,18},{28,24},{3... | collective-permute-start | bytes 1572872 | tf_op jit(solution)/shard_map/ppermute | solution.py:895
  194.2 48.1 %collective-permute-start.17 = (bf16[512,2048]{1,0:T(8,128)(2,1)}, bf16[512,2048]{1,0:T(8,128)(2,1)S(1)}, u32[]{:S(2)}, u32[]{:S(2)}) collective-permute-start(bf16[512,2048]{1,0:T(8,128)(2,1)} %times_turned.2), channel_id=1, source_target_pairs={{0,1},{1,0},{2,3},{3,2},{4,5},{5,4},{6,7},{7,6},{8,9},{9,8},{10,11... | collective-permute-start | bytes 6291464 | tf_op jit(solution)/shard_map/ppermute | solution.py:1000
  286.3 19.5 %collective-permute-start.18 = (bf16[8,128,6144]{2,1,0:T(8,128)(2,1)}, bf16[8,128,6144]{2,1,0:T(8,128)(2,1)}, u32[]{:S(2)}, u32[]{:S(2)}) collective-permute-start(bf16[8,128,6144]{2,1,0:T(8,128)(2,1)} %weight_grads.8), channel_id=1, source_target_pairs={{0,2},{2,0},{4,6},{6,4},{8,10},{10,8},{12,14},{14,12},{16,18},{18,... | collective-permute-start | bytes 37748744 | tf_op jit(solution)/shard_map/ppermute | solution.py:898
  324.8 20.0 %collective-permute-start.19 = (bf16[128,3072]{1,0:T(8,128)(2,1)}, bf16[128,3072]{1,0:T(8,128)(2,1)}, u32[]{:S(2)}, u32[]{:S(2)}) collective-permute-start(bf16[128,3072]{1,0:T(8,128)(2,1)} %get-tuple-element.220), channel_id=1, source_target_pairs={{0,8},{2,10},{8,16},{10,18},{16,24},{18,26},{24,28},{26,30},{28,20... | collective-permute-start | bytes 2359304 | tf_op jit(solution)/shard_map/ppermute | solution.py:895
  325.9 19.7 %collective-permute-start.20 = (bf16[128,3072]{1,0:T(8,128)(2,1)}, bf16[128,3072]{1,0:T(8,128)(2,1)}, u32[]{:S(2)}, u32[]{:S(2)}) collective-permute-start(bf16[128,3072]{1,0:T(8,128)(2,1)} %get-tuple-element.221), channel_id=1, source_target_pairs={{0,4},{2,6},{8,0},{10,2},{16,8},{18,10},{24,16},{26,18},{28,24},{3... | collective-permute-start | bytes 2359304 | tf_op jit(solution)/shard_map/ppermute | solution.py:895
  349.8 35.5 %collective-permute-start.21 = (bf16[128,6144]{1,0:T(8,128)(2,1)S(1)}, bf16[128,6144]{1,0:T(8,128)(2,1)S(1)}, u32[]{:S(2)}, u32[]{:S(2)}) collective-permute-start(bf16[128,6144]{1,0:T(8,128)(2,1)S(1)} %get-tuple-element.228), channel_id=1, source_target_pairs={{0,8},{2,10},{8,16},{10,18},{16,24},{18,26},{24,28},{26,30},{28,20... | collective-permute-start | bytes 4718600 | tf_op jit(solution)/shard_map/ppermute | solution.py:895
  350.4 35.3 %collective-permute-start.22 = (bf16[128,6144]{1,0:T(8,128)(2,1)S(1)}, bf16[128,6144]{1,0:T(8,128)(2,1)}, u32[]{:S(2)}, u32[]{:S(2)}) collective-permute-start(bf16[128,6144]{1,0:T(8,128)(2,1)S(1)} %get-tuple-element.229), channel_id=1, source_target_pairs={{0,4},{2,6},{8,0},{10,2},{16,8},{18,10},{24,16},{26,18},{28,24},{3... | collective-permute-start | bytes 4718600 | tf_op jit(solution)/shard_map/ppermute | solution.py:895
  390.5 34.5 %collective-permute-start.26 = (bf16[128,6144]{1,0:T(8,128)(2,1)}, bf16[128,6144]{1,0:T(8,128)(2,1)S(1)}, u32[]{:S(2)}, u32[]{:S(2)}) collective-permute-start(bf16[128,6144]{1,0:T(8,128)(2,1)} %get-tuple-element.236), channel_id=1, source_target_pairs={{0,8},{2,10},{8,16},{10,18},{16,24},{18,26},{24,28},{26,30},{28,20... | collective-permute-start | bytes 4718600 | tf_op jit(solution)/shard_map/ppermute | solution.py:895
  391.9 33.8 %collective-permute-start.27 = (bf16[128,6144]{1,0:T(8,128)(2,1)S(1)}, bf16[128,6144]{1,0:T(8,128)(2,1)S(1)}, u32[]{:S(2)}, u32[]{:S(2)}) collective-permute-start(bf16[128,6144]{1,0:T(8,128)(2,1)S(1)} %get-tuple-element.237), channel_id=1, source_target_pairs={{0,4},{2,6},{8,0},{10,2},{16,8},{18,10},{24,16},{26,18},{28,24},{3... | collective-permute-start | bytes 4718600 | tf_op jit(solution)/shard_map/ppermute | solution.py:895
  425.7 44.2 %collective-permute-start.30 = (bf16[8,128,2304]{2,1,0:T(8,128)(2,1)}, bf16[8,128,2304]{2,1,0:T(8,128)(2,1)}, u32[]{:S(2)}, u32[]{:S(2)}) collective-permute-start(bf16[8,128,2304]{2,1,0:T(8,128)(2,1)} %weight_grads.10), channel_id=1, source_target_pairs={{0,2},{2,0},{4,6},{6,4},{8,10},{10,8},{12,14},{14,12},{16,18},{18,... | collective-permute-start | bytes 14155784 | tf_op jit(solution)/shard_map/ppermute | solution.py:898
  432.8 35.9 %collective-permute-start.28 = (bf16[128,6144]{1,0:T(8,128)(2,1)}, bf16[128,6144]{1,0:T(8,128)(2,1)S(1)}, u32[]{:S(2)}, u32[]{:S(2)}) collective-permute-start(bf16[128,6144]{1,0:T(8,128)(2,1)} %get-tuple-element.243), channel_id=1, source_target_pairs={{0,8},{2,10},{8,16},{10,18},{16,24},{18,26},{24,28},{26,30},{28,20... | collective-permute-start | bytes 4718600 | tf_op jit(solution)/shard_map/ppermute | solution.py:895
  434.1 35.8 %collective-permute-start.29 = (bf16[128,6144]{1,0:T(8,128)(2,1)}, bf16[128,6144]{1,0:T(8,128)(2,1)S(1)}, u32[]{:S(2)}, u32[]{:S(2)}) collective-permute-start(bf16[128,6144]{1,0:T(8,128)(2,1)} %copy-done.53), channel_id=1, source_target_pairs={{0,4},{2,6},{8,0},{10,2},{16,8},{18,10},{24,16},{26,18},{28,24},{3... | collective-permute-start | bytes 4718600 | tf_op jit(solution)/shard_map/ppermute | solution.py:895
  434.9 17.9 %collective-permute-start.24 = (bf16[160,2048]{1,0:T(8,128)(2,1)}, bf16[160,2048]{1,0:T(8,128)(2,1)S(1)}, u32[]{:S(2)}, u32[]{:S(2)}) collective-permute-start(bf16[160,2048]{1,0:T(8,128)(2,1)} %get-tuple-element.408), channel_id=1, source_target_pairs={{0,1},{1,0},{2,3},{3,2},{4,5},{5,4},{6,7},{7,6},{8,9},{9,8},{10,11... | collective-permute-start | bytes 1966088 | tf_op jit(solution)/shard_map/ppermute | solution.py:1000
  437.1 46.4 %collective-permute-start.23 = (bf16[192,2048]{1,0:T(8,128)(2,1)}, bf16[192,2048]{1,0:T(8,128)(2,1)}, u32[]{:S(2)}, u32[]{:S(2)}) collective-permute-start(bf16[192,2048]{1,0:T(8,128)(2,1)} %slice.89), channel_id=1, source_target_pairs={{0,1},{1,0},{2,3},{3,2},{4,5},{5,4},{6,7},{7,6},{8,9},{9,8},{10,11... | collective-permute-start | bytes 2359304 | tf_op jit(solution)/shard_map/ppermute | solution.py:1000
  493.9 21.7 %collective-permute-start.33 = (bf16[128,2304]{1,0:T(8,128)(2,1)S(1)}, bf16[128,2304]{1,0:T(8,128)(2,1)S(1)}, u32[]{:S(2)}, u32[]{:S(2)}) collective-permute-start(bf16[128,2304]{1,0:T(8,128)(2,1)S(1)} %get-tuple-element.252), channel_id=1, source_target_pairs={{0,8},{2,10},{8,16},{10,18},{16,24},{18,26},{24,28},{26,30},{28,20... | collective-permute-start | bytes 1769480 | tf_op jit(solution)/shard_map/ppermute | solution.py:895
  495.7 19.9 %collective-permute-start.34 = (bf16[128,2304]{1,0:T(8,128)(2,1)S(1)}, bf16[128,2304]{1,0:T(8,128)(2,1)S(1)}, u32[]{:S(2)}, u32[]{:S(2)}) collective-permute-start(bf16[128,2304]{1,0:T(8,128)(2,1)S(1)} %get-tuple-element.253), channel_id=1, source_target_pairs={{0,4},{2,6},{8,0},{10,2},{16,8},{18,10},{24,16},{26,18},{28,24},{3... | collective-permute-start | bytes 1769480 | tf_op jit(solution)/shard_map/ppermute | solution.py:895
  515.7 34.0 %collective-permute-start.35 = (bf16[160,2048]{1,0:T(8,128)(2,1)S(1)}, bf16[160,2048]{1,0:T(8,128)(2,1)S(1)}, u32[]{:S(2)}, u32[]{:S(2)}) collective-permute-start(bf16[160,2048]{1,0:T(8,128)(2,1)S(1)} %get-tuple-element.406), channel_id=1, source_target_pairs={{0,1},{1,0},{2,3},{3,2},{4,5},{5,4},{6,7},{7,6},{8,9},{9,8},{10,11... | collective-permute-start | bytes 1966088 | tf_op jit(solution)/shard_map/ppermute | solution.py:1000
  521.2 28.6 %collective-permute-start.36 = (bf16[128,2304]{1,0:T(8,128)(2,1)S(1)}, bf16[128,2304]{1,0:T(8,128)(2,1)S(1)}, u32[]{:S(2)}, u32[]{:S(2)}) collective-permute-start(bf16[128,2304]{1,0:T(8,128)(2,1)S(1)} %get-tuple-element.262), channel_id=1, source_target_pairs={{0,8},{2,10},{8,16},{10,18},{16,24},{18,26},{24,28},{26,30},{28,20... | collective-permute-start | bytes 1769480 | tf_op jit(solution)/shard_map/ppermute | solution.py:895
  522.7 27.0 %collective-permute-start.37 = (bf16[128,2304]{1,0:T(8,128)(2,1)S(1)}, bf16[128,2304]{1,0:T(8,128)(2,1)S(1)}, u32[]{:S(2)}, u32[]{:S(2)}) collective-permute-start(bf16[128,2304]{1,0:T(8,128)(2,1)S(1)} %get-tuple-element.263), channel_id=1, source_target_pairs={{0,4},{2,6},{8,0},{10,2},{16,8},{18,10},{24,16},{26,18},{28,24},{3... | collective-permute-start | bytes 1769480 | tf_op jit(solution)/shard_map/ppermute | solution.py:895
  567.3 17.5 %collective-permute-start.41 = (bf16[8,128,2560]{2,1,0:T(8,128)(2,1)}, bf16[8,128,2560]{2,1,0:T(8,128)(2,1)}, u32[]{:S(2)}, u32[]{:S(2)}) collective-permute-start(bf16[8,128,2560]{2,1,0:T(8,128)(2,1)} %weight_grads.12), channel_id=1, source_target_pairs={{0,2},{2,0},{4,6},{6,4},{8,10},{10,8},{12,14},{14,12},{16,18},{18,... | collective-permute-start | bytes 15728648 | tf_op jit(solution)/shard_map/ppermute | solution.py:898
  567.3 17.5 %collective-permute-start.38 = (bf16[160,2048]{1,0:T(8,128)(2,1)S(1)}, bf16[160,2048]{1,0:T(8,128)(2,1)S(1)}, u32[]{:S(2)}, u32[]{:S(2)}) collective-permute-start(bf16[160,2048]{1,0:T(8,128)(2,1)S(1)} %get-tuple-element.405), channel_id=1, source_target_pairs={{0,1},{1,0},{2,3},{3,2},{4,5},{5,4},{6,7},{7,6},{8,9},{9,8},{10,11... | collective-permute-start | bytes 1966088 | tf_op jit(solution)/shard_map/ppermute | solution.py:1000
  570.1 43.9 %collective-permute-start.42 = (bf16[192,2048]{1,0:T(8,128)(2,1)}, bf16[192,2048]{1,0:T(8,128)(2,1)}, u32[]{:S(2)}, u32[]{:S(2)}) collective-permute-start(bf16[192,2048]{1,0:T(8,128)(2,1)} %slice.94), channel_id=1, source_target_pairs={{0,1},{1,0},{2,3},{3,2},{4,5},{5,4},{6,7},{7,6},{8,9},{9,8},{10,11... | collective-permute-start | bytes 2359304 | tf_op jit(solution)/shard_map/ppermute | solution.py:1000
  617.1 16.2 %collective-permute-start.45 = (bf16[128,2560]{1,0:T(8,128)(2,1)S(1)}, bf16[128,2560]{1,0:T(8,128)(2,1)S(1)}, u32[]{:S(2)}, u32[]{:S(2)}) collective-permute-start(bf16[128,2560]{1,0:T(8,128)(2,1)S(1)} %get-tuple-element.296), channel_id=1, source_target_pairs={{0,8},{2,10},{8,16},{10,18},{16,24},{18,26},{24,28},{26,30},{28,20... | collective-permute-start | bytes 1966088 | tf_op jit(solution)/shard_map/ppermute | solution.py:895
  618.6 15.6 %collective-permute-start.46 = (bf16[128,2560]{1,0:T(8,128)(2,1)S(1)}, bf16[128,2560]{1,0:T(8,128)(2,1)S(1)}, u32[]{:S(2)}, u32[]{:S(2)}) collective-permute-start(bf16[128,2560]{1,0:T(8,128)(2,1)S(1)} %get-tuple-element.297), channel_id=1, source_target_pairs={{0,4},{2,6},{8,0},{10,2},{16,8},{18,10},{24,16},{26,18},{28,24},{3... | collective-permute-start | bytes 1966088 | tf_op jit(solution)/shard_map/ppermute | solution.py:895
  655.1 27.2 %collective-permute-start.54 = (bf16[8,128,1536]{2,1,0:T(8,128)(2,1)}, bf16[8,128,1536]{2,1,0:T(8,128)(2,1)}, u32[]{:S(2)}, u32[]{:S(2)}) collective-permute-start(bf16[8,128,1536]{2,1,0:T(8,128)(2,1)} %weight_grads.14), channel_id=1, source_target_pairs={{0,2},{2,0},{4,6},{6,4},{8,10},{10,8},{12,14},{14,12},{16,18},{18,... | collective-permute-start | bytes 9437192 | tf_op jit(solution)/shard_map/ppermute | solution.py:898
  655.1 27.2 %collective-permute-start.48 = (bf16[160,2048]{1,0:T(8,128)(2,1)}, bf16[160,2048]{1,0:T(8,128)(2,1)}, u32[]{:S(2)}, u32[]{:S(2)}) collective-permute-start(bf16[160,2048]{1,0:T(8,128)(2,1)} %get-tuple-element.404), channel_id=1, source_target_pairs={{0,1},{1,0},{2,3},{3,2},{4,5},{5,4},{6,7},{7,6},{8,9},{9,8},{10,11... | collective-permute-start | bytes 1966088 | tf_op jit(solution)/shard_map/ppermute | solution.py:1000
  660.6 21.7 %collective-permute-start.52 = (bf16[128,2560]{1,0:T(8,128)(2,1)}, bf16[128,2560]{1,0:T(8,128)(2,1)S(1)}, u32[]{:S(2)}, u32[]{:S(2)}) collective-permute-start(bf16[128,2560]{1,0:T(8,128)(2,1)} %get-tuple-element.318), channel_id=1, source_target_pairs={{0,8},{2,10},{8,16},{10,18},{16,24},{18,26},{24,28},{26,30},{28,20... | collective-permute-start | bytes 1966088 | tf_op jit(solution)/shard_map/ppermute | solution.py:895
  662.0 20.3 %collective-permute-start.53 = (bf16[128,2560]{1,0:T(8,128)(2,1)}, bf16[128,2560]{1,0:T(8,128)(2,1)}, u32[]{:S(2)}, u32[]{:S(2)}) collective-permute-start(bf16[128,2560]{1,0:T(8,128)(2,1)} %get-tuple-element.319), channel_id=1, source_target_pairs={{0,4},{2,6},{8,0},{10,2},{16,8},{18,10},{24,16},{26,18},{28,24},{3... | collective-permute-start | bytes 1966088 | tf_op jit(solution)/shard_map/ppermute | solution.py:895
  672.7 32.6 %collective-permute-start.47 = (bf16[192,2048]{1,0:T(8,128)(2,1)}, bf16[192,2048]{1,0:T(8,128)(2,1)}, u32[]{:S(2)}, u32[]{:S(2)}) collective-permute-start(bf16[192,2048]{1,0:T(8,128)(2,1)} %slice.95), channel_id=1, source_target_pairs={{0,1},{1,0},{2,3},{3,2},{4,5},{5,4},{6,7},{7,6},{8,9},{9,8},{10,11... | collective-permute-start | bytes 2359304 | tf_op jit(solution)/shard_map/ppermute | solution.py:1000
  722.8 19.0 %all-to-all-start.1 = ((f32[16,1,2056]{2,1,0:T(1,128)}), f32[16,1,2056]{2,1,0:T(1,128)}, u32[]{:S(2)}, u32[]{:S(2)}) async-start(f32[16,1,2056]{2,1,0:T(1,128)} %copy.81), calls=%async_computation.1 | async-start | bytes 278528 | tf_op jit(solution)/shard_map/all_to_all | solution.py:1251
  733.4 15.9 %collective-permute-start.62 = (bf16[128,1536]{1,0:T(8,128)(2,1)}, bf16[128,1536]{1,0:T(8,128)(2,1)S(1)}, u32[]{:S(2)}, u32[]{:S(2)}) collective-permute-start(bf16[128,1536]{1,0:T(8,128)(2,1)} %get-tuple-element.356), channel_id=1, source_target_pairs={{0,8},{2,10},{8,16},{10,18},{16,24},{18,26},{24,28},{26,30},{28,20... | collective-permute-start | bytes 1179656 | tf_op jit(solution)/shard_map/ppermute | solution.py:895
  (109 other events, 1531.9 us)
Sparse Core Ops, SparseCore 0:
  100.7 138.4 all-gather.2
  241.4 81.0 all-gather.4

commit v4 on v3

--- a/solution.py
+++ b/solution.py
@@ -310,10 +310,10 @@
             gproj_ref[:, column : column + width] = gsignal.astype(BF16)
 
 
-def mixer_specs(length, wide, first):
+def mixer_specs(length, wide, first, skip):
     fixed = lambda shape: pl.BlockSpec(shape, lambda g: (0,) * len(shape))
     return [
-        pl.BlockSpec((length, 3 * wide), lambda g: (0, g + first)),
+        pl.BlockSpec((length, 3 * wide), lambda g: (0, g + skip)),
         fixed((length, 128)),
         pl.BlockSpec((3, 4, wide), lambda g: (0, 0, g + first)),
         fixed((1, 128)),
@@ -322,58 +322,59 @@
     ]
 
 
-def mixer_forward(projected, logits, conv, gain, seg_ids, heads, passes, first, count):
+CHEAP = pl.CostEstimate(flops=1000, bytes_accessed=1000, transcendentals=0)
+
+
+def mixer_forward(projected, logits, conv, gain, seg_ids, heads, passes, first):
     length = projected.shape[0]
     wide = heads * 128
+    count = projected.shape[1] // (3 * wide)
     f32 = jax.ShapeDtypeStruct((length, count * wide), F32)
     block = pl.BlockSpec((length, wide), lambda g: (0, g))
     return pl.pallas_call(
         functools.partial(forward_kernel, heads, passes, first),
         grid=(count,),
-        in_specs=mixer_specs(length, wide, first),
+        in_specs=mixer_specs(length, wide, first, 0),
         out_specs=[block] * 5,
         out_shape=[jax.ShapeDtypeStruct((length, count * wide), BF16), f32, f32, f32, f32],
         scratch_shapes=[pltpu.VMEM((length, wide), F32)] * 3,
-        compiler_params=pltpu.CompilerParams(vmem_limit_bytes=48 * 2**20),
-        cost_estimate=pl.CostEstimate(flops=1000, bytes_accessed=1000, transcendentals=0),
+        compiler_params=pltpu.CompilerParams(vmem_limit_bytes=60 * 2**20),
+        cost_estimate=CHEAP,
         name="mixer_forward",
     )(projected, logits, conv, gain, seg_ids[:, None], seg_ids[None, :])
 
 
-def mixer_backward(projected, logits, conv, gain, seg_ids, saved, grad_mixed, heads, passes, first, count, base):
+def mixer_backward(projected, logits, conv, gain, seg_ids, saved, grad_mixed, heads, passes, first, skip):
     length = projected.shape[0]
     wide = heads * 128
-    block = pl.BlockSpec((length, wide), lambda g: (0, g + first - base))
+    block = pl.BlockSpec((length, wide), lambda g: (0, g + skip))
     grads = pl.BlockSpec((length, wide), lambda g: (0, g + first))
     fixed = lambda shape: pl.BlockSpec(shape, lambda g: (0,) * len(shape))
+    outs = [
+        jax.ShapeDtypeStruct((length, 3 * wide), BF16),
+        jax.ShapeDtypeStruct((length, 128), F32),
+        jax.ShapeDtypeStruct((3, 4, wide), F32),
+        jax.ShapeDtypeStruct((1, 128), F32),
+    ]
     return pl.pallas_call(
         functools.partial(backward_kernel, heads, passes, first),
-        grid=(count,),
-        in_specs=mixer_specs(length, wide, first) + [block] * 4 + [grads],
-        out_specs=[
-            pl.BlockSpec((length, 3 * wide), lambda g: (0, g)),
-            fixed((length, 128)),
-            pl.BlockSpec((3, 4, wide), lambda g: (0, 0, g)),
-            fixed((1, 128)),
-        ],
-        out_shape=[
-            jax.ShapeDtypeStruct((length, 3 * count * wide), BF16),
-            jax.ShapeDtypeStruct((length, 128), F32),
-            jax.ShapeDtypeStruct((3, 4, count * wide), F32),
-            jax.ShapeDtypeStruct((1, 128), F32),
-        ],
+        grid=(1,),
+        in_specs=mixer_specs(length, wide, first, skip) + [block] * 4 + [grads],
+        out_specs=[fixed(out.shape) for out in outs],
+        out_shape=outs,
         scratch_shapes=[pltpu.VMEM((length, wide), F32)] * 7,
-        compiler_params=pltpu.CompilerParams(vmem_limit_bytes=48 * 2**20),
-        cost_estimate=pl.CostEstimate(flops=1000, bytes_accessed=1000, transcendentals=0),
+        compiler_params=pltpu.CompilerParams(vmem_limit_bytes=50 * 2**20),
+        cost_estimate=CHEAP,
         name="mixer_backward",
     )(projected, logits, conv, gain, seg_ids[:, None], seg_ids[None, :], *saved, grad_mixed)
 
 
-LIMIT = 48 * 2**20
-
-
 def whole(array):
     return pl.BlockSpec(array.shape, lambda *_: (0,) * array.ndim)
+
+
+def room(name):
+    return (40 if name == "weight_grads" else 50) * 2**20
 
 
 def call(kernel, grid, in_specs, out_specs, out_shape, name, table, *operands, scratch=()):
@@ -387,8 +388,8 @@
             scratch_shapes=scratch,
         ),
         out_shape=out_shape,
-        compiler_params=pltpu.CompilerParams(vmem_limit_bytes=LIMIT),
-        cost_estimate=pl.CostEstimate(flops=1000, bytes_accessed=1000, transcendentals=0),
+        compiler_params=pltpu.CompilerParams(vmem_limit_bytes=room(name)),
+        cost_estimate=CHEAP,
         name=name,
     )(table, *operands)
 
@@ -849,7 +850,7 @@
         in_specs=[pl.BlockSpec((step, 4, width), lambda i: (i, 0, 0))],
         out_specs=pl.BlockSpec((step, 4 * width), lambda i: (i, 0)),
         out_shape=jax.ShapeDtypeStruct((rows, 4 * width), BF16),
-        cost_estimate=pl.CostEstimate(flops=1000, bytes_accessed=1000, transcendentals=0),
+        cost_estimate=CHEAP,
         name="pack_mixer",
     )(weights)
 
@@ -892,10 +893,12 @@
             self.hops[turn] = hops
 
     def send(self, value, turn):
-        return Box(lax.ppermute(value, "dp", self.hops[turn]))
+        with jax.named_scope("ring_send"):
+            return Box(lax.ppermute(value, "dp", self.hops[turn]))
 
     def swap(self, value):
-        return Box(lax.ppermute(value, "dp", self.core_swap))
+        with jax.named_scope("core_swap"):
+            return Box(lax.ppermute(value, "dp", self.core_swap))
 
     def steps(self, portion):
         total = self.chips // 2
@@ -956,6 +959,7 @@
         self.other = Box(grads(1, None))
         self.own = None
         self.got = []
+        self.out = []
 
     def swap(self):
         self.other = self.ring.swap(self.other.value)
@@ -963,14 +967,20 @@
     def join(self):
         self.own = Box(self.grads(0, self.other.value))
 
-    def advance(self, portion):
+    def hop(self, portion):
         chips = self.ring.chips
         for step in self.ring.steps(portion):
+            self.send()
             away = chips // 2 - step + 1
             kind = {1: "first", 2: "second"}.get(step, "middle")
             got = [box.value for box in self.got]
             out = ring_hop(kind, self.own.value, got, self.ring.around, away, chips - away)
-            self.got = [self.ring.send(out[0], 1), self.ring.send(out[1], -1)]
+            self.out = [Box(o) for o in out]
+
+    def send(self):
+        if self.out:
+            self.got = [self.ring.send(self.out[0].value, 1), self.ring.send(self.out[1].value, -1)]
+            self.out = []
 
     def boxes(self):
         return [self.other if self.own is None else self.own] + self.got
@@ -997,7 +1007,8 @@
 
 
 def swap_tensor(value):
-    return lax.ppermute(value, "tensor", [(0, 1), (1, 0)])
+    with jax.named_scope("tensor_swap"):
+        return lax.ppermute(value, "tensor", [(0, 1), (1, 0)])
 
 
 def norm_back(values, scale, gain, grad):
@@ -1066,6 +1077,8 @@
     if in_ring:
         sync(*attn.boxes())
         attn.advance(1)
+        sync(*attn.boxes(), small, *mlp_local)
+        attn.advance(2)
     at = [0, rows, 2 * rows, 2 * rows + rows * head_count]
     small = small.value
     gain_in = small[:, at[0] : at[1]].reshape(-1).astype(F32)
@@ -1080,9 +1093,7 @@
     normed = Box((inputs_f * scale_in * gain_in).astype(BF16))
     logits = Box(matmul(normed.value, beta_pad.value, NN))
     if in_ring:
-        sync(*attn.boxes(), normed, logits, taps, gain_heads, beta_pad)
-        attn.advance(2)
-        sync(*attn.boxes(), normed, *mlp_local)
+        sync(*attn.boxes(), normed, logits, taps, gain_heads, beta_pad, *mlp_local)
         attn.advance(3)
         sync(*attn.boxes(), normed, mlp_local[1])
         attn.swap()
@@ -1093,78 +1104,83 @@
         table = jnp.arange(width // 128, dtype=jnp.int32)
     mats = [lax.all_gather(mlp_local[0].value, "dp", axis=0, tiled=True)]
 
+    half = qkv // 2
+    span = groups // 2
     projected = Box(times_rows(normed.value, attn_blocks, table, 0, qkv, 512, F32))
     sync(projected, mlp_local[1])
     mats.append(lax.all_gather(mlp_local[1].value, "dp", axis=0, tiled=True))
     mixed, *saved = mixer_forward(
-        projected.value,
-        logits.value,
-        taps.value,
-        gain_heads.value,
-        seg_ids,
-        HEADS_PER_STEP,
-        PASSES,
-        0,
-        groups,
+        projected.value, logits.value, taps.value, gain_heads.value, seg_ids, HEADS_PER_STEP, PASSES, 0
     )
     part = times_turned([([mixed], attn_blocks, qkv)], table)
     hidden = inputs_f + part.astype(F32) + swap_tensor(part).astype(F32)
     scale_mid = lax.rsqrt(jnp.mean(hidden * hidden, axis=-1, keepdims=True) + 1e-05)
-    normed_mlp = (hidden * scale_mid * gain_mid).astype(BF16)
+    normed_mlp = Box((hidden * scale_mid * gain_mid).astype(BF16))
+
+    acts = []
+
+    def gated(which):
+        acts.append(Box(gated_units(normed_mlp.value, cotangent, mats[which], table, 256)))
 
     def mlp_grads(which):
+        def grads(core, plus):
+            act = acts[which].value
+            size = act.shape[2]
+            tile = size // 2 if size % 512 == 0 else size
+            pairs = [(normed_mlp.value, act, 0, 2), (cotangent, act, 2, 1)]
+            return weight_grads(pairs, tile, rows, ring.cores, core, plus)
+
+        return grads
+
+    def turned(which, kind, plus):
         act = acts[which].value
-        size = act.shape[2]
-        pairs = [(normed_mlp, act, 0, 2), (cotangent, act, 2, 1)]
-        tile = size // 2 if size % 512 == 0 else size
-
-        def grads(half, plus):
-            return weight_grads(pairs, tile, rows, ring.cores, half, plus)
-
-        return grads
-
-    acts = [Box(gated_units(normed_mlp, cotangent, mats[0], table, 256))]
-    sync(*acts)
+        return Box(
+            units_turned([(act, p, mats[which]) for p in range(2)], 256, kind, table, plus=plus)
+        )
+
+    gated(0)
     sums = [Scatter(ring, mlp_grads(0))]
-    sync(*acts, *sums[0].boxes())
+    sync(*sums[0].boxes(), *acts)
     sums[0].swap()
-    act = acts[0].value
-    part = Box(units_turned([(act, p, mats[0]) for p in range(2)], 256, F32, table))
-    sync(part, *acts, *sums[0].boxes())
+    part = turned(0, F32, None)
+    sync(part, *sums[0].boxes(), *acts)
     sums[0].join()
-    sync(part, *acts, *sums[0].boxes())
-    sums[0].advance(0)
-    acts.append(Box(gated_units(normed_mlp, cotangent, mats[1], table, 256)))
-    sync(part, *acts, *sums[0].boxes())
-    sums[0].advance(1)
-    act = acts[1].value
-    part = Box(units_turned([(act, p, mats[1]) for p in range(2)], 256, BF16, table, plus=part.value))
-    sync(part, *acts, *sums[0].boxes())
+    sums[0].hop(0)
+    sync(*sums[0].out, normed_mlp)
+    sums[0].send()
+    gated(1)
+    part = turned(1, BF16, part.value)
+    sync(part, *sums[0].boxes())
     exchange = Exchange(part.value, 3)
-    sums[0].advance(2)
+    piece_a = exchange.advance()
+    sums[0].hop(1)
+    sync(*sums[0].out, *acts)
+    sums[0].send()
     sums.append(Scatter(ring, mlp_grads(1)))
-    sync(exchange.advance(), *acts, *sums[0].boxes(), *sums[1].boxes())
-    sums[0].advance(3)
+    sync(piece_a, *sums[1].boxes(), *acts)
     sums[1].swap()
+    piece_b = exchange.advance()
     down = Box(units_turned([(a.value, 2, mat) for a, mat in zip(acts, mats)], 256, BF16, table))
-    sync(exchange.advance(), down, *acts, *sums[0].boxes(), *sums[1].boxes())
+    sync(piece_b, down, *sums[1].boxes(), *acts)
+    piece_c = exchange.advance()
     sums[1].join()
-    sync(*sums[1].boxes())
-    sums[1].advance(0)
-    sync(exchange.advance(), *sums[1].boxes())
-    sums[1].advance(1)
+    sync(*sums[0].boxes(), *sums[1].boxes())
+    sums[0].hop(2)
+    sums[0].send()
+    sync(piece_c)
 
     grad_norm, grad_gain_mid = norm_back(hidden, scale_mid, gain_mid, exchange.result())
     grad_hidden = cotangent.astype(F32) + grad_norm
-    grad_hidden_low = grad_hidden.astype(BF16)
+    grad_hidden_low = Box(grad_hidden.astype(BF16))
     grad_mixed = Box(
-        times_rows(grad_hidden_low, attn_blocks, table, qkv, local_width, 512, F32)
+        times_rows(grad_hidden_low.value, attn_blocks, table, qkv, local_width, 512, F32)
     )
-    sync(*sums[1].boxes(), grad_mixed, down)
-    sums[1].advance(2)
-    down = Exchange(down.value, 3)
-
-    def mixer_grads(first, count):
+    sync(grad_mixed, grad_hidden_low, down)
+    down = Exchange(down.value, 4)
+    back = []
+
+    def mixer_grads():
+        group = len(back)
         made = mixer_backward(
             projected.value,
             logits.value,
@@ -1175,80 +1191,109 @@
             grad_mixed.value,
             HEADS_PER_STEP,
             PASSES,
-            first,
-            count,
-            0,
+            group,
+            group,
         )
-        return [Box(m) for m in made]
-
-    half = groups // 2
-    back = [mixer_grads(0, half)]
-    sync(down.advance(), *sums[1].boxes(), back[0][0], grad_mixed)
-    sums[1].advance(3)
-
-    def early_grads(which, plus):
-        pairs = [(normed.value, back[0][0].value, 0, 1), (grad_hidden_low, mixed, 0, 1)]
-        return weight_grads(pairs, 512, rows, ring.cores, which, plus)
-
+        back.append([Box(m) for m in made])
+
+    def early_grads(core, plus):
+        pairs = [(normed.value, b[0].value, 0, 1) for b in back[:span]]
+        pairs.append((grad_hidden_low.value, mixed, 0, 1))
+        return weight_grads(pairs, 256, rows, ring.cores, core, plus)
+
+    def late_grads(core, plus):
+        pairs = [(normed.value, b[0].value, 0, 1) for b in back[span:]]
+        return weight_grads(pairs, 3 * wide, rows, ring.cores, core, plus)
+
+    quarter = [groups * i // 4 for i in range(5)]
+
+    def mixer_grads_to(count):
+        while len(back) < count:
+            mixer_grads()
+
+    mixer_grads_to(quarter[1])
+    sync(down.advance(), *sums[0].boxes(), back[-1][0], grad_mixed)
+    sums[0].hop(3)
+    sync(*sums[0].out, grad_mixed)
+    sums[0].send()
+    mixer_grads_to(quarter[2])
     first = Scatter(ring, early_grads)
-    sync(*sums[1].boxes(), *first.boxes(), grad_mixed)
+    sync(down.advance(), *first.boxes(), *sums[0].boxes(), *sums[1].boxes(), grad_mixed)
     first.swap()
-    back.append(mixer_grads(half, half // 2))
-    sync(down.advance(), back[1][0], grad_mixed, *first.boxes())
+    sums[1].hop(0)
+    sync(*sums[1].out, grad_mixed)
+    sums[1].send()
+    mixer_grads_to(quarter[3])
+    sync(down.advance(), *first.boxes(), *sums[1].boxes(), back[-1][0], grad_mixed)
+    sums[1].hop(1)
+    sync(*sums[1].out, *first.boxes())
+    sums[1].send()
     first.join()
-    sync(grad_mixed, *first.boxes())
-    first.advance(0)
-    back.append(mixer_grads(half + half // 2, half - half // 2))
-    sync(down.advance(), back[2][0], *first.boxes())
-    first.advance(1)
-    grad_logits_low = sum(b[1].value for b in back).astype(BF16)
-    lefts = [b[0].value for b in back]
-    part = Box(times_turned([(lefts, attn_blocks, 0)], table, extra=(grad_logits_low, beta_pad.value)))
-    sync(part, back[1][0], back[2][0], *first.boxes())
+    sync(down.advance(), *first.boxes(), *sums[1].boxes(), grad_mixed)
+    sums[1].hop(2)
+    first.hop(0)
+    sync(*sums[1].out, *first.out, grad_mixed)
+    sums[1].send()
+    first.send()
+    mixer_grads_to(groups)
+    sync(*first.boxes(), *sums[1].boxes(), *[b[0] for b in back])
+    sums[1].hop(3)
+    first.hop(1)
+    sync(*sums[1].out, *first.out, *[b[0] for b in back])
+    sums[1].send()
+    first.send()
+    second = Scatter(ring, late_grads)
+    grad_logits_low = Box(sum(b[1].value for b in back).astype(BF16))
+    sync(*second.boxes(), *[b[0] for b in back], grad_logits_low)
+    part = Box(
+        times_turned(
+            [([b[0].value for b in back], attn_blocks, 0)],
+            table,
+            extra=(grad_logits_low.value, beta_pad.value),
+        )
+    )
+    sync(part, *first.boxes(), *sums[1].boxes(), *[b[0] for b in back], *second.boxes(), grad_logits_low)
     exchange = Exchange(part.value, 3)
-    first.advance(2)
-
-    def late_grads(which, plus):
-        pairs = [(normed.value, b[0].value, 0, 1) for b in back[1:]]
-        return weight_grads(pairs, back[1][0].value.shape[1], rows, ring.cores, which, plus)
-
-    second = Scatter(ring, late_grads)
-    sync(exchange.advance(), back[1][0], back[2][0], *first.boxes(), *second.boxes())
-    first.advance(3)
+    piece_a = exchange.advance()
     second.swap()
-    grad_beta = Box(matmul(normed.value, grad_logits_low, TN)[:, :head_count])
+    first.hop(2)
+    sync(*first.out, *sums[1].boxes(), grad_logits_low)
+    first.send()
     mlp_grad = Box(units_result([s.parts() for s in sums], ring.around))
-    sync(exchange.advance(), grad_beta, mlp_grad, *first.boxes(), *second.boxes())
+    grad_beta = Box(matmul(normed.value, grad_logits_low.value, TN)[:, :head_count])
+    sync(piece_a, mlp_grad, grad_beta, *first.boxes(), *second.boxes(), *[b[0] for b in back])
+    piece_b = exchange.advance()
     second.join()
-    second.advance(0)
-    result = Box((hidden + down.result()).astype(BF16))
-    sync(exchange.advance(), result, *first.boxes(), *second.boxes())
-    second.advance(1)
-    grad_normed = exchange.result()
-    grad_beta = grad_beta.value
-    sync(*second.boxes())
-    second.advance(2)
-    sync(*second.boxes())
-    second.advance(3)
-
-    grad_first, grad_gain_in = norm_back(inputs_f, scale_in, gain_in, grad_normed)
-    grad_inputs = grad_hidden + grad_first
-
+    second.hop(0)
+    first.hop(3)
+    sync(*second.out, *first.out, grad_beta)
+    second.send()
+    first.send()
     grad_gain_heads = sum(b[3].value[0] for b in back)
     grad_gain_heads = grad_gain_heads + swap_tensor(grad_gain_heads)
     grad_taps = jnp.concatenate([b[2].value for b in back], axis=2)
     grad_taps = grad_taps.reshape(3, 4, head_count, devices, piece).transpose(3, 0, 1, 2, 4)
-    packed = jnp.concatenate(
-        [
-            grad_gain_in.reshape(devices, -1),
-            grad_gain_mid.reshape(devices, -1),
-            grad_beta.reshape(devices, -1),
-            grad_taps.reshape(devices, -1),
-            grad_gain_heads.reshape(devices, -1),
-        ],
-        axis=1,
-    )
-    packed = jnp.sum(lax.all_to_all(packed, "dp", 0, 0, tiled=True), axis=0)
+    early = [grad_gain_mid, grad_beta.value, grad_taps, grad_gain_heads]
+    early = Box(jnp.concatenate([value.reshape(devices, -1) for value in early], axis=1))
+    sync(piece_b, early, *second.boxes(), *first.boxes())
+    piece_c = exchange.advance()
+    second.hop(1)
+    sync(early, *second.out)
+    second.send()
+    early = Box(lax.all_to_all(early.value, "dp", 0, 0, tiled=True))
+    result = Box((hidden + down.result()).astype(BF16))
+    sync(piece_c, result, *second.boxes())
+    second.hop(2)
+    second.send()
+    sync(early, *second.boxes())
+    second.hop(3)
+    second.send()
+
+    grad_first, grad_gain_in = norm_back(inputs_f, scale_in, gain_in, exchange.result())
+    grad_inputs = grad_hidden + grad_first
+
+    late = lax.all_to_all(grad_gain_in.reshape(devices, -1), "dp", 0, 0, tiled=True)
+    packed = jnp.concatenate([jnp.sum(late, axis=0), jnp.sum(early.value, axis=0)])
     attn_grad = mixer_result([first.parts(), second.parts()], wide, local_width, ring.around)
     return (
         result.value,

time: 773 us -> 722 us (0.934)
  waiting for transfers between devices: 221 us -> 184 us
  local copies, waits for them, and re-layouts: 78.8 us -> 61.5 us
    ppermute x40, waiting for transfers between devices: 144 us -> 102 us  [send(): return Box(lax.ppermute(value, 'dp', self.hops[turn]))]
    ppermute x11 -> x12, waiting for transfers between devices: 61.7 us -> 74.5 us  [swap_tensor(): return lax.ppermute(value, 'tensor', [(0, 1), (1, 0)])]
    all_to_all x1, waiting for transfers between devices: 13 us -> 0.24 us  [body(): small = Box(lax.all_to_all(small, 'dp', 0, 0, tiled=True))]
    unnamed x194 -> x153, local copies, waits for them, and re-layouts: 37.3 us -> 25.2 us
    pallas_call x3 -> x4, Pallas kernels: 53.1 us -> 53.8 us  [mixer_backward(): pl.pallas_call(functools.partial(backward_kernel, heads, passes, first),...]
  transfers between devices with their start and end apart: 68 -> 70, of which waited for: 32 -> 34; matrix products, arithmetic and copies ran while one was open for 13% -> 13% of each run, Pallas kernels for 39% -> 41%
where the time goes in v4:
time: 722 us; the launch traced here: 712 us
  Pallas kernels  331 us (46%)
  waiting for transfers between devices  184 us (25%)
  starting transfers between devices  72.3 us (10%)
  local copies, waits for them, and re-layouts  61.5 us (9%)
  other arithmetic  46.1 us (6%)
  between operations  15.3 us (2%)
    pallas_call x35, Pallas kernels, call(): pl.pallas_call(kernel, grid_spec=pltpu.PrefetchScalarGridSpec(num_scalar_...  243 us
    ppermute x40, waiting for transfers between devices, send(): return Box(lax.ppermute(value, 'dp', self.hops[turn]))  102 us
    ppermute x12, waiting for transfers between devices, swap_tensor(): return lax.ppermute(value, 'tensor', [(0, 1), (1, 0)])  74.5 us
    pallas_call x4, Pallas kernels, mixer_backward(): pl.pallas_call(functools.partial(backward_kernel, heads, passes, first),...  53.8 us
    ppermute x40, starting transfers between devices, send(): return Box(lax.ppermute(value, 'dp', self.hops[turn]))  43.5 us
    pallas_call x1, Pallas kernels, mixer_forward(): pl.pallas_call(functools.partial(forward_kernel, heads, passes, first), g...  29.7 us
    unnamed x153, local copies, waits for them, and re-layouts  25.2 us
  transfers between devices with their start and end apart: 70, of which 34 were waited for; matrix products, arithmetic and copies ran while one was open for 13% of the time, Pallas kernels for 41%

profile of v4, /device:TPU:0, one launch (start us, length us, event | category | flops | bytes accessed | tf_op | source)
XLA Modules:
  0.0 712.5 jit_solution(6070960529169966994)
XLA Ops:
  7.2 4.6 pack_mixer.1.refs_0_.refs_1_.refs_4_
  14.8 23.3 %collective-permute-done.refs_7_.refs_8_.refs_11_ = bf16[128,4096]{1,0:T(8,128)(2,1)S(1)} collective-permute-done((bf16[128,4096]{1,0:T(8,128)(2,1)}, bf16[128,4096]{1,0:T(8,128)(2,1)S(1)}, u32[]{:S(2)}, u32[]{:S(2)}) %collective-permute-start) | collective-permute-done | bytes 1048608 | tf_op jit(solution)/shard_map/ring_send/ppermute | solution.py:897
  49.3 4.9 all-to-all-start
  77.7 15.4 %collective-permute-done.7.refs_5_.refs_6_.refs_9_ = bf16[128,4096]{1,0:T(8,128)(2,1)} collective-permute-done((bf16[128,4096]{1,0:T(8,128)(2,1)}, bf16[128,4096]{1,0:T(8,128)(2,1)}, u32[]{:S(2)}, u32[]{:S(2)}) %collective-permute-start.7) | collective-permute-done | bytes 1048608 | tf_op jit(solution)/shard_map/ring_send/ppermute | solution.py:897
  106.1 20.7 %collective-permute-done.11 = bf16[128,2048]{1,0:T(8,128)(2,1)} collective-permute-done((bf16[128,2048]{1,0:T(8,128)(2,1)}, bf16[128,2048]{1,0:T(8,128)(2,1)}, u32[]{:S(2)}, u32[]{:S(2)}) %collective-permute-start.11) | collective-permute-done | bytes 524320 | tf_op jit(solution)/shard_map/ring_send/ppermute | solution.py:897
  134.1 14.2 %times_rows.2.proj_ref = f32[512,3072]{1,0:T(8,128)} custom-call(s32[16]{0:T(128)S(1)} %pad_add_fusion.table_ref, bf16[512,2048]{1,0:T(8,128)(2,1)} %copy-done.4, bf16[128,4096]{1,0:T(8,128)(2,1)S(1)} %copy-done.15, bf16[128,4096]{1,0:T(8,128)(2,1)S(1)} %copy-done.19, bf16[128,4096]{1,0:T(8,128)(2,1)S(1)} %copy-done.22, ...), custom_call_target="tpu_custom_call" | custom-call | flops 1000 | bytes 1000 | tf_op jit(solution)/shard_map/times_rows/pallas_call | solution.py:381
  151.4 29.7 %mixer_forward.1 = (bf16[512,1024]{1,0:T(8,128)(2,1)}, f32[512,1024]{1,0:T(8,128)}, f32[512,1024]{1,0:T(8,128)}, f32[512,1024]{1,0:T(8,128)}, f32[512,1024]{1,0:T(8,128)}) custom-call(f32[512,3072]{1,0:T(8,128)} %times_rows.2.proj_ref, f32[512,128]{1,0:T(8,128)} %fusion.16.beta_ref, f32[3,4,1024]{2,1,0:T(4,128)} %reshape.212.conv_ref, ...), custom_call_target="tpu_custom_call" | custom-call | flops 1000 | bytes 1000 | tf_op jit(solution)/shard_map/mixer_forward/pallas_call | solution.py:334
  182.5 8.2 %times_turned.2 = bf16[512,2048]{1,0:T(8,128)(2,1)} custom-call(s32[16]{0:T(128)S(1)} %pad_add_fusion.table_ref, bf16[512,1024]{1,0:T(8,128)(2,1)S(1)} %copy-done.26, bf16[128,4096]{1,0:T(8,128)(2,1)S(1)} %copy-done.15, bf16[128,4096]{1,0:T(8,128)(2,1)S(1)} %copy-done.19, bf16[128,4096]{1,0:T(8,128)(2,1)} %copy-done.21, ...), custom_call_target="tpu_custom_call" | custom-call | flops 1000 | bytes 1000 | tf_op jit(solution)/shard_map/times_turned/pallas_call | solution.py:381
  192.4 46.2 %collective-permute-done.17 = bf16[512,2048]{1,0:T(8,128)(2,1)S(1)} collective-permute-done((bf16[512,2048]{1,0:T(8,128)(2,1)}, bf16[512,2048]{1,0:T(8,128)(2,1)S(1)}, u32[]{:S(2)}, u32[]{:S(2)}) %collective-permute-start.17) | collective-permute-done | bytes 2097184 | tf_op jit(solution)/shard_map/tensor_swap/ppermute | solution.py:1011
  238.5 5.2 multiply_reduce_fusion.2
  243.7 3.9 multiply_convert_fusion.normed_ref.refs_0_
  249.4 20.5 %gated_units.2.refs_2_.refs_3_.refs_0_.refs_1_ = bf16[3,512,2048]{2,1,0:T(8,128)(2,1)} custom-call(s32[16]{0:T(128)S(1)} %pad_add_fusion.table_ref, bf16[512,2048]{1,0:T(8,128)(2,1)S(1)} %copy-done.10, bf16[512,2048]{1,0:T(8,128)(2,1)} %refs_1_.7, bf16[2048,6144]{1,0:T(8,128)(2,1)} %all-gather.3.cloned.1.call-done.gate_ref.up_ref.down_ref.refs_2_.refs_3_, ...), custom_call_target="tpu_custom_call" | custom-call | flops 1000 | bytes 1000 | tf_op jit(solution)/shard_map/gated_units/pallas_call | solution.py:381
  272.7 11.5 %weight_grads.8 = bf16[8,128,6144]{2,1,0:T(8,128)(2,1)} custom-call(s32[2]{0:T(128)S(1)} %pad_add_fusion.1.table_ref, bf16[512,2048]{1,0:T(8,128)(2,1)S(1)} %copy-done.11, bf16[512,2048]{1,0:T(8,128)(2,1)S(1)} %copy-done.8, bf16[3,512,2048]{2,1,0:T(8,128)(2,1)S(1)} %copy-done.2, bf16[3,512,2048]{2,1,0:T(8,128)(2,1)S(1)} %copy-done.2), custom_call_target="tpu_custom_call" | custom-call | flops 1000 | bytes 1000 | tf_op jit(solution)/shard_map/weight_grads/pallas_call | solution.py:381
  284.3 16.3 %units_turned.3.refs_4_ = f32[512,2048]{1,0:T(8,128)} custom-call(s32[16]{0:T(128)S(1)} %pad_add_fusion.table_ref, bf16[3,512,2048]{2,1,0:T(8,128)(2,1)} %gated_units.2.refs_2_.refs_3_.refs_0_.refs_1_, bf16[3,512,2048]{2,1,0:T(8,128)(2,1)} %gated_units.2.refs_2_.refs_3_.refs_0_.refs_1_, ...), custom_call_target="tpu_custom_call" | custom-call | flops 1000 | bytes 1000 | tf_op jit(solution)/shard_map/units_turned/pallas_call | solution.py:381
  303.8 14.4 %weight_grads.9.refs_0_.refs_1_ = bf16[8,128,6144]{2,1,0:T(8,128)(2,1)} custom-call(s32[2]{0:T(128)S(1)} %pad_add_fusion.1.table_ref, bf16[512,2048]{1,0:T(8,128)(2,1)S(1)} %copy-done.11, bf16[512,2048]{1,0:T(8,128)(2,1)S(1)} %copy-done.8, bf16[3,512,2048]{2,1,0:T(8,128)(2,1)S(1)} %bitcast.39, bf16[3,512,2048]{2,1,0:T(8,128)(2,1)S(1)} %bitcast.39, ...), custom_call_target="tpu_custom_call" | custom-call | flops 1000 | bytes 1000 | tf_op jit(solution)/shard_map/weight_grads/pallas_call | solution.py:381
  323.3 10.3 %gated_units.3.refs_0_.refs_1_.refs_2_.refs_3_ = bf16[3,512,768]{2,1,0:T(8,128)(2,1)} custom-call(s32[16]{0:T(128)S(1)} %pad_add_fusion.table_ref, bf16[512,2048]{1,0:T(8,128)(2,1)S(1)} %copy-done.12, bf16[512,2048]{1,0:T(8,128)(2,1)} %refs_1_.7, bf16[2048,2304]{1,0:T(8,128)(2,1)} %all-gather.5.cloned.1.call-done.gate_ref.up_ref.down_ref.refs_2_.refs_3_, ...), custom_call_target="tpu_custom_call" | custom-call | flops 1000 | bytes 1000 | tf_op jit(solution)/shard_map/gated_units/pallas_call | solution.py:381
  333.6 9.8 %units_turned.4 = bf16[512,2048]{1,0:T(8,128)(2,1)S(1)} custom-call(s32[16]{0:T(128)S(1)} %pad_add_fusion.table_ref, bf16[3,512,768]{2,1,0:T(8,128)(2,1)} %gated_units.3.refs_0_.refs_1_.refs_2_.refs_3_, bf16[3,512,768]{2,1,0:T(8,128)(2,1)} %gated_units.3.refs_0_.refs_1_.refs_2_.refs_3_, ...), custom_call_target="tpu_custom_call" | custom-call | flops 1000 | bytes 1000 | tf_op jit(solution)/shard_map/units_turned/pallas_call | solution.py:381
  346.0 5.1 ring_hop.17
  351.1 5.6 weight_grads.10
  365.8 12.0 %units_turned.5 = bf16[512,2048]{1,0:T(8,128)(2,1)S(1)} custom-call(s32[16]{0:T(128)S(1)} %pad_add_fusion.table_ref, bf16[3,512,2048]{2,1,0:T(8,128)(2,1)} %gated_units.2.refs_2_.refs_3_.refs_0_.refs_1_, bf16[3,512,768]{2,1,0:T(8,128)(2,1)} %gated_units.3.refs_0_.refs_1_.refs_2_.refs_3_, ...), custom_call_target="tpu_custom_call" | custom-call | flops 1000 | bytes 1000 | tf_op jit(solution)/shard_map/units_turned/pallas_call | solution.py:381
  377.8 4.6 collective-permute-done.24
  382.4 13.6 %collective-permute-done.22 = bf16[160,2048]{1,0:T(8,128)(2,1)} collective-permute-done((bf16[160,2048]{1,0:T(8,128)(2,1)}, bf16[160,2048]{1,0:T(8,128)(2,1)}, u32[]{:S(2)}, u32[]{:S(2)}) %collective-permute-start.22) | collective-permute-done | bytes 655392 | tf_op jit(solution)/shard_map/tensor_swap/ppermute | solution.py:1011
  396.0 6.2 weight_grads.11.refs_0_.refs_1_.refs_3_
  402.2 5.6 multiply_reduce_fusion
  407.8 4.4 ring_hop.18
  414.3 7.1 %fusion.18 = (bf16[512,2048]{1,0:T(8,128)(2,1)}, f32[512,2048]{1,0:T(8,128)}) fusion(f32[512]{0:T(512)S(1)} %broadcast_multiply_fusion.1, f32[512,2048]{1,0:T(8,128)} %get-tuple-element.528, f32[512]{0:T(512)S(1)} %get-tuple-element.541, bf16[192,2048]{1,0:T(8,128)(2,1)} %collective-permute-done.24, bf16[160,2048]{1,0:T(8,128)(2,1)} %collective-permute-done.22, ...), kind=kLoop, calls=%fused_computation.64 | loop fusion | flops 16777216 | bytes 16791552 | tf_op jit(solution)/shard_map/convert_element_type | solution.py:1174
  421.4 7.8 %times_rows.3.gmix_ref = f32[512,1024]{1,0:T(8,128)} custom-call(s32[16]{0:T(128)S(1)} %pad_add_fusion.table_ref, bf16[512,2048]{1,0:T(8,128)(2,1)} %get-tuple-element.293.left_ref.refs_2_, bf16[128,4096]{1,0:T(8,128)(2,1)S(1)} %copy-done.15, bf16[128,4096]{1,0:T(8,128)(2,1)S(1)} %copy-done.20, bf16[128,4096]{1,0:T(8,128)(2,1)S(1)} %copy-done.23, ...), custom_call_target="tpu_custom_call" | custom-call | flops 1000 | bytes 1000 | tf_op jit(solution)/shard_map/times_rows/pallas_call | solution.py:381
  432.0 13.4 %mixer_backward.4 = (bf16[512,768]{1,0:T(8,128)(2,1)S(1)}, f32[512,128]{1,0:T(8,128)S(1)}, f32[3,4,256]{2,1,0:T(4,128)S(1)}, f32[1,128]{1,0:T(1,128)S(1)}) custom-call(f32[512,3072]{1,0:T(8,128)} %times_rows.2.proj_ref, f32[512,128]{1,0:T(8,128)S(1)} %copy-done.25, f32[3,4,1024]{2,1,0:T(4,128)S(1)} %copy-done.29, f32[1,128]{1,0:T(1,128)S(1)} %copy-done.38, ...), custom_call_target="tpu_custom_call" | custom-call | flops 1000 | bytes 1000 | tf_op jit(solution)/shard_map/mixer_backward/pallas_call | solution.py:359
  449.5 5.1 ring_hop.19
  458.5 13.5 %mixer_backward.5 = (bf16[512,768]{1,0:T(8,128)(2,1)S(1)}, f32[512,128]{1,0:T(8,128)S(1)}, f32[3,4,256]{2,1,0:T(4,128)S(1)}, f32[1,128]{1,0:T(1,128)S(1)}) custom-call(f32[512,3072]{1,0:T(8,128)} %times_rows.2.proj_ref, f32[512,128]{1,0:T(8,128)S(1)} %copy-done.25, f32[3,4,1024]{2,1,0:T(4,128)S(1)} %copy-done.29, f32[1,128]{1,0:T(1,128)S(1)} %copy-done.38, ...), custom_call_target="tpu_custom_call" | custom-call | flops 1000 | bytes 1000 | tf_op jit(solution)/shard_map/mixer_backward/pallas_call | solution.py:359
  472.0 8.7 %weight_grads.12 = bf16[8,128,2560]{2,1,0:T(8,128)(2,1)} custom-call(s32[2]{0:T(128)S(1)} %pad_add_fusion.1.table_ref, bf16[512,2048]{1,0:T(8,128)(2,1)S(1)} %copy-done.5, bf16[512,2048]{1,0:T(8,128)(2,1)S(1)} %copy-done.5, bf16[512,2048]{1,0:T(8,128)(2,1)S(1)} %copy-done.14, bf16[512,768]{1,0:T(8,128)(2,1)S(1)} %get-tuple-element.378.refs_3_.refs_0_, ...), custom_call_target="tpu_custom_call" | custom-call | flops 1000 | bytes 1000 | tf_op jit(solution)/shard_map/weight_grads/pallas_call | solution.py:381
  480.7 8.8 %collective-permute-done.33.refs_1_ = bf16[128,6144]{1,0:T(8,128)(2,1)S(1)} collective-permute-done((bf16[128,6144]{1,0:T(8,128)(2,1)}, bf16[128,6144]{1,0:T(8,128)(2,1)S(1)}, u32[]{:S(2)}, u32[]{:S(2)}) %collective-permute-start.33) | collective-permute-done | bytes 1572896 | tf_op jit(solution)/shard_map/ring_send/ppermute | solution.py:897
  497.3 13.4 %mixer_backward.6 = (bf16[512,768]{1,0:T(8,128)(2,1)S(1)}, f32[512,128]{1,0:T(8,128)S(1)}, f32[3,4,256]{2,1,0:T(4,128)S(1)}, f32[1,128]{1,0:T(1,128)S(1)}) custom-call(f32[512,3072]{1,0:T(8,128)} %times_rows.2.proj_ref, f32[512,128]{1,0:T(8,128)S(1)} %copy-done.25, f32[3,4,1024]{2,1,0:T(4,128)S(1)} %copy-done.29, f32[1,128]{1,0:T(1,128)S(1)} %copy-done.38, ...), custom_call_target="tpu_custom_call" | custom-call | flops 1000 | bytes 1000 | tf_op jit(solution)/shard_map/mixer_backward/pallas_call | solution.py:359
  520.6 9.9 %weight_grads.13.refs_0_.refs_1_ = bf16[8,128,2560]{2,1,0:T(8,128)(2,1)S(1)} custom-call(s32[2]{0:T(128)S(1)} %pad_add_fusion.1.table_ref, bf16[512,2048]{1,0:T(8,128)(2,1)S(1)} %copy-done.5, bf16[512,2048]{1,0:T(8,128)(2,1)S(1)} %copy-done.5, bf16[512,2048]{1,0:T(8,128)(2,1)S(1)} %copy-done.14, bf16[512,768]{1,0:T(8,128)(2,1)S(1)} %get-tuple-element.378.refs_3_.refs_0_, ...), custom_call_target="tpu_custom_call" | custom-call | flops 1000 | bytes 1000 | tf_op jit(solution)/shard_map/weight_grads/pallas_call | solution.py:381
  536.5 4.8 ring_hop.22
  545.4 13.4 %mixer_backward.7 = (bf16[512,768]{1,0:T(8,128)(2,1)S(1)}, f32[512,128]{1,0:T(8,128)S(1)}, f32[3,4,256]{2,1,0:T(4,128)S(1)}, f32[1,128]{1,0:T(1,128)S(1)}) custom-call(f32[512,3072]{1,0:T(8,128)} %times_rows.2.proj_ref, f32[512,128]{1,0:T(8,128)S(1)} %copy-done.25, f32[3,4,1024]{2,1,0:T(4,128)S(1)} %copy-done.29, f32[1,128]{1,0:T(1,128)S(1)} %copy-done.38, ...), custom_call_target="tpu_custom_call" | custom-call | flops 1000 | bytes 1000 | tf_op jit(solution)/shard_map/mixer_backward/pallas_call | solution.py:359
  573.8 4.5 weight_grads.14
  578.3 13.2 %times_turned.3 = bf16[512,2048]{1,0:T(8,128)(2,1)} custom-call(s32[16]{0:T(128)S(1)} %pad_add_fusion.table_ref, bf16[512,768]{1,0:T(8,128)(2,1)S(1)} %get-tuple-element.378.refs_3_.refs_0_, bf16[512,768]{1,0:T(8,128)(2,1)S(1)} %get-tuple-element.379.refs_4_.refs_1_, bf16[512,768]{1,0:T(8,128)(2,1)S(1)} %get-tuple-element.415.refs_2_, ...), custom_call_target="tpu_custom_call" | custom-call | flops 1000 | bytes 1000 | tf_op jit(solution)/shard_map/times_turned/pallas_call | solution.py:381
  591.5 4.5 collective-permute-done.46.refs_4_
  607.9 5.6 units_result.1
  617.5 3.9 collective-permute-done.51.refs_2_
  626.2 4.2 ring_hop.28
  644.6 6.1 collective-permute-done.55.refs_2_
  651.0 4.0 ring_hop.29
  657.8 5.3 all-to-all-start.2
  663.1 4.3 add_convert_fusion
  691.1 4.8 fusion.8
  700.8 4.6 mixer_result.1
  (367 shorter events, 210.1 us)
Async XLA Ops:
  11.8 26.3 %collective-permute-start = (bf16[128,4096]{1,0:T(8,128)(2,1)}, bf16[128,4096]{1,0:T(8,128)(2,1)S(1)}, u32[]{:S(2)}, u32[]{:S(2)}) collective-permute-start(bf16[128,4096]{1,0:T(8,128)(2,1)} %pack_mixer.1.refs_0_.refs_1_.refs_4_), channel_id=1, source_target_pairs={{0,8},{2,10},{8,16},{10,18},{16,24},{18,26},{24,28},{26,30},{28,20... | collective-permute-start | bytes 3145736 | tf_op jit(solution)/shard_map/ring_send/ppermute | solution.py:897
  14.8 24.8 %collective-permute-start.1 = (bf16[128,4096]{1,0:T(8,128)(2,1)}, bf16[128,4096]{1,0:T(8,128)(2,1)S(1)}, u32[]{:S(2)}, u32[]{:S(2)}) collective-permute-start(bf16[128,4096]{1,0:T(8,128)(2,1)} %pack_mixer.1.refs_0_.refs_1_.refs_4_), channel_id=1, source_target_pairs={{0,4},{2,6},{8,0},{10,2},{16,8},{18,10},{24,16},{26,18},{28,24},{3... | collective-permute-start | bytes 3145736 | tf_op jit(solution)/shard_map/ring_send/ppermute | solution.py:897
  14.8 24.8 %collective-permute-start.2 = (bf16[128,4096]{1,0:T(8,128)(2,1)}, bf16[128,4096]{1,0:T(8,128)(2,1)S(1)}, u32[]{:S(2)}, u32[]{:S(2)}) collective-permute-start(bf16[128,4096]{1,0:T(8,128)(2,1)} %pack_mixer.1.refs_0_.refs_1_.refs_4_), channel_id=1, source_target_pairs={{0,2},{2,0},{4,6},{6,4},{8,10},{10,8},{12,14},{14,12},{16,18},{18,... | collective-permute-start | bytes 3145736 | tf_op jit(solution)/shard_map/core_swap/ppermute | solution.py:901
  39.6 27.8 %collective-permute-start.3 = (bf16[128,4096]{1,0:T(8,128)(2,1)S(1)}, bf16[128,4096]{1,0:T(8,128)(2,1)}, u32[]{:S(2)}, u32[]{:S(2)}) collective-permute-start(bf16[128,4096]{1,0:T(8,128)(2,1)S(1)} %collective-permute-done.refs_7_.refs_8_.refs_11_), channel_id=1, source_target_pairs={{0,8},{2,10},{8,16},{10,18},{16,24},{18,26},{24,28},{26,30},{28,20... | collective-permute-start | bytes 3145736 | tf_op jit(solution)/shard_map/ring_send/ppermute | solution.py:897
  41.3 26.2 %collective-permute-start.4 = (bf16[128,4096]{1,0:T(8,128)(2,1)S(1)}, bf16[128,4096]{1,0:T(8,128)(2,1)S(1)}, u32[]{:S(2)}, u32[]{:S(2)}) collective-permute-start(bf16[128,4096]{1,0:T(8,128)(2,1)S(1)} %collective-permute-done.1.refs_1_.refs_2_.refs_5_), channel_id=1, source_target_pairs={{0,4},{2,6},{8,0},{10,2},{16,8},{18,10},{24,16},{26,18},{28,24},{3... | collective-permute-start | bytes 3145736 | tf_op jit(solution)/shard_map/ring_send/ppermute | solution.py:897
  41.7 25.7 %collective-permute-start.5 = (bf16[128,4096]{1,0:T(8,128)(2,1)S(1)}, bf16[128,4096]{1,0:T(8,128)(2,1)}, u32[]{:S(2)}, u32[]{:S(2)}) collective-permute-start(bf16[128,4096]{1,0:T(8,128)(2,1)S(1)} %collective-permute-done.refs_7_.refs_8_.refs_11_), channel_id=1, source_target_pairs={{0,2},{2,0},{4,6},{6,4},{8,10},{10,8},{12,14},{14,12},{16,18},{18,... | collective-permute-start | bytes 3145736 | tf_op jit(solution)/shard_map/core_swap/ppermute | solution.py:901
  41.7 25.7 %collective-permute-start.6 = (bf16[128,4096]{1,0:T(8,128)(2,1)S(1)}, bf16[128,4096]{1,0:T(8,128)(2,1)}, u32[]{:S(2)}, u32[]{:S(2)}) collective-permute-start(bf16[128,4096]{1,0:T(8,128)(2,1)S(1)} %collective-permute-done.1.refs_1_.refs_2_.refs_5_), channel_id=1, source_target_pairs={{0,2},{2,0},{4,6},{6,4},{8,10},{10,8},{12,14},{14,12},{16,18},{18,... | collective-permute-start | bytes 3145736 | tf_op jit(solution)/shard_map/core_swap/ppermute | solution.py:901
  49.3 18.0 %all-to-all-start = ((bf16[16,2,1028]{2,1,0:T(2,128)(2,1)}), bf16[16,2,1028]{2,1,0:T(2,128)(2,1)S(1)}, u32[]{:S(2)}, u32[]{:S(2)}) async-start(bf16[16,2,1028]{2,1,0:T(2,128)(2,1)} %reshape.224), calls=%async_computation | async-start | bytes 147456 | tf_op jit(solution)/shard_map/all_to_all | solution.py:1076
  54.2 193.5 %all-gather.3.cloned.1.call-start = ((), (), s32[]{:S(2)}) async-start(), calls=%async_computation.3 | async-start | bytes 26738688 | tf_op jit(solution)/shard_map/all_gather | solution.py:1105
  67.5 25.6 %collective-permute-start.7 = (bf16[128,4096]{1,0:T(8,128)(2,1)}, bf16[128,4096]{1,0:T(8,128)(2,1)}, u32[]{:S(2)}, u32[]{:S(2)}) collective-permute-start(bf16[128,4096]{1,0:T(8,128)(2,1)} %collective-permute-done.3.refs_6_.refs_7_.refs_10_), channel_id=1, source_target_pairs={{0,8},{2,10},{8,16},{10,18},{16,24},{18,26},{24,28},{26,30},{28,20... | collective-permute-start | bytes 3145736 | tf_op jit(solution)/shard_map/ring_send/ppermute | solution.py:897
  69.2 25.7 %collective-permute-start.9 = (bf16[128,4096]{1,0:T(8,128)(2,1)}, bf16[128,4096]{1,0:T(8,128)(2,1)}, u32[]{:S(2)}, u32[]{:S(2)}) collective-permute-start(bf16[128,4096]{1,0:T(8,128)(2,1)} %collective-permute-done.3.refs_6_.refs_7_.refs_10_), channel_id=1, source_target_pairs={{0,2},{2,0},{4,6},{6,4},{8,10},{10,8},{12,14},{14,12},{16,18},{18,... | collective-permute-start | bytes 3145736 | tf_op jit(solution)/shard_map/core_swap/ppermute | solution.py:901
  69.2 25.7 %collective-permute-start.8 = (bf16[128,4096]{1,0:T(8,128)(2,1)S(1)}, bf16[128,4096]{1,0:T(8,128)(2,1)}, u32[]{:S(2)}, u32[]{:S(2)}) collective-permute-start(bf16[128,4096]{1,0:T(8,128)(2,1)S(1)} %collective-permute-done.4.refs_2_.refs_3_.refs_6_), channel_id=1, source_target_pairs={{0,4},{2,6},{8,0},{10,2},{16,8},{18,10},{24,16},{26,18},{28,24},{3... | collective-permute-start | bytes 3145736 | tf_op jit(solution)/shard_map/ring_send/ppermute | solution.py:897
  69.5 25.3 %collective-permute-start.10 = (bf16[128,4096]{1,0:T(8,128)(2,1)S(1)}, bf16[128,4096]{1,0:T(8,128)(2,1)}, u32[]{:S(2)}, u32[]{:S(2)}) collective-permute-start(bf16[128,4096]{1,0:T(8,128)(2,1)S(1)} %collective-permute-done.4.refs_2_.refs_3_.refs_6_), channel_id=1, source_target_pairs={{0,2},{2,0},{4,6},{6,4},{8,10},{10,8},{12,14},{14,12},{16,18},{18,... | collective-permute-start | bytes 3145736 | tf_op jit(solution)/shard_map/core_swap/ppermute | solution.py:901
  97.5 225.8 %all-gather.5.cloned.1.call-start = ((), (), s32[]{:S(2)}) async-start(), calls=%async_computation.4 | async-start | bytes 10027008 | tf_op jit(solution)/shard_map/all_gather | solution.py:1111
  97.6 31.8 %collective-permute-start.13 = (bf16[128,4096]{1,0:T(8,128)(2,1)}, bf16[128,4096]{1,0:T(8,128)(2,1)}, u32[]{:S(2)}, u32[]{:S(2)}) collective-permute-start(bf16[128,4096]{1,0:T(8,128)(2,1)} %collective-permute-done.7.refs_5_.refs_6_.refs_9_), channel_id=1, source_target_pairs={{0,2},{2,0},{4,6},{6,4},{8,10},{10,8},{12,14},{14,12},{16,18},{18,... | collective-permute-start | bytes 3145736 | tf_op jit(solution)/shard_map/core_swap/ppermute | solution.py:901
  97.7 31.7 %collective-permute-start.14 = (bf16[128,4096]{1,0:T(8,128)(2,1)}, bf16[128,4096]{1,0:T(8,128)(2,1)}, u32[]{:S(2)}, u32[]{:S(2)}) collective-permute-start(bf16[128,4096]{1,0:T(8,128)(2,1)} %collective-permute-done.8.refs_3_.refs_4_.refs_7_), channel_id=1, source_target_pairs={{0,2},{2,0},{4,6},{6,4},{8,10},{10,8},{12,14},{14,12},{16,18},{18,... | collective-permute-start | bytes 3145736 | tf_op jit(solution)/shard_map/core_swap/ppermute | solution.py:901
  101.9 24.9 %collective-permute-start.11 = (bf16[128,2048]{1,0:T(8,128)(2,1)}, bf16[128,2048]{1,0:T(8,128)(2,1)}, u32[]{:S(2)}, u32[]{:S(2)}) collective-permute-start(bf16[128,2048]{1,0:T(8,128)(2,1)} %slice.86), channel_id=1, source_target_pairs={{0,8},{2,10},{8,16},{10,18},{16,24},{18,26},{24,28},{26,30},{28,20... | collective-permute-start | bytes 1572872 | tf_op jit(solution)/shard_map/ring_send/ppermute | solution.py:897
  103.4 25.9 %collective-permute-start.12 = (bf16[128,2048]{1,0:T(8,128)(2,1)}, bf16[128,2048]{1,0:T(8,128)(2,1)}, u32[]{:S(2)}, u32[]{:S(2)}) collective-permute-start(bf16[128,2048]{1,0:T(8,128)(2,1)} %slice.87), channel_id=1, source_target_pairs={{0,4},{2,6},{8,0},{10,2},{16,8},{18,10},{24,16},{26,18},{28,24},{3... | collective-permute-start | bytes 1572872 | tf_op jit(solution)/shard_map/ring_send/ppermute | solution.py:897
  190.7 47.8 %collective-permute-start.17 = (bf16[512,2048]{1,0:T(8,128)(2,1)}, bf16[512,2048]{1,0:T(8,128)(2,1)S(1)}, u32[]{:S(2)}, u32[]{:S(2)}) collective-permute-start(bf16[512,2048]{1,0:T(8,128)(2,1)} %times_turned.2), channel_id=1, source_target_pairs={{0,1},{1,0},{2,3},{3,2},{4,5},{5,4},{6,7},{7,6},{8,9},{9,8},{10,11... | collective-permute-start | bytes 6291464 | tf_op jit(solution)/shard_map/tensor_swap/ppermute | solution.py:1011
  284.3 19.5 %collective-permute-start.18 = (bf16[8,128,6144]{2,1,0:T(8,128)(2,1)}, bf16[8,128,6144]{2,1,0:T(8,128)(2,1)}, u32[]{:S(2)}, u32[]{:S(2)}) collective-permute-start(bf16[8,128,6144]{2,1,0:T(8,128)(2,1)} %weight_grads.8), channel_id=1, source_target_pairs={{0,2},{2,0},{4,6},{6,4},{8,10},{10,8},{12,14},{14,12},{16,18},{18,... | collective-permute-start | bytes 37748744 | tf_op jit(solution)/shard_map/core_swap/ppermute | solution.py:901
  321.3 22.1 %collective-permute-start.19 = (bf16[128,3072]{1,0:T(8,128)(2,1)}, bf16[128,3072]{1,0:T(8,128)(2,1)}, u32[]{:S(2)}, u32[]{:S(2)}) collective-permute-start(bf16[128,3072]{1,0:T(8,128)(2,1)} %get-tuple-element.276), channel_id=1, source_target_pairs={{0,8},{2,10},{8,16},{10,18},{16,24},{18,26},{24,28},{26,30},{28,20... | collective-permute-start | bytes 2359304 | tf_op jit(solution)/shard_map/ring_send/ppermute | solution.py:897
  322.7 20.7 %collective-permute-start.20 = (bf16[128,3072]{1,0:T(8,128)(2,1)}, bf16[128,3072]{1,0:T(8,128)(2,1)}, u32[]{:S(2)}, u32[]{:S(2)}) collective-permute-start(bf16[128,3072]{1,0:T(8,128)(2,1)} %get-tuple-element.277), channel_id=1, source_target_pairs={{0,4},{2,6},{8,0},{10,2},{16,8},{18,10},{24,16},{26,18},{28,24},{3... | collective-permute-start | bytes 2359304 | tf_op jit(solution)/shard_map/ring_send/ppermute | solution.py:897
  360.7 35.3 %collective-permute-start.23 = (bf16[8,128,2304]{2,1,0:T(8,128)(2,1)}, bf16[8,128,2304]{2,1,0:T(8,128)(2,1)}, u32[]{:S(2)}, u32[]{:S(2)}) collective-permute-start(bf16[8,128,2304]{2,1,0:T(8,128)(2,1)} %weight_grads.10), channel_id=1, source_target_pairs={{0,2},{2,0},{4,6},{6,4},{8,10},{10,8},{12,14},{14,12},{16,18},{18,... | collective-permute-start | bytes 14155784 | tf_op jit(solution)/shard_map/core_swap/ppermute | solution.py:901
  361.7 20.7 %collective-permute-start.24 = (bf16[192,2048]{1,0:T(8,128)(2,1)}, bf16[192,2048]{1,0:T(8,128)(2,1)}, u32[]{:S(2)}, u32[]{:S(2)}) collective-permute-start(bf16[192,2048]{1,0:T(8,128)(2,1)} %slice.91), channel_id=1, source_target_pairs={{0,1},{1,0},{2,3},{3,2},{4,5},{5,4},{6,7},{7,6},{8,9},{9,8},{10,11... | collective-permute-start | bytes 2359304 | tf_op jit(solution)/shard_map/tensor_swap/ppermute | solution.py:1011
  363.1 44.7 %collective-permute-start.27 = (bf16[128,6144]{1,0:T(8,128)(2,1)S(1)}, bf16[128,6144]{1,0:T(8,128)(2,1)}, u32[]{:S(2)}, u32[]{:S(2)}) collective-permute-start(bf16[128,6144]{1,0:T(8,128)(2,1)S(1)} %get-tuple-element.294), channel_id=1, source_target_pairs={{0,8},{2,10},{8,16},{10,18},{16,24},{18,26},{24,28},{26,30},{28,20... | collective-permute-start | bytes 4718600 | tf_op jit(solution)/shard_map/ring_send/ppermute | solution.py:897
  364.6 43.2 %collective-permute-start.28 = (bf16[128,6144]{1,0:T(8,128)(2,1)}, bf16[128,6144]{1,0:T(8,128)(2,1)}, u32[]{:S(2)}, u32[]{:S(2)}) collective-permute-start(bf16[128,6144]{1,0:T(8,128)(2,1)} %get-tuple-element.295), channel_id=1, source_target_pairs={{0,4},{2,6},{8,0},{10,2},{16,8},{18,10},{24,16},{26,18},{28,24},{3... | collective-permute-start | bytes 4718600 | tf_op jit(solution)/shard_map/ring_send/ppermute | solution.py:897
  365.1 30.8 %collective-permute-start.22 = (bf16[160,2048]{1,0:T(8,128)(2,1)}, bf16[160,2048]{1,0:T(8,128)(2,1)}, u32[]{:S(2)}, u32[]{:S(2)}) collective-permute-start(bf16[160,2048]{1,0:T(8,128)(2,1)} %get-tuple-element.536), channel_id=1, source_target_pairs={{0,1},{1,0},{2,3},{3,2},{4,5},{5,4},{6,7},{7,6},{8,9},{9,8},{10,11... | collective-permute-start | bytes 1966088 | tf_op jit(solution)/shard_map/tensor_swap/ppermute | solution.py:1011
  412.2 36.1 %collective-permute-start.29 = (bf16[128,6144]{1,0:T(8,128)(2,1)S(1)}, bf16[128,6144]{1,0:T(8,128)(2,1)}, u32[]{:S(2)}, u32[]{:S(2)}) collective-permute-start(bf16[128,6144]{1,0:T(8,128)(2,1)S(1)} %get-tuple-element.301), channel_id=1, source_target_pairs={{0,8},{2,10},{8,16},{10,18},{16,24},{18,26},{24,28},{26,30},{28,20... | collective-permute-start | bytes 4718600 | tf_op jit(solution)/shard_map/ring_send/ppermute | solution.py:897
  413.7 35.8 %collective-permute-start.30 = (bf16[128,6144]{1,0:T(8,128)(2,1)S(1)}, bf16[128,6144]{1,0:T(8,128)(2,1)}, u32[]{:S(2)}, u32[]{:S(2)}) collective-permute-start(bf16[128,6144]{1,0:T(8,128)(2,1)S(1)} %get-tuple-element.302), channel_id=1, source_target_pairs={{0,4},{2,6},{8,0},{10,2},{16,8},{18,10},{24,16},{26,18},{28,24},{3... | collective-permute-start | bytes 4718600 | tf_op jit(solution)/shard_map/ring_send/ppermute | solution.py:897
  454.6 35.0 %collective-permute-start.33 = (bf16[128,6144]{1,0:T(8,128)(2,1)}, bf16[128,6144]{1,0:T(8,128)(2,1)S(1)}, u32[]{:S(2)}, u32[]{:S(2)}) collective-permute-start(bf16[128,6144]{1,0:T(8,128)(2,1)} %get-tuple-element.318), channel_id=1, source_target_pairs={{0,8},{2,10},{8,16},{10,18},{16,24},{18,26},{24,28},{26,30},{28,20... | collective-permute-start | bytes 4718600 | tf_op jit(solution)/shard_map/ring_send/ppermute | solution.py:897
  456.1 35.0 %collective-permute-start.34 = (bf16[128,6144]{1,0:T(8,128)(2,1)S(1)}, bf16[128,6144]{1,0:T(8,128)(2,1)}, u32[]{:S(2)}, u32[]{:S(2)}) collective-permute-start(bf16[128,6144]{1,0:T(8,128)(2,1)S(1)} %get-tuple-element.319), channel_id=1, source_target_pairs={{0,4},{2,6},{8,0},{10,2},{16,8},{18,10},{24,16},{26,18},{28,24},{3... | collective-permute-start | bytes 4718600 | tf_op jit(solution)/shard_map/ring_send/ppermute | solution.py:897
  457.0 23.7 %collective-permute-start.32 = (bf16[128,2048]{1,0:T(8,128)(2,1)}, bf16[128,2048]{1,0:T(8,128)(2,1)S(1)}, u32[]{:S(2)}, u32[]{:S(2)}) collective-permute-start(bf16[128,2048]{1,0:T(8,128)(2,1)} %get-tuple-element.531), channel_id=1, source_target_pairs={{0,1},{1,0},{2,3},{3,2},{4,5},{5,4},{6,7},{7,6},{8,9},{9,8},{10,11... | collective-permute-start | bytes 1572872 | tf_op jit(solution)/shard_map/tensor_swap/ppermute | solution.py:1011
  491.0 20.5 %collective-permute-start.35 = (bf16[8,128,2560]{2,1,0:T(8,128)(2,1)}, bf16[8,128,2560]{2,1,0:T(8,128)(2,1)}, u32[]{:S(2)}, u32[]{:S(2)}) collective-permute-start(bf16[8,128,2560]{2,1,0:T(8,128)(2,1)} %weight_grads.12), channel_id=1, source_target_pairs={{0,2},{2,0},{4,6},{6,4},{8,10},{10,8},{12,14},{14,12},{16,18},{18,... | collective-permute-start | bytes 15728648 | tf_op jit(solution)/shard_map/core_swap/ppermute | solution.py:901
  491.0 20.4 %collective-permute-start.31 = (bf16[128,2048]{1,0:T(8,128)(2,1)}, bf16[128,2048]{1,0:T(8,128)(2,1)S(1)}, u32[]{:S(2)}, u32[]{:S(2)}) collective-permute-start(bf16[128,2048]{1,0:T(8,128)(2,1)} %get-tuple-element.532), channel_id=1, source_target_pairs={{0,1},{1,0},{2,3},{3,2},{4,5},{5,4},{6,7},{7,6},{8,9},{9,8},{10,11... | collective-permute-start | bytes 1572872 | tf_op jit(solution)/shard_map/tensor_swap/ppermute | solution.py:1011
  541.3 21.0 %collective-permute-start.42 = (bf16[128,2304]{1,0:T(8,128)(2,1)}, bf16[128,2304]{1,0:T(8,128)(2,1)S(1)}, u32[]{:S(2)}, u32[]{:S(2)}) collective-permute-start(bf16[128,2304]{1,0:T(8,128)(2,1)} %get-tuple-element.351), channel_id=1, source_target_pairs={{0,8},{2,10},{8,16},{10,18},{16,24},{18,26},{24,28},{26,30},{28,20... | collective-permute-start | bytes 1769480 | tf_op jit(solution)/shard_map/ring_send/ppermute | solution.py:897
  541.9 20.4 %collective-permute-start.43 = (bf16[128,2304]{1,0:T(8,128)(2,1)S(1)}, bf16[128,2304]{1,0:T(8,128)(2,1)S(1)}, u32[]{:S(2)}, u32[]{:S(2)}) collective-permute-start(bf16[128,2304]{1,0:T(8,128)(2,1)S(1)} %get-tuple-element.352), channel_id=1, source_target_pairs={{0,4},{2,6},{8,0},{10,2},{16,8},{18,10},{24,16},{26,18},{28,24},{3... | collective-permute-start | bytes 1769480 | tf_op jit(solution)/shard_map/ring_send/ppermute | solution.py:897
  543.3 18.8 %collective-permute-start.40 = (bf16[128,1280]{1,0:T(8,128)(2,1)}, bf16[128,1280]{1,0:T(8,128)(2,1)S(1)}, u32[]{:S(2)}, u32[]{:S(2)}) collective-permute-start(bf16[128,1280]{1,0:T(8,128)(2,1)} %get-tuple-element.349), channel_id=1, source_target_pairs={{0,8},{2,10},{8,16},{10,18},{16,24},{18,26},{24,28},{26,30},{28,20... | collective-permute-start | bytes 983048 | tf_op jit(solution)/shard_map/ring_send/ppermute | solution.py:897
  543.9 18.3 %collective-permute-start.41 = (bf16[128,1280]{1,0:T(8,128)(2,1)}, bf16[128,1280]{1,0:T(8,128)(2,1)S(1)}, u32[]{:S(2)}, u32[]{:S(2)}) collective-permute-start(bf16[128,1280]{1,0:T(8,128)(2,1)} %get-tuple-element.350), channel_id=1, source_target_pairs={{0,4},{2,6},{8,0},{10,2},{16,8},{18,10},{24,16},{26,18},{28,24},{3... | collective-permute-start | bytes 983048 | tf_op jit(solution)/shard_map/ring_send/ppermute | solution.py:897
  569.2 27.9 %collective-permute-start.44 = (bf16[128,2560]{1,0:T(8,128)(2,1)S(1)}, bf16[128,2560]{1,0:T(8,128)(2,1)S(1)}, u32[]{:S(2)}, u32[]{:S(2)}) collective-permute-start(bf16[128,2560]{1,0:T(8,128)(2,1)S(1)} %get-tuple-element.384), channel_id=1, source_target_pairs={{0,8},{2,10},{8,16},{10,18},{16,24},{18,26},{24,28},{26,30},{28,20... | collective-permute-start | bytes 1966088 | tf_op jit(solution)/shard_map/ring_send/ppermute | solution.py:897
  570.0 27.2 %collective-permute-start.45 = (bf16[128,2560]{1,0:T(8,128)(2,1)S(1)}, bf16[128,2560]{1,0:T(8,128)(2,1)S(1)}, u32[]{:S(2)}, u32[]{:S(2)}) collective-permute-start(bf16[128,2560]{1,0:T(8,128)(2,1)S(1)} %get-tuple-element.385), channel_id=1, source_target_pairs={{0,4},{2,6},{8,0},{10,2},{16,8},{18,10},{24,16},{26,18},{28,24},{3... | collective-permute-start | bytes 1966088 | tf_op jit(solution)/shard_map/ring_send/ppermute | solution.py:897
  571.3 24.6 %collective-permute-start.46 = (bf16[128,2304]{1,0:T(8,128)(2,1)}, bf16[128,2304]{1,0:T(8,128)(2,1)S(1)}, u32[]{:S(2)}, u32[]{:S(2)}) collective-permute-start(bf16[128,2304]{1,0:T(8,128)(2,1)} %copy-done.39), channel_id=1, source_target_pairs={{0,8},{2,10},{8,16},{10,18},{16,24},{18,26},{24,28},{26,30},{28,20... | collective-permute-start | bytes 1769480 | tf_op jit(solution)/shard_map/ring_send/ppermute | solution.py:897
  572.0 24.3 %collective-permute-start.47 = (bf16[128,2304]{1,0:T(8,128)(2,1)S(1)}, bf16[128,2304]{1,0:T(8,128)(2,1)S(1)}, u32[]{:S(2)}, u32[]{:S(2)}) collective-permute-start(bf16[128,2304]{1,0:T(8,128)(2,1)S(1)} %get-tuple-element.387), channel_id=1, source_target_pairs={{0,4},{2,6},{8,0},{10,2},{16,8},{18,10},{24,16},{26,18},{28,24},{3... | collective-permute-start | bytes 1769480 | tf_op jit(solution)/shard_map/ring_send/ppermute | solution.py:897
  597.2 24.6 %collective-permute-start.53 = (bf16[8,128,1536]{2,1,0:T(8,128)(2,1)}, bf16[8,128,1536]{2,1,0:T(8,128)(2,1)S(1)}, u32[]{:S(2)}, u32[]{:S(2)}) collective-permute-start(bf16[8,128,1536]{2,1,0:T(8,128)(2,1)} %weight_grads.14), channel_id=1, source_target_pairs={{0,2},{2,0},{4,6},{6,4},{8,10},{10,8},{12,14},{14,12},{16,18},{18,... | collective-permute-start | bytes 9437192 | tf_op jit(solution)/shard_map/core_swap/ppermute | solution.py:901
  599.7 17.8 %collective-permute-start.50 = (bf16[160,2048]{1,0:T(8,128)(2,1)}, bf16[160,2048]{1,0:T(8,128)(2,1)}, u32[]{:S(2)}, u32[]{:S(2)}) collective-permute-start(bf16[160,2048]{1,0:T(8,128)(2,1)} %get-tuple-element.529), channel_id=1, source_target_pairs={{0,1},{1,0},{2,3},{3,2},{4,5},{5,4},{6,7},{7,6},{8,9},{9,8},{10,11... | collective-permute-start | bytes 1966088 | tf_op jit(solution)/shard_map/tensor_swap/ppermute | solution.py:1011
  606.6 36.0 %collective-permute-start.49 = (bf16[160,2048]{1,0:T(8,128)(2,1)}, bf16[160,2048]{1,0:T(8,128)(2,1)}, u32[]{:S(2)}, u32[]{:S(2)}) collective-permute-start(bf16[160,2048]{1,0:T(8,128)(2,1)} %get-tuple-element.530), channel_id=1, source_target_pairs={{0,1},{1,0},{2,3},{3,2},{4,5},{5,4},{6,7},{7,6},{8,9},{9,8},{10,11... | collective-permute-start | bytes 1966088 | tf_op jit(solution)/shard_map/tensor_swap/ppermute | solution.py:1011
  630.4 20.6 %collective-permute-start.57 = (bf16[128,2560]{1,0:T(8,128)(2,1)}, bf16[128,2560]{1,0:T(8,128)(2,1)S(1)}, u32[]{:S(2)}, u32[]{:S(2)}) collective-permute-start(bf16[128,2560]{1,0:T(8,128)(2,1)} %get-tuple-element.437), channel_id=1, source_target_pairs={{0,8},{2,10},{8,16},{10,18},{16,24},{18,26},{24,28},{26,30},{28,20... | collective-permute-start | bytes 1966088 | tf_op jit(solution)/shard_map/ring_send/ppermute | solution.py:897
  631.0 20.0 %collective-permute-start.58 = (bf16[128,2560]{1,0:T(8,128)(2,1)}, bf16[128,2560]{1,0:T(8,128)(2,1)S(1)}, u32[]{:S(2)}, u32[]{:S(2)}) collective-permute-start(bf16[128,2560]{1,0:T(8,128)(2,1)} %get-tuple-element.438), channel_id=1, source_target_pairs={{0,4},{2,6},{8,0},{10,2},{16,8},{18,10},{24,16},{26,18},{28,24},{3... | collective-permute-start | bytes 1966088 | tf_op jit(solution)/shard_map/ring_send/ppermute | solution.py:897
  638.2 34.0 %collective-permute-start.48 = (bf16[192,2048]{1,0:T(8,128)(2,1)}, bf16[192,2048]{1,0:T(8,128)(2,1)}, u32[]{:S(2)}, u32[]{:S(2)}) collective-permute-start(bf16[192,2048]{1,0:T(8,128)(2,1)} %slice.96), channel_id=1, source_target_pairs={{0,1},{1,0},{2,3},{3,2},{4,5},{5,4},{6,7},{7,6},{8,9},{9,8},{10,11... | collective-permute-start | bytes 2359304 | tf_op jit(solution)/shard_map/tensor_swap/ppermute | solution.py:1011
  (92 other events, 1019.1 us)
Sparse Core Ops, SparseCore 0:
  97.6 139.8 all-gather.2
  239.8 80.5 all-gather.4
